TPU v7x, 128 devices: a whole 4x4x4 slice. The times are simulated.
128 devices in a mesh: seq: 16 (over x, z), head: 8 (over y, core).
Axes of the slice: x: 4, y: 4, z: 4, core: 2. Of those that a mesh axis runs over, the one named last changes fastest.
Arguments:
- tokens: bfloat16 [2048, 4, 2048], P('seq', None, 'head'), may hold values from -6 to 6
- attn_gain: bfloat16 [2048], replicated, may hold values from 0.25 to 1.75
- query_weight: bfloat16 [2048, 2048], P(None, 'head'), may hold values from -0.125 to 0.125
- key_weight: bfloat16 [2048, 2048], P(None, 'head'), may hold values from -0.125 to 0.125
- value_weight: bfloat16 [2048, 2048], P(None, 'head'), may hold values from -0.125 to 0.125
- head_gain: bfloat16 [2048], P('head'), may hold values from 0.25 to 1.75
- out_weight: bfloat16 [2048, 2048], P('head'), may hold values from -0.125 to 0.125
- moe_gain: bfloat16 [2048], replicated, may hold values from 0.25 to 1.75
- route_ids: int32 [2048, 4, 8], P(('seq', 'head')), may hold values from 0 to 63, all different within a row; in each aligned block of 64 rows (0 to 63, 64 to 127, ..., all dimensions but the last counted through in order) at most 12 rows name the same one
- route_weight: float32 [2048, 4, 8], P(('seq', 'head')), may hold values from 0.05 to 0.3
- expert_gate: bfloat16 [128, 2048, 512], P(('seq', 'head')), may hold values from -0.125 to 0.125
- expert_up: bfloat16 [128, 2048, 512], P(('seq', 'head')), may hold values from -0.125 to 0.125
- expert_down: bfloat16 [128, 512, 2048], P(('seq', 'head')), may hold values from -0.1875 to 0.1875
Outputs:
- layer_output: bfloat16 [2048, 4, 2048], P(('seq', 'head'))
Inputs may be any that keep to these rules, and one draw needn't show every extreme that they name: `route_ids`: the rows [position, sequence] taken position-major form aligned blocks of 64 rows, the rows of one device; within every block no expert is named by more than 12 routes, and in every draw some block has an expert named by exactly 12 routes. The 8 experts of a row differ.
All inputs are finite; a program needn't handle non-finite values.
Results may differ from a plain program's by a relative error of at most 0.017.
Values may be sent and summed in bfloat16 or wider, within the bound.
No kernel may reach another device: no remote copies, remote signals or barrier semaphores. Data moves between devices by JAX's collectives and lax.ppermute only.
A program may use at most 128 MiB of HBM per device.

v0:
```python
import jax
import jax.numpy as jnp
import numpy as np
from jax import lax
from jax.experimental import pallas as pl
from jax.experimental.pallas import tpu as pltpu
from jax.sharding import Mesh, PartitionSpec as P


EXPERTS = 64
TOP = 8
CAP = 12
QUART = 4
PACK = CAP * QUART
COLS = EXPERTS * PACK
WIDE = 8
REST = CAP - WIDE
GROUP = 16

norm_eps = 1e-05
head_eps = 1e-06

BF = jnp.bfloat16
F32 = jnp.float32


def shifted(x, axis, by):
    count = lax.axis_size(axis)
    return lax.ppermute(x, axis, [(i, (i + by) % count) for i in range(count)])


def exchanged(x, axes):
    return lax.all_to_all(x, axes, split_axis=0, concat_axis=0, tiled=True)


def dot(a, b, dims=((1,), (0,))):
    return lax.dot_general(a, b, (dims, ((), ())), preferred_element_type=F32)


def silu(v):
    return v / (1.0 + jnp.exp(-v))


def vmem(count):
    return [pl.BlockSpec(memory_space=pltpu.VMEM)] * count


class Inside:
    def __init__(self, x):
        self.x = x


def placed_inside(x):
    return Inside(pltpu.with_memory_space_constraint(x, pltpu.VMEM))


def outside(x):
    return pltpu.with_memory_space_constraint(x, pltpu.HBM)


def limit(mib):
    return pltpu.CompilerParams(vmem_limit_bytes=mib * 2**20)


def call(kernel, out_shape, *args, scratch=(), mib=24):
    several = isinstance(out_shape, (list, tuple))
    args = [x.x if isinstance(x, Inside) else outside(x) for x in args]
    return pl.pallas_call(
        kernel,
        out_shape=out_shape,
        in_specs=vmem(len(args)),
        out_specs=vmem(len(out_shape)) if several else vmem(1)[0],
        scratch_shapes=list(scratch),
        compiler_params=limit(mib),
    )(*args)


def route_kernel(ids_ref, ids_t_ref, weight_ref, send_ref, sum_ref):
    rows = ids_ref.shape[0]
    ids = ids_ref[...]
    ids_t = ids_t_ref[...]
    weights = weight_ref[...]
    across = lax.broadcasted_iota(jnp.int32, (rows, EXPERTS), 1)
    down = lax.broadcasted_iota(jnp.int32, (EXPERTS, rows), 0)
    named = jnp.zeros((rows, EXPERTS), F32)
    named_t = jnp.zeros((EXPERTS, rows), F32)
    weight = jnp.zeros((rows, EXPERTS), F32)
    for j in range(TOP):
        hit = ids[:, j : j + 1] == across
        named = named + jnp.where(hit, 1.0, 0.0)
        weight = weight + jnp.where(hit, weights[:, j : j + 1], 0.0)
        named_t = named_t + jnp.where(ids_t[j : j + 1, :] == down, 1.0, 0.0)
    i0 = lax.broadcasted_iota(jnp.int32, (rows, rows), 0)
    i1 = lax.broadcasted_iota(jnp.int32, (rows, rows), 1)
    before = dot(jnp.where(i1 < i0, 1.0, 0.0).astype(BF), named.astype(BF))
    before_t = dot(named_t.astype(BF), jnp.where(i0 < i1, 1.0, 0.0).astype(BF))
    slot = jnp.where(named > 0.5, before, 128.0)
    slot_t = jnp.where(named_t > 0.5, before_t, 128.0)

    def placed(slots, q):
        return jnp.where(slots < WIDE - 0.5, slots + float(WIDE * q), slots + float(WIDE * (QUART - 1) + REST * q))

    slot_all = jnp.concatenate([placed(slot, q) for q in range(QUART)], axis=0).astype(BF)
    slot_all_t = jnp.concatenate([placed(slot_t, q) for q in range(QUART)], axis=1).astype(BF)

    def split(shape, dim, other):
        index = lax.broadcasted_iota(jnp.int32, shape, dim).astype(F32)
        expert = jnp.floor((index + 0.5) * (1.0 / PACK))
        spread = jnp.where(expert == lax.broadcasted_iota(jnp.int32, shape, other).astype(F32), 1.0, 0.0)
        return spread.astype(BF), index - expert * PACK

    spread_t, place_t = split((COLS, EXPERTS), 0, 1)
    send_ref[...] = jnp.where(dot(spread_t, slot_all_t) == place_t[:, :1], 1.0, 0.0).astype(BF)
    spread, place = split((EXPERTS, COLS), 1, 0)
    match = dot(slot_all, spread) == place[:1, :]
    weight_all = dot(weight.astype(BF), spread)
    sum_ref[...] = jnp.where(match, jnp.concatenate([weight_all] * QUART, axis=0), 0.0).astype(BF)


def local_kernel(*refs):
    pieces, refs = refs[:10], refs[10:]
    wk_ref, wv_ref, gain_ref, normed_ref, k_ref, v_ref, state_ref, own_ref = refs
    y = lax.axis_index("y")
    c = lax.axis_index("c")
    rows, width = pieces[0].shape
    half = rows // 2
    blocks = []
    for part, core in ((pieces[:5], c), (pieces[5:], 1 - c)):
        for ref, away, lo, hi in (
            (part[0], 0, 0, rows),
            (part[1], 3, 0, rows),
            (part[2], 1, 0, rows),
            (part[3], 2, 0, half),
            (part[4], 2, half, rows),
        ):
            blocks.append((ref, ((y + away) & 3) * 2 + core, lo, hi))
    total = [jnp.zeros((half, 1), F32), jnp.zeros((half, 1), F32)]
    for ref, block, lo, hi in blocks:
        for h in range(lo // half, hi // half):
            values = ref[pl.ds(h * half - lo, half), :].astype(F32)
            total[h] = total[h] + jnp.sum(values * values, axis=1, keepdims=True)
    scale = [lax.rsqrt(t / (8 * width) + norm_eps) for t in total]
    mine = y * 2 + c
    own_rows = rows // 8
    for ref, block, lo, hi in blocks:
        gain = gain_ref[block]
        columns = pl.ds(pl.multiple_of(block * width, width), width)
        for h in range(lo // half, hi // half):
            values = ref[pl.ds(h * half - lo, half), :].astype(F32)
            normed_ref[pl.ds(h * half, half), columns] = (values * scale[h] * gain).astype(BF)
        if lo == 0 and hi == rows:
            own_ref[:, columns] = ref[pl.ds(pl.multiple_of(mine * own_rows, own_rows), own_rows), :]
        else:
            @pl.when((mine >= 4) == (lo > 0))
            def _():
                start = pl.multiple_of((mine & 3) * own_rows, own_rows)
                own_ref[:, columns] = ref[pl.ds(start, own_rows), :]
    normed = normed_ref[...]
    k = silu(dot(normed, wk_ref[...])).astype(BF)
    v = dot(normed, wv_ref[...]).astype(BF)
    k_ref[...] = k
    v_ref[...] = v
    sequence = lax.broadcasted_iota(jnp.int32, (rows, 128), 0) & 3
    for h in range(2):
        cols = slice(h * 128, (h + 1) * 128)
        keys = k[:, cols].astype(F32)
        apart = jnp.concatenate([jnp.where(sequence == b, keys, 0.0).astype(BF) for b in range(4)], axis=1)
        state_ref[h * rows : (h + 1) * rows, :] = dot(apart, v[:, cols], ((0,), (0,))).astype(BF)


def score_kernel(normed_ref, wq_ref, k_ref, v_ref, q_ref, local_ref):
    rows = normed_ref.shape[0]
    q = silu(dot(normed_ref[...], wq_ref[...])).astype(BF)
    q_ref[...] = q
    i0 = lax.broadcasted_iota(jnp.int32, (rows, rows), 0)
    i1 = lax.broadcasted_iota(jnp.int32, (rows, rows), 1)
    seen = (((i0 ^ i1) & 3) == 0) & (i1 <= i0)
    for h in range(2):
        cols = slice(h * 128, (h + 1) * 128)
        scores = jnp.where(seen, dot(q[:, cols], k_ref[:, cols], ((1,), (1,))), 0.0).astype(BF)
        local_ref[:, cols] = dot(scores, v_ref[:, cols])


def prefix_kernel(states_ref, before_ref):
    running = jnp.zeros(states_ref.shape[1:], F32)
    for i in range(states_ref.shape[0]):
        before_ref[i] = running.astype(BF)
        running = running + states_ref[i].astype(F32)


def mix_kernel(q_ref, local_ref, carried_ref, gain_ref, out_ref):
    rows = q_ref.shape[0]
    sequence = lax.broadcasted_iota(jnp.int32, (rows, 128), 0) & 3
    for h in range(2):
        cols = slice(h * 128, (h + 1) * 128)
        q = q_ref[:, cols].astype(F32)
        apart = jnp.concatenate([jnp.where(sequence == b, q, 0.0).astype(BF) for b in range(4)], axis=1)
        mixed = local_ref[:, cols] + dot(apart, carried_ref[h * rows : (h + 1) * rows, :])
        mean = jnp.mean(mixed * mixed, axis=1, keepdims=True)
        out_ref[:, cols] = (mixed * lax.rsqrt(mean + head_eps) * gain_ref[:, cols].astype(F32)).astype(BF)


def dispatch_kernel(*refs):
    weights, refs = refs[:10], refs[10:]
    attended_ref, own_ref, gain_ref, send_table_ref, residual_ref, out_ref = refs
    y = lax.axis_index("y")
    c = lax.axis_index("c")
    _, width = own_ref.shape
    residual = own_ref[...].astype(F32)
    for part, core in ((weights[:5], c), (weights[5:], 1 - c)):
        for ref, away in ((part[0], 0), (part[1], 3), (part[2], 1)):
            attended = attended_ref[((y + away) & 3) * 2 + core]
            residual = residual + dot(attended, ref[...]).astype(BF).astype(F32)
        attended = attended_ref[((y + 2) & 3) * 2 + core]
        half = part[3].shape[0]
        term = dot(attended[:, :half], part[3][...]) + dot(attended[:, half:], part[4][...])
        residual = residual + term.astype(BF).astype(F32)
    residual_ref[...] = residual
    mean = jnp.mean(residual * residual, axis=1, keepdims=True)
    entering = (residual * lax.rsqrt(mean + norm_eps) * gain_ref[...].astype(F32)).astype(BF)
    step = width // QUART
    stacked = jnp.concatenate([entering[:, q * step : (q + 1) * step] for q in range(QUART)], axis=0)
    out_ref[...] = dot(send_table_ref[...], stacked).astype(BF)


def expert_kernel(
    rows_ref, order_ref, back_ref, gate_hbm, up_hbm, down_hbm, gate_b_hbm, up_b_hbm, down_b_hbm, out_ref,
    x_ref, gate_ref, up_ref, down_ref, weight_sem,
):
    copies = [
        pltpu.make_async_copy(source, target.at[half], weight_sem.at[half, i])
        for half, given in enumerate(((gate_hbm, up_hbm, down_hbm), (gate_b_hbm, up_b_hbm, down_b_hbm)))
        for i, (source, target) in enumerate(zip(given, (gate_ref, up_ref, down_ref)))
    ]
    for copy in copies:
        copy.start()
    sources, _, step = rows_ref.shape
    head = sources * WIDE
    part = GROUP * REST
    wide = WIDE * QUART
    for q in range(QUART):
        for i in range(sources):
            x_ref[i * WIDE : (i + 1) * WIDE, q * step : (q + 1) * step] = rows_ref[i, q * WIDE : (q + 1) * WIDE, :]
    for g in range(sources // GROUP):
        rest = rows_ref[g * GROUP : (g + 1) * GROUP, wide:, :].reshape(GROUP * REST * QUART, step)
        rest = dot(order_ref[...], rest).astype(BF)
        for q in range(QUART):
            at = head + g * part
            x_ref[at : at + part, q * step : (q + 1) * step] = rest[q * part : (q + 1) * part]
    for first, lines in ((True, slice(0, head)), (False, slice(head, sources * CAP))):
        halves = []
        for half in range(2):
            if first:
                copies[3 * half].wait()
                copies[3 * half + 1].wait()
            gated = dot(x_ref[lines, :], gate_ref[half])
            active = (silu(gated) * dot(x_ref[lines, :], up_ref[half])).astype(BF)
            if first:
                copies[3 * half + 2].wait()
            halves.append(dot(active, down_ref[half]).astype(BF))
        x_ref[lines, :] = (halves[0].astype(F32) + halves[1].astype(F32)).astype(BF)
    for q in range(QUART):
        for i in range(sources):
            out_ref[i, q * WIDE : (q + 1) * WIDE, :] = x_ref[i * WIDE : (i + 1) * WIDE, q * step : (q + 1) * step]
    for g in range(sources // GROUP):
        at = head + g * part
        rest = jnp.concatenate([x_ref[at : at + part, q * step : (q + 1) * step] for q in range(QUART)], axis=0)
        rest = dot(back_ref[...], rest).astype(BF)
        out_ref[g * GROUP : (g + 1) * GROUP, wide:, :] = rest.reshape(GROUP, REST * QUART, step)


def combine_kernel(rows_ref, table_ref, residual_ref, out_ref):
    rows = residual_ref.shape[0]
    step = rows_ref.shape[1]
    total = dot(table_ref[...], rows_ref[...])
    for q in range(QUART):
        cols = slice(q * step, (q + 1) * step)
        out_ref[:, cols] = (residual_ref[:, cols] + total[q * rows : (q + 1) * rows]).astype(BF)


def sorting():
    size = GROUP * REST * QUART
    order = np.zeros((size, size), np.float32)
    for q in range(QUART):
        for s in range(GROUP):
            for r in range(REST):
                order[(q * GROUP + s) * REST + r, (s * QUART + q) * REST + r] = 1.0
    return order


def body(
    tokens, attn_gain, query_weight, key_weight, value_weight, head_gain, out_weight, moe_gain,
    route_ids, route_weight, expert_gate, expert_up, expert_down,
):
    shape = jax.ShapeDtypeStruct
    block_len, batch, width = tokens.shape
    rows = block_len * batch
    model = attn_gain.shape[0]
    own_rows = rows // 8
    hidden = expert_gate.shape[2]
    order = sorting()

    mine = tokens.reshape(rows, width)
    from_left = shifted(mine, "y", 1)
    from_right = shifted(mine, "y", -1)
    far_low = shifted(from_left[: rows // 2], "y", 1)
    far_high = shifted(from_right[rows // 2 :], "y", -1)
    pieces = [mine, from_left, from_right, far_low, far_high]
    pieces = pieces + [shifted(p, "c", 1) for p in pieces]

    later_out, *pieces[5:] = lax.optimization_barrier((out_weight, *pieces[5:]))
    out_left = shifted(later_out, "y", 1)
    out_right = shifted(later_out, "y", -1)
    out_half = out_weight.shape[0] // 2
    out_low = shifted(out_left[:out_half], "y", 1)
    out_high = shifted(out_right[out_half:], "y", -1)
    projections = [out_weight, out_left, out_right, out_low, out_high]
    projections = projections + [shifted(p, "c", 1) for p in projections[:3]]
    projections = projections + [shifted(p, "c", 1) for p in projections[3:5]]
    gate = expert_gate.reshape(model, hidden)
    up = expert_up.reshape(model, hidden)
    down = expert_down.reshape(hidden, model)
    other_gate = shifted(gate, "c", 1)
    other_up = shifted(up, "c", 1)
    other_down = shifted(down, "c", 1)

    ids = route_ids.reshape(own_rows, TOP)
    send_table, sum_table = call(
        route_kernel,
        (pltpu.HBM((COLS, QUART * own_rows), BF), pltpu.HBM((QUART * own_rows, COLS), BF)),
        ids,
        ids.T,
        route_weight.reshape(own_rows, TOP),
    )

    normed, k, v, state, own = call(
        local_kernel,
        (
            pltpu.HBM((rows, model), BF),
            pltpu.HBM((rows, width), BF),
            pltpu.HBM((rows, width), BF),
            pltpu.VMEM((2 * rows, 128), BF),
            pltpu.HBM((own_rows, model), BF),
        ),
        *[placed_inside(p) for p in pieces],
        key_weight,
        value_weight,
        attn_gain.astype(F32).reshape(8, 1, width),
    )
    q, local_mix = call(
        score_kernel, (pltpu.HBM((rows, width), BF), pltpu.HBM((rows, width), F32)), normed, query_weight, k, v
    )
    blocks = lax.axis_size(("x", "z"))
    states = placed_inside(exchanged(state.reshape(blocks, 2 * rows // blocks, 128), ("x", "z")))
    before = call(prefix_kernel, pltpu.HBM(states.x.shape, BF), states)
    carried = placed_inside(exchanged(before, ("x", "z")).reshape(2 * rows, 128))
    attended = call(mix_kernel, pltpu.VMEM((rows, width), BF), q, local_mix, carried, head_gain.reshape(1, width))
    attended = placed_inside(exchanged(attended.reshape(8, own_rows, width), ("y", "c")))
    step = model // QUART
    residual, sending = call(
        dispatch_kernel,
        (pltpu.HBM((own_rows, model), F32), pltpu.HBM((COLS, step), BF)),
        *projections,
        attended,
        own,
        moe_gain.reshape(1, model),
        send_table,
    )
    chips = ("x", "z", "y")
    received = placed_inside(exchanged(sending.reshape(EXPERTS, PACK, step), chips))
    inside, anywhere = vmem(1)[0], pl.BlockSpec(memory_space=pltpu.HBM)
    results = pl.pallas_call(
        expert_kernel,
        out_shape=pltpu.VMEM((EXPERTS, PACK, step), BF),
        in_specs=[inside] * 3 + [anywhere] * 6,
        out_specs=inside,
        scratch_shapes=[
            pltpu.VMEM((EXPERTS * CAP, model), BF),
            pltpu.VMEM((2, model, hidden), BF),
            pltpu.VMEM((2, model, hidden), BF),
            pltpu.VMEM((2, hidden, model), BF),
            pltpu.SemaphoreType.DMA((2, 3)),
        ],
        compiler_params=limit(36),
        name="experts",
    )(received.x, jnp.asarray(order, BF), jnp.asarray(order.T, BF), *[outside(w) for w in (gate, up, down, other_gate, other_up, other_down)])
    returned = placed_inside(exchanged(results, chips).reshape(COLS, step))
    out = call(combine_kernel, shape((own_rows, model), BF), returned, sum_table, residual)
    return out.reshape(own_rows // batch, batch, model)


def solution(mesh):
    fine = Mesh(mesh.devices.reshape(4, 4, 4, 2), ("x", "z", "y", "c"))
    seq, head, every = ("x", "z"), ("y", "c"), ("x", "z", "y", "c")
    in_specs = (
        P(seq, None, head),
        P(),
        P(None, head),
        P(None, head),
        P(None, head),
        P(head),
        P(head, None),
        P(),
        P(every, None, None),
        P(every, None, None),
        P(every, None, None),
        P(every, None, None),
        P(every, None, None),
    )

    return jax.shard_map(body, mesh=fine, in_specs=in_specs, out_specs=P(every, None, None), check_vma=False)
```

profile of v0, /device:TPU:1, one launch (start us, length us, event | category | flops | bytes accessed | tf_op | source)
XLA Modules:
  0.0 225.8 jit_solution(3815338722749421874)
XLA Ops:
  0.0 1.0 reshape.47.refs_0_
  1.0 2.2 collective-permute-start.1
  3.2 1.5 collective-permute-start.3
  4.7 1.0 collective-permute-start
  5.7 4.8 %collective-permute-done.1.refs_1_ = bf16[512,256]{1,0:T(8,128)(2,1)S(1)} collective-permute-done((bf16[512,256]{1,0:T(8,128)(2,1)S(1)}, bf16[512,256]{1,0:T(8,128)(2,1)S(1)}, u32[]{:S(2)}, u32[]{:S(2)}) %collective-permute-start.1) | collective-permute-done | bytes 262176 | tf_op jit(solution)/shard_map/ppermute | solution.py:29
  10.7 2.7 %collective-permute-start.7 = (bf16[256,256]{1,0:T(8,128)(2,1)S(1)}, bf16[256,256]{1,0:T(8,128)(2,1)S(1)}, u32[]{:S(2)}, u32[]{:S(2)}) collective-permute-start(bf16[256,256]{1,0:T(8,128)(2,1)S(1)} %slice.17), channel_id=1, source_target_pairs={{0,6},{2,0},{4,2},{6,4},{1,7},{3,1},{5,3},{7,5},{8,14},{10,8},{12,... | collective-permute-start | bytes 393224 | tf_op jit(solution)/shard_map/ppermute | solution.py:29
  13.4 1.9 collective-permute-start.2
  15.3 0.3 collective-permute-done.5.refs_3_
  15.7 2.5 %collective-permute-start.6 = (bf16[256,256]{1,0:T(8,128)(2,1)S(1)}, bf16[256,256]{1,0:T(8,128)(2,1)S(1)}, u32[]{:S(2)}, u32[]{:S(2)}) collective-permute-start(bf16[256,256]{1,0:T(8,128)(2,1)S(1)} %collective-permute-done.5.refs_3_), channel_id=1, source_target_pairs={{0,1},{1,0},{2,3},{3,2},{4,5},{5,4},{6,7},{7,6},{8,9},{9,8},{10,11... | collective-permute-start | bytes 393224 | tf_op jit(solution)/shard_map/ppermute | solution.py:29
  18.2 1.0 collective-permute-done.6.refs_8_
  19.2 0.4 collective-permute-done.8.refs_9_
  19.6 2.6 %collective-permute-start.10 = (bf16[256,2048]{1,0:T(8,128)(2,1)}, bf16[256,2048]{1,0:T(8,128)(2,1)S(1)}, u32[]{:S(2)}, u32[]{:S(2)}) collective-permute-start(bf16[256,2048]{1,0:T(8,128)(2,1)} %refs_0_.1), channel_id=1, source_target_pairs={{0,6},{2,0},{4,2},{6,4},{1,7},{3,1},{5,3},{7,5},{8,14},{10,8},{12,... | collective-permute-start | bytes 3145736 | tf_op jit(solution)/shard_map/ppermute | solution.py:29
  22.3 0.7 collective-permute-start.13
  23.0 22.5 %collective-permute-done.9.refs_1_ = bf16[256,2048]{1,0:T(8,128)(2,1)S(1)} collective-permute-done((bf16[256,2048]{1,0:T(8,128)(2,1)}, bf16[256,2048]{1,0:T(8,128)(2,1)S(1)}, u32[]{:S(2)}, u32[]{:S(2)}) %collective-permute-start.9) | collective-permute-done | bytes 1048608 | tf_op jit(solution)/shard_map/ppermute | solution.py:29
  45.5 0.9 slice.18
  46.4 0.9 slice.19
  47.3 2.7 %collective-permute-start.12 = (bf16[128,2048]{1,0:T(8,128)(2,1)}, bf16[128,2048]{1,0:T(8,128)(2,1)}, u32[]{:S(2)}, u32[]{:S(2)}) collective-permute-start(bf16[128,2048]{1,0:T(8,128)(2,1)} %slice.19), channel_id=1, source_target_pairs={{0,6},{2,0},{4,2},{6,4},{1,7},{3,1},{5,3},{7,5},{8,14},{10,8},{12,... | collective-permute-start | bytes 1572872 | tf_op jit(solution)/shard_map/ppermute | solution.py:29
  50.0 1.6 collective-permute-start.14
  51.6 0.6 reshape.63
  52.2 5.3 %shard_map.145 = (bf16[512,2048]{1,0:T(8,128)(2,1)}, bf16[512,256]{1,0:T(8,128)(2,1)}, bf16[512,256]{1,0:T(8,128)(2,1)}, bf16[1024,128]{1,0:T(8,128)(2,1)}, bf16[64,2048]{1,0:T(8,128)(2,1)}) custom-call(bf16[512,256]{1,0:T(8,128)(2,1)S(1)} %reshape.47.refs_0_, bf16[512,256]{1,0:T(8,128)(2,1)S(1)} %collective-permute-done.1.refs_1_, ...), custom_call_target="tpu_custom_call" | custom-call | tf_op jit(solution)/shard_map/pallas_call | solution.py:68
  57.5 7.6 %all-to-all-start = ((bf16[16,64,128]{2,1,0:T(8,128)(2,1)}), bf16[16,64,128]{2,1,0:T(8,128)(2,1)S(1)}, u32[]{:S(2)}, u32[]{:S(2)}) async-start(bf16[16,64,128]{2,1,0:T(8,128)(2,1)} %bitcast.1), calls=%async_computation | async-start | bytes 524288 | tf_op jit(solution)/shard_map/all_to_all | solution.py:33
  65.1 0.9 collective-permute-start.16
  66.1 6.5 %all-to-all-done.states_ref = bf16[16,64,128]{2,1,0:T(8,128)(2,1)S(1)} async-done(((bf16[16,64,128]{2,1,0:T(8,128)(2,1)}), bf16[16,64,128]{2,1,0:T(8,128)(2,1)S(1)}, u32[]{:S(2)}, u32[]{:S(2)}) %all-to-all-start) | async-done | bytes 262176 | tf_op jit(solution)/shard_map/all_to_all | solution.py:33
  72.5 0.7 shard_map.147
  73.3 3.7 %all-to-all-start.1 = ((bf16[16,64,128]{2,1,0:T(8,128)(2,1)}), bf16[16,64,128]{2,1,0:T(8,128)(2,1)S(1)}, u32[]{:S(2)}, u32[]{:S(2)}) async-start(bf16[16,64,128]{2,1,0:T(8,128)(2,1)} %shard_map.147), calls=%async_computation.1 | async-start | bytes 524288 | tf_op jit(solution)/shard_map/all_to_all | solution.py:33
  77.0 0.6 reshape.52.gain_ref
  77.6 5.1 %shard_map.146 = (bf16[512,256]{1,0:T(8,128)(2,1)}, f32[512,256]{1,0:T(8,128)}) custom-call(bf16[512,2048]{1,0:T(8,128)(2,1)} %get-tuple-element.28.normed_ref, bf16[2048,256]{1,0:T(8,128)(2,1)} %wq_ref.1, bf16[512,256]{1,0:T(8,128)(2,1)} %get-tuple-element.29.k_ref, bf16[512,256]{1,0:T(8,128)(2,1)} %get-tuple-element.30.v_ref), custom_call_target="tpu_custom_call" | custom-call | tf_op jit(solution)/shard_map/pallas_call | solution.py:68
  82.7 1.6 all-to-all-done.1
  84.3 2.3 %shard_map.148 = bf16[512,256]{1,0:T(8,128)(2,1)} custom-call(bf16[512,256]{1,0:T(8,128)(2,1)} %get-tuple-element.31.q_ref, f32[512,256]{1,0:T(8,128)} %get-tuple-element.32.local_ref, bf16[1024,128]{1,0:T(8,128)(2,1)S(1)} %bitcast.13, bf16[1,256]{1,0:T(2,128)(2,1)} %reshape.52.gain_ref), custom_call_target="tpu_custom_call" | custom-call | tf_op jit(solution)/shard_map/pallas_call | solution.py:68
  86.6 6.4 %all-to-all-start.2 = ((bf16[8,64,256]{2,1,0:T(8,128)(2,1)}), bf16[8,64,256]{2,1,0:T(8,128)(2,1)S(1)}, u32[]{:S(2)}, u32[]{:S(2)}) async-start(bf16[8,64,256]{2,1,0:T(8,128)(2,1)} %bitcast.3), calls=%async_computation.2 | async-start | bytes 524288 | tf_op jit(solution)/shard_map/all_to_all | solution.py:33
  93.1 0.7 copy.20
  93.8 0.7 copy.21
  94.5 0.6 reshape.54.refs_12_
  95.1 3.7 %shard_map.149 = (bf16[3072,256]{1,0:T(8,128)(2,1)}, bf16[256,3072]{1,0:T(8,128)(2,1)}) custom-call(s32[64,8]{1,0:T(8,128)} %bitcast.22, s32[8,64]{1,0:T(8,128)} %bitcast.25, f32[64,8]{1,0:T(8,128)} %bitcast.23), custom_call_target="tpu_custom_call" | custom-call | tf_op jit(solution)/shard_map/pallas_call | solution.py:68
  98.7 0.8 all-to-all-done.2.refs_10_
  99.7 8.2 %shard_map.150 = (f32[64,2048]{1,0:T(8,128)}, bf16[3072,512]{1,0:T(8,128)(2,1)}) custom-call(bf16[256,2048]{1,0:T(8,128)(2,1)} %refs_0_.1, bf16[256,2048]{1,0:T(8,128)(2,1)} %copy-done.2, bf16[256,2048]{1,0:T(8,128)(2,1)} %copy-done.3, bf16[128,2048]{1,0:T(8,128)(2,1)} %collective-permute-done.11.refs_3_, bf16[128,2048]{1,0:T(8,128)(2,1)} %collective-permute-done.12.refs_4_, ...), custom_call_target="tpu_custom_call" | custom-call | tf_op jit(solution)/shard_map/pallas_call | solution.py:68
  108.0 7.9 %all-to-all-start.3 = ((bf16[64,48,512]{2,1,0:T(8,128)(2,1)}), bf16[64,48,512]{2,1,0:T(8,128)(2,1)S(1)}, u32[]{:S(2)}, u32[]{:S(2)}) async-start(bf16[64,48,512]{2,1,0:T(8,128)(2,1)} %bitcast.14), calls=%async_computation.3 | async-start | bytes 6291456 | tf_op jit(solution)/shard_map/all_to_all | solution.py:33
  115.9 0.7 collective-permute-start.18
  116.7 0.4 collective-permute-start.20
  117.1 3.5 %collective-permute-done.18.gate_b_hbm = bf16[2048,512]{1,0:T(8,128)(2,1)S(1)} collective-permute-done((bf16[2048,512]{1,0:T(8,128)(2,1)}, bf16[2048,512]{1,0:T(8,128)(2,1)S(1)}, u32[]{:S(2)}, u32[]{:S(2)}) %collective-permute-start.18) | collective-permute-done | bytes 2097184 | tf_op jit(solution)/shard_map/ppermute | solution.py:29
  120.6 3.0 %collective-permute-done.19.up_b_hbm = bf16[2048,512]{1,0:T(8,128)(2,1)S(1)} collective-permute-done((bf16[2048,512]{1,0:T(8,128)(2,1)}, bf16[2048,512]{1,0:T(8,128)(2,1)S(1)}, u32[]{:S(2)}, u32[]{:S(2)}) %collective-permute-start.19) | collective-permute-done | bytes 2097184 | tf_op jit(solution)/shard_map/ppermute | solution.py:29
  123.6 1.3 copy-done.5
  124.9 1.8 collective-permute-done.20.down_b_hbm
  126.7 29.5 %all-to-all-done.3.rows_ref = bf16[64,48,512]{2,1,0:T(8,128)(2,1)S(1)} async-done(((bf16[64,48,512]{2,1,0:T(8,128)(2,1)}), bf16[64,48,512]{2,1,0:T(8,128)(2,1)S(1)}, u32[]{:S(2)}, u32[]{:S(2)}) %all-to-all-start.3) | async-done | bytes 3145760 | tf_op jit(solution)/shard_map/all_to_all | solution.py:33
  156.2 13.8 %experts.1 = bf16[64,48,512]{2,1,0:T(8,128)(2,1)S(1)} custom-call(bf16[64,48,512]{2,1,0:T(8,128)(2,1)S(1)} %all-to-all-done.3.rows_ref, bf16[256,256]{1,0:T(8,128)(2,1)S(1)} %copy-done, bf16[256,256]{1,0:T(8,128)(2,1)S(1)} %copy-done.1, bf16[2048,512]{1,0:T(8,128)(2,1)} %bitcast.16, bf16[2048,512]{1,0:T(8,128)(2,1)} %bitcast.18, bf16[512,2048]{1,0:T(8,128)(2,1)} %bitcast.20, ...), custom_call_target="tpu_custom_call" | custom-call | tf_op jit(solution)/shard_map/experts/pallas_call | solution.py:372
  170.0 52.5 %all_to_all.25 = bf16[64,48,512]{2,1,0:T(8,128)(2,1)S(1)} all-to-all(bf16[64,48,512]{2,1,0:T(8,128)(2,1)S(1)} %experts.1), channel_id=1, replica_groups=mesh['x'=4,'z'=4,'y'=4,'c'=2] {'x','z','y'}, dimensions={0} | all-to-all | bytes 6291456 | tf_op jit(solution)/shard_map/all_to_all | solution.py:33
  222.5 2.5 %shard_map.151 = bf16[64,2048]{1,0:T(8,128)(2,1)S(1)} custom-call(bf16[3072,512]{1,0:T(8,128)(2,1)S(1)} %bitcast.12, bf16[256,3072]{1,0:T(8,128)(2,1)} %get-tuple-element.37.table_ref, f32[64,2048]{1,0:T(8,128)} %get-tuple-element.38.residual_ref), custom_call_target="tpu_custom_call" | custom-call | tf_op jit(solution)/shard_map/pallas_call | solution.py:68
  225.0 0.8 reshape.62
  (49 shorter events, 0.7 us)
Async XLA Ops:
  0.0 51.6 %copy-start.10 = (bf16[2048]{0:T(1024)(128)(2,1)S(1)}, bf16[2048]{0:T(1024)(128)(2,1)}, u32[]{:S(2)}) copy-start(bf16[2048]{0:T(1024)(128)(2,1)} %param.16) | copy-start | bytes 12292
  1.0 9.5 %collective-permute-start.1 = (bf16[512,256]{1,0:T(8,128)(2,1)S(1)}, bf16[512,256]{1,0:T(8,128)(2,1)S(1)}, u32[]{:S(2)}, u32[]{:S(2)}) collective-permute-start(bf16[512,256]{1,0:T(8,128)(2,1)S(1)} %reshape.47.refs_0_), channel_id=1, source_target_pairs={{0,2},{2,4},{4,6},{6,0},{1,3},{3,5},{5,7},{7,1},{8,10},{10,12},{12... | collective-permute-start | bytes 786440 | tf_op jit(solution)/shard_map/ppermute | solution.py:29
  3.2 7.4 %collective-permute-start.3 = (bf16[512,256]{1,0:T(8,128)(2,1)S(1)}, bf16[512,256]{1,0:T(8,128)(2,1)S(1)}, u32[]{:S(2)}, u32[]{:S(2)}) collective-permute-start(bf16[512,256]{1,0:T(8,128)(2,1)S(1)} %reshape.47.refs_0_), channel_id=1, source_target_pairs={{0,6},{2,0},{4,2},{6,4},{1,7},{3,1},{5,3},{7,5},{8,14},{10,8},{12,... | collective-permute-start | bytes 786440 | tf_op jit(solution)/shard_map/ppermute | solution.py:29
  4.7 13.5 %collective-permute-start = (bf16[512,256]{1,0:T(8,128)(2,1)S(1)}, bf16[512,256]{1,0:T(8,128)(2,1)S(1)}, u32[]{:S(2)}, u32[]{:S(2)}) collective-permute-start(bf16[512,256]{1,0:T(8,128)(2,1)S(1)} %reshape.47.refs_0_), channel_id=1, source_target_pairs={{0,1},{1,0},{2,3},{3,2},{4,5},{5,4},{6,7},{7,6},{8,9},{9,8},{10,11... | collective-permute-start | bytes 786440 | tf_op jit(solution)/shard_map/ppermute | solution.py:29
  10.6 5.1 %collective-permute-start.5 = (bf16[256,256]{1,0:T(8,128)(2,1)S(1)}, bf16[256,256]{1,0:T(8,128)(2,1)S(1)}, u32[]{:S(2)}, u32[]{:S(2)}) collective-permute-start(bf16[256,256]{1,0:T(8,128)(2,1)S(1)} %slice.16), channel_id=1, source_target_pairs={{0,2},{2,4},{4,6},{6,0},{1,3},{3,5},{5,7},{7,1},{8,10},{10,12},{12... | collective-permute-start | bytes 393224 | tf_op jit(solution)/shard_map/ppermute | solution.py:29
  10.7 7.5 %collective-permute-start.7 = (bf16[256,256]{1,0:T(8,128)(2,1)S(1)}, bf16[256,256]{1,0:T(8,128)(2,1)S(1)}, u32[]{:S(2)}, u32[]{:S(2)}) collective-permute-start(bf16[256,256]{1,0:T(8,128)(2,1)S(1)} %slice.17), channel_id=1, source_target_pairs={{0,6},{2,0},{4,2},{6,4},{1,7},{3,1},{5,3},{7,5},{8,14},{10,8},{12,... | collective-permute-start | bytes 393224 | tf_op jit(solution)/shard_map/ppermute | solution.py:29
  13.4 6.1 %collective-permute-start.2 = (bf16[512,256]{1,0:T(8,128)(2,1)S(1)}, bf16[512,256]{1,0:T(8,128)(2,1)S(1)}, u32[]{:S(2)}, u32[]{:S(2)}) collective-permute-start(bf16[512,256]{1,0:T(8,128)(2,1)S(1)} %collective-permute-done.1.refs_1_), channel_id=1, source_target_pairs={{0,1},{1,0},{2,3},{3,2},{4,5},{5,4},{6,7},{7,6},{8,9},{9,8},{10,11... | collective-permute-start | bytes 786440 | tf_op jit(solution)/shard_map/ppermute | solution.py:29
  15.3 4.2 %collective-permute-start.4 = (bf16[512,256]{1,0:T(8,128)(2,1)S(1)}, bf16[512,256]{1,0:T(8,128)(2,1)S(1)}, u32[]{:S(2)}, u32[]{:S(2)}) collective-permute-start(bf16[512,256]{1,0:T(8,128)(2,1)S(1)} %collective-permute-done.3.refs_2_), channel_id=1, source_target_pairs={{0,1},{1,0},{2,3},{3,2},{4,5},{5,4},{6,7},{7,6},{8,9},{9,8},{10,11... | collective-permute-start | bytes 786440 | tf_op jit(solution)/shard_map/ppermute | solution.py:29
  15.7 3.5 %collective-permute-start.6 = (bf16[256,256]{1,0:T(8,128)(2,1)S(1)}, bf16[256,256]{1,0:T(8,128)(2,1)S(1)}, u32[]{:S(2)}, u32[]{:S(2)}) collective-permute-start(bf16[256,256]{1,0:T(8,128)(2,1)S(1)} %collective-permute-done.5.refs_3_), channel_id=1, source_target_pairs={{0,1},{1,0},{2,3},{3,2},{4,5},{5,4},{6,7},{7,6},{8,9},{9,8},{10,11... | collective-permute-start | bytes 393224 | tf_op jit(solution)/shard_map/ppermute | solution.py:29
  18.2 1.3 collective-permute-start.8
  19.5 26.0 %collective-permute-start.9 = (bf16[256,2048]{1,0:T(8,128)(2,1)}, bf16[256,2048]{1,0:T(8,128)(2,1)S(1)}, u32[]{:S(2)}, u32[]{:S(2)}) collective-permute-start(bf16[256,2048]{1,0:T(8,128)(2,1)} %refs_0_.1), channel_id=1, source_target_pairs={{0,2},{2,4},{4,6},{6,0},{1,3},{3,5},{5,7},{7,1},{8,10},{10,12},{12... | collective-permute-start | bytes 3145736 | tf_op jit(solution)/shard_map/ppermute | solution.py:29
  19.6 26.8 %collective-permute-start.10 = (bf16[256,2048]{1,0:T(8,128)(2,1)}, bf16[256,2048]{1,0:T(8,128)(2,1)S(1)}, u32[]{:S(2)}, u32[]{:S(2)}) collective-permute-start(bf16[256,2048]{1,0:T(8,128)(2,1)} %refs_0_.1), channel_id=1, source_target_pairs={{0,6},{2,0},{4,2},{6,4},{1,7},{3,1},{5,3},{7,5},{8,14},{10,8},{12,... | collective-permute-start | bytes 3145736 | tf_op jit(solution)/shard_map/ppermute | solution.py:29
  22.3 76.4 %collective-permute-start.13 = (bf16[256,2048]{1,0:T(8,128)(2,1)}, bf16[256,2048]{1,0:T(8,128)(2,1)S(1)}, u32[]{:S(2)}, u32[]{:S(2)}) collective-permute-start(bf16[256,2048]{1,0:T(8,128)(2,1)} %refs_0_.1), channel_id=1, source_target_pairs={{0,1},{1,0},{2,3},{3,2},{4,5},{5,4},{6,7},{7,6},{8,9},{9,8},{10,11... | collective-permute-start | bytes 3145736 | tf_op jit(solution)/shard_map/ppermute | solution.py:29
  45.5 12.0 %copy-start.2 = (bf16[256,2048]{1,0:T(8,128)(2,1)}, bf16[256,2048]{1,0:T(8,128)(2,1)S(1)}, u32[]{:S(2)}) copy-start(bf16[256,2048]{1,0:T(8,128)(2,1)S(1)} %collective-permute-done.9.refs_1_) | copy-start | bytes 3145732
  46.4 18.6 %collective-permute-start.11 = (bf16[128,2048]{1,0:T(8,128)(2,1)}, bf16[128,2048]{1,0:T(8,128)(2,1)}, u32[]{:S(2)}, u32[]{:S(2)}) collective-permute-start(bf16[128,2048]{1,0:T(8,128)(2,1)} %slice.18), channel_id=1, source_target_pairs={{0,2},{2,4},{4,6},{6,0},{1,3},{3,5},{5,7},{7,1},{8,10},{10,12},{12... | collective-permute-start | bytes 1572872 | tf_op jit(solution)/shard_map/ppermute | solution.py:29
  46.4 11.0 %copy-start.3 = (bf16[256,2048]{1,0:T(8,128)(2,1)}, bf16[256,2048]{1,0:T(8,128)(2,1)S(1)}, u32[]{:S(2)}) copy-start(bf16[256,2048]{1,0:T(8,128)(2,1)S(1)} %collective-permute-done.10.refs_2_) | copy-start | bytes 3145732
  47.3 18.6 %collective-permute-start.12 = (bf16[128,2048]{1,0:T(8,128)(2,1)}, bf16[128,2048]{1,0:T(8,128)(2,1)}, u32[]{:S(2)}, u32[]{:S(2)}) collective-permute-start(bf16[128,2048]{1,0:T(8,128)(2,1)} %slice.19), channel_id=1, source_target_pairs={{0,6},{2,0},{4,2},{6,4},{1,7},{3,1},{5,3},{7,5},{8,14},{10,8},{12,... | collective-permute-start | bytes 1572872 | tf_op jit(solution)/shard_map/ppermute | solution.py:29
  50.0 49.5 %collective-permute-start.14 = (bf16[256,2048]{1,0:T(8,128)(2,1)S(1)}, bf16[256,2048]{1,0:T(8,128)(2,1)}, u32[]{:S(2)}, u32[]{:S(2)}) collective-permute-start(bf16[256,2048]{1,0:T(8,128)(2,1)S(1)} %collective-permute-done.9.refs_1_), channel_id=1, source_target_pairs={{0,1},{1,0},{2,3},{3,2},{4,5},{5,4},{6,7},{7,6},{8,9},{9,8},{10,11... | collective-permute-start | bytes 3145736 | tf_op jit(solution)/shard_map/ppermute | solution.py:29
  51.6 47.9 %collective-permute-start.15 = (bf16[256,2048]{1,0:T(8,128)(2,1)S(1)}, bf16[256,2048]{1,0:T(8,128)(2,1)}, u32[]{:S(2)}, u32[]{:S(2)}) collective-permute-start(bf16[256,2048]{1,0:T(8,128)(2,1)S(1)} %collective-permute-done.10.refs_2_), channel_id=1, source_target_pairs={{0,1},{1,0},{2,3},{3,2},{4,5},{5,4},{6,7},{7,6},{8,9},{9,8},{10,11... | collective-permute-start | bytes 3145736 | tf_op jit(solution)/shard_map/ppermute | solution.py:29
  52.2 24.8 %copy-start.12 = (bf16[256]{0:T(256)(128)(2,1)S(1)}, bf16[256]{0:T(256)(128)(2,1)}, u32[]{:S(2)}) copy-start(bf16[256]{0:T(256)(128)(2,1)} %param.20) | copy-start | bytes 1540
  57.5 15.1 %all-to-all-start = ((bf16[16,64,128]{2,1,0:T(8,128)(2,1)}), bf16[16,64,128]{2,1,0:T(8,128)(2,1)S(1)}, u32[]{:S(2)}, u32[]{:S(2)}) async-start(bf16[16,64,128]{2,1,0:T(8,128)(2,1)} %bitcast.1), calls=%async_computation | async-start | bytes 524288 | tf_op jit(solution)/shard_map/all_to_all | solution.py:33
  65.1 34.5 %collective-permute-start.16 = (bf16[128,2048]{1,0:T(8,128)(2,1)}, bf16[128,2048]{1,0:T(8,128)(2,1)}, u32[]{:S(2)}, u32[]{:S(2)}) collective-permute-start(bf16[128,2048]{1,0:T(8,128)(2,1)} %collective-permute-done.11.refs_3_), channel_id=1, source_target_pairs={{0,1},{1,0},{2,3},{3,2},{4,5},{5,4},{6,7},{7,6},{8,9},{9,8},{10,11... | collective-permute-start | bytes 1572872 | tf_op jit(solution)/shard_map/ppermute | solution.py:29
  66.0 33.6 %collective-permute-start.17 = (bf16[128,2048]{1,0:T(8,128)(2,1)}, bf16[128,2048]{1,0:T(8,128)(2,1)}, u32[]{:S(2)}, u32[]{:S(2)}) collective-permute-start(bf16[128,2048]{1,0:T(8,128)(2,1)} %collective-permute-done.12.refs_4_), channel_id=1, source_target_pairs={{0,1},{1,0},{2,3},{3,2},{4,5},{5,4},{6,7},{7,6},{8,9},{9,8},{10,11... | collective-permute-start | bytes 1572872 | tf_op jit(solution)/shard_map/ppermute | solution.py:29
  73.3 11.0 %all-to-all-start.1 = ((bf16[16,64,128]{2,1,0:T(8,128)(2,1)}), bf16[16,64,128]{2,1,0:T(8,128)(2,1)S(1)}, u32[]{:S(2)}, u32[]{:S(2)}) async-start(bf16[16,64,128]{2,1,0:T(8,128)(2,1)} %shard_map.147), calls=%async_computation.1 | async-start | bytes 524288 | tf_op jit(solution)/shard_map/all_to_all | solution.py:33
  77.6 15.5 %copy-start.8 = (s32[16,4,8]{0,2,1:T(8,128)S(1)}, s32[16,4,8]{0,2,1:T(8,128)}, u32[]{:S(2)}) copy-start(s32[16,4,8]{0,2,1:T(8,128)} %param.23) | copy-start | bytes 6148
  77.6 16.2 %copy-start.9 = (f32[16,4,8]{0,2,1:T(8,128)S(1)}, f32[16,4,8]{0,2,1:T(8,128)}, u32[]{:S(2)}) copy-start(f32[16,4,8]{0,2,1:T(8,128)} %param.24) | copy-start | bytes 6148
  77.6 16.9 %copy-start.11 = (bf16[2048]{0:T(1024)(128)(2,1)S(1)}, bf16[2048]{0:T(1024)(128)(2,1)}, u32[]{:S(2)}) copy-start(bf16[2048]{0:T(1024)(128)(2,1)} %param.22) | copy-start | bytes 12292
  86.6 12.9 %all-to-all-start.2 = ((bf16[8,64,256]{2,1,0:T(8,128)(2,1)}), bf16[8,64,256]{2,1,0:T(8,128)(2,1)S(1)}, u32[]{:S(2)}, u32[]{:S(2)}) async-start(bf16[8,64,256]{2,1,0:T(8,128)(2,1)} %bitcast.3), calls=%async_computation.2 | async-start | bytes 524288 | tf_op jit(solution)/shard_map/all_to_all | solution.py:33
  93.1 1.9 copy-start.7
  98.7 1.0 copy-start.6
  108.0 48.2 %copy-start = (bf16[256,256]{1,0:T(8,128)(2,1)S(1)}, bf16[256,256]{1,0:T(8,128)(2,1)}, u32[]{:S(2)}) copy-start(bf16[256,256]{1,0:T(8,128)(2,1)} %constant.4.clone.order_ref) | copy-start | bytes 393220
  108.0 48.2 %copy-start.1 = (bf16[256,256]{1,0:T(8,128)(2,1)S(1)}, bf16[256,256]{1,0:T(8,128)(2,1)}, u32[]{:S(2)}) copy-start(bf16[256,256]{1,0:T(8,128)(2,1)} %constant.5.clone.back_ref) | copy-start | bytes 393220
  108.0 48.2 %all-to-all-start.3 = ((bf16[64,48,512]{2,1,0:T(8,128)(2,1)}), bf16[64,48,512]{2,1,0:T(8,128)(2,1)S(1)}, u32[]{:S(2)}, u32[]{:S(2)}) async-start(bf16[64,48,512]{2,1,0:T(8,128)(2,1)} %bitcast.14), calls=%async_computation.3 | async-start | bytes 6291456 | tf_op jit(solution)/shard_map/all_to_all | solution.py:33
  115.9 4.7 %collective-permute-start.18 = (bf16[2048,512]{1,0:T(8,128)(2,1)}, bf16[2048,512]{1,0:T(8,128)(2,1)S(1)}, u32[]{:S(2)}, u32[]{:S(2)}) collective-permute-start(bf16[2048,512]{1,0:T(8,128)(2,1)} %bitcast.15), channel_id=1, source_target_pairs={{0,1},{1,0},{2,3},{3,2},{4,5},{5,4},{6,7},{7,6},{8,9},{9,8},{10,11... | collective-permute-start | bytes 6291464 | tf_op jit(solution)/shard_map/ppermute | solution.py:29
  116.6 7.0 %collective-permute-start.19 = (bf16[2048,512]{1,0:T(8,128)(2,1)}, bf16[2048,512]{1,0:T(8,128)(2,1)S(1)}, u32[]{:S(2)}, u32[]{:S(2)}) collective-permute-start(bf16[2048,512]{1,0:T(8,128)(2,1)} %bitcast.17), channel_id=1, source_target_pairs={{0,1},{1,0},{2,3},{3,2},{4,5},{5,4},{6,7},{7,6},{8,9},{9,8},{10,11... | collective-permute-start | bytes 6291464 | tf_op jit(solution)/shard_map/ppermute | solution.py:29
  116.7 10.0 %collective-permute-start.20 = (bf16[512,2048]{1,0:T(8,128)(2,1)}, bf16[512,2048]{1,0:T(8,128)(2,1)}, u32[]{:S(2)}, u32[]{:S(2)}) collective-permute-start(bf16[512,2048]{1,0:T(8,128)(2,1)} %bitcast.19), channel_id=1, source_target_pairs={{0,1},{1,0},{2,3},{3,2},{4,5},{5,4},{6,7},{7,6},{8,9},{9,8},{10,11... | collective-permute-start | bytes 6291464 | tf_op jit(solution)/shard_map/ppermute | solution.py:29
  120.6 3.0 %copy-start.4 = (bf16[2048,512]{1,0:T(8,128)(2,1)}, bf16[2048,512]{1,0:T(8,128)(2,1)S(1)}, u32[]{:S(2)}) copy-start(bf16[2048,512]{1,0:T(8,128)(2,1)S(1)} %collective-permute-done.18.gate_b_hbm) | copy-start | bytes 6291460
  123.6 1.3 copy-start.5
where the time goes:
time: 228 us; the launch traced here: 226 us
  waiting for transfers between devices  75.7 us (33%)
  blocking collectives  52.5 us (23%)
  starting transfers between devices  47.4 us (21%)
  Pallas kernels  41.6 us (18%)
  local copies, waits for them, and re-layouts  7.81 us (3%)
    all_to_all x1, blocking collectives, exchanged(): return lax.all_to_all(x, axes, split_axis=0, concat_axis=0, tiled=True)  52.5 us
    all_to_all x4, waiting for transfers between devices, exchanged(): return lax.all_to_all(x, axes, split_axis=0, concat_axis=0, tiled=True)  38.3 us
    ppermute x21, waiting for transfers between devices, shifted(): return lax.ppermute(x, axis, [(i, (i + by) % count) for i in range(count)])  37.4 us
    pallas_call x7, Pallas kernels, call(): pl.pallas_call(kernel, out_shape=out_shape, in_specs=vmem(len(args)), out...  27.9 us
    all_to_all x4, starting transfers between devices, exchanged(): return lax.all_to_all(x, axes, split_axis=0, concat_axis=0, tiled=True)  25.5 us
    ppermute x21, starting transfers between devices, shifted(): return lax.ppermute(x, axis, [(i, (i + by) % count) for i in range(count)])  21.8 us
    pallas_call x1, Pallas kernels, body(): pl.pallas_call(expert_kernel, out_shape=pltpu.VMEM((EXPERTS, PACK, step),...  13.8 us
  transfers between devices with their start and end apart: 25, of which 12 were waited for; matrix products, arithmetic and copies ran while one was open for 2% of the time, Pallas kernels for 8%

commit v1 on v0

--- a/solution.py
+++ b/solution.py
@@ -16,6 +16,7 @@
 WIDE = 8
 REST = CAP - WIDE
 GROUP = 16
+STEPS = 4
 
 norm_eps = 1e-05
 head_eps = 1e-06
@@ -29,6 +30,12 @@
     return lax.ppermute(x, axis, [(i, (i + by) % count) for i in range(count)])
 
 
+def swirled(x, by):
+    ways = lax.axis_size("y")
+    pairs = [(2 * y + c, 2 * ((y + (by if c == 0 else -by)) % ways) + c) for y in range(ways) for c in range(2)]
+    return lax.ppermute(x, ("y", "c"), pairs)
+
+
 def exchanged(x, axes):
     return lax.all_to_all(x, axes, split_axis=0, concat_axis=0, tiled=True)
 
@@ -41,38 +48,44 @@
     return v / (1.0 + jnp.exp(-v))
 
 
-def vmem(count):
-    return [pl.BlockSpec(memory_space=pltpu.VMEM)] * count
-
-
-class Inside:
-    def __init__(self, x):
-        self.x = x
-
-
-def placed_inside(x):
-    return Inside(pltpu.with_memory_space_constraint(x, pltpu.VMEM))
+INSIDE = pl.BlockSpec(memory_space=pltpu.VMEM)
+OUTSIDE = pl.BlockSpec(memory_space=pltpu.HBM)
+
+
+class Placed:
+    def __init__(self, x, spec, fixed):
+        self.x = x if fixed is None else pltpu.with_memory_space_constraint(x, fixed)
+        self.spec = spec
+
+
+def inside(x):
+    return Placed(x, INSIDE, pltpu.VMEM)
 
 
 def outside(x):
-    return pltpu.with_memory_space_constraint(x, pltpu.HBM)
-
-
-def limit(mib):
-    return pltpu.CompilerParams(vmem_limit_bytes=mib * 2**20)
-
-
-def call(kernel, out_shape, *args, scratch=(), mib=24):
-    several = isinstance(out_shape, (list, tuple))
-    args = [x.x if isinstance(x, Inside) else outside(x) for x in args]
+    return Placed(x, OUTSIDE, pltpu.HBM)
+
+
+def loaded(x):
+    return Placed(x, INSIDE, pltpu.HBM)
+
+
+def either(x):
+    return Placed(x, INSIDE, None)
+
+
+def call(kernel, out_shape, *args, out_specs=INSIDE, scratch=(), mib=24):
+    args = [x if isinstance(x, Placed) else loaded(x) for x in args]
+    if isinstance(out_shape, (list, tuple)) and not isinstance(out_specs, (list, tuple)):
+        out_specs = [out_specs] * len(out_shape)
     return pl.pallas_call(
         kernel,
         out_shape=out_shape,
-        in_specs=vmem(len(args)),
-        out_specs=vmem(len(out_shape)) if several else vmem(1)[0],
+        in_specs=[x.spec for x in args],
+        out_specs=out_specs,
         scratch_shapes=list(scratch),
-        compiler_params=limit(mib),
-    )(*args)
+        compiler_params=pltpu.CompilerParams(vmem_limit_bytes=mib * 2**20),
+    )(*[x.x for x in args])
 
 
 def route_kernel(ids_ref, ids_t_ref, weight_ref, send_ref, sum_ref):
@@ -117,55 +130,51 @@
     sum_ref[...] = jnp.where(match, jnp.concatenate([weight_all] * QUART, axis=0), 0.0).astype(BF)
 
 
-def local_kernel(*refs):
-    pieces, refs = refs[:10], refs[10:]
-    wk_ref, wv_ref, gain_ref, normed_ref, k_ref, v_ref, state_ref, own_ref = refs
+def copied(source, target, sem):
+    copy = pltpu.make_async_copy(source, target, sem)
+    copy.start()
+    return copy
+
+
+def block_order():
     y = lax.axis_index("y")
     c = lax.axis_index("c")
+    return [((y + away) & 3) * 2 + core for core in (c, 1 - c) for away in (0, 3 - 2 * core, 1 + 2 * core, 2)]
+
+
+def local_kernel(*refs):
+    pieces, refs = refs[:8], refs[8:]
+    wk_hbm, wv_hbm, gain_ref, normed_hbm, k_hbm, v_hbm, state_ref, own_ref, refs = *refs[:8], refs[8:]
+    normed_ref, k_ref, v_ref, wk_ref, wv_ref, in_sem, out_sem = refs
+    weight_copies = [copied(wk_hbm, wk_ref, in_sem.at[0]), copied(wv_hbm, wv_ref, in_sem.at[1])]
     rows, width = pieces[0].shape
-    half = rows // 2
-    blocks = []
-    for part, core in ((pieces[:5], c), (pieces[5:], 1 - c)):
-        for ref, away, lo, hi in (
-            (part[0], 0, 0, rows),
-            (part[1], 3, 0, rows),
-            (part[2], 1, 0, rows),
-            (part[3], 2, 0, half),
-            (part[4], 2, half, rows),
-        ):
-            blocks.append((ref, ((y + away) & 3) * 2 + core, lo, hi))
-    total = [jnp.zeros((half, 1), F32), jnp.zeros((half, 1), F32)]
-    for ref, block, lo, hi in blocks:
-        for h in range(lo // half, hi // half):
-            values = ref[pl.ds(h * half - lo, half), :].astype(F32)
-            total[h] = total[h] + jnp.sum(values * values, axis=1, keepdims=True)
-    scale = [lax.rsqrt(t / (8 * width) + norm_eps) for t in total]
-    mine = y * 2 + c
+    blocks = block_order()
+    total = jnp.zeros((rows, 1), F32)
+    for ref in pieces:
+        values = ref[...].astype(F32)
+        total = total + jnp.sum(values * values, axis=1, keepdims=True)
+    scale = lax.rsqrt(total / (8 * width) + norm_eps)
     own_rows = rows // 8
-    for ref, block, lo, hi in blocks:
-        gain = gain_ref[block]
+    start = pl.multiple_of((lax.axis_index("y") * 2 + lax.axis_index("c")) * own_rows, own_rows)
+    for ref, block in zip(pieces, blocks):
         columns = pl.ds(pl.multiple_of(block * width, width), width)
-        for h in range(lo // half, hi // half):
-            values = ref[pl.ds(h * half - lo, half), :].astype(F32)
-            normed_ref[pl.ds(h * half, half), columns] = (values * scale[h] * gain).astype(BF)
-        if lo == 0 and hi == rows:
-            own_ref[:, columns] = ref[pl.ds(pl.multiple_of(mine * own_rows, own_rows), own_rows), :]
-        else:
-            @pl.when((mine >= 4) == (lo > 0))
-            def _():
-                start = pl.multiple_of((mine & 3) * own_rows, own_rows)
-                own_ref[:, columns] = ref[pl.ds(start, own_rows), :]
-    normed = normed_ref[...]
-    k = silu(dot(normed, wk_ref[...])).astype(BF)
-    v = dot(normed, wv_ref[...]).astype(BF)
-    k_ref[...] = k
-    v_ref[...] = v
+        normed_ref[:, columns] = (ref[...].astype(F32) * scale * gain_ref[block]).astype(BF)
+        own_ref[:, columns] = ref[pl.ds(start, own_rows), :]
+    out_copies = [copied(normed_ref, normed_hbm, out_sem.at[0])]
+    weight_copies[0].wait()
+    k_ref[...] = silu(dot(normed_ref[...], wk_ref[...])).astype(BF)
+    out_copies.append(copied(k_ref, k_hbm, out_sem.at[1]))
+    weight_copies[1].wait()
+    v_ref[...] = dot(normed_ref[...], wv_ref[...]).astype(BF)
+    out_copies.append(copied(v_ref, v_hbm, out_sem.at[2]))
     sequence = lax.broadcasted_iota(jnp.int32, (rows, 128), 0) & 3
     for h in range(2):
         cols = slice(h * 128, (h + 1) * 128)
-        keys = k[:, cols].astype(F32)
+        keys = k_ref[:, cols].astype(F32)
         apart = jnp.concatenate([jnp.where(sequence == b, keys, 0.0).astype(BF) for b in range(4)], axis=1)
-        state_ref[h * rows : (h + 1) * rows, :] = dot(apart, v[:, cols], ((0,), (0,))).astype(BF)
+        state_ref[h * rows : (h + 1) * rows, :] = dot(apart, v_ref[:, cols], ((0,), (0,))).astype(BF)
+    for copy in out_copies:
+        copy.wait()
 
 
 def score_kernel(normed_ref, wq_ref, k_ref, v_ref, q_ref, local_ref):
@@ -201,26 +210,30 @@
 
 
 def dispatch_kernel(*refs):
-    weights, refs = refs[:10], refs[10:]
-    attended_ref, own_ref, gain_ref, send_table_ref, residual_ref, out_ref = refs
-    y = lax.axis_index("y")
-    c = lax.axis_index("c")
+    weights, refs = refs[:8], refs[8:]
+    attended_ref, own_ref, gain_ref, table_hbm, residual_ref, out_hbm, refs = *refs[:6], refs[6:]
+    weight_ref, table_ref, out_ref, weight_sem, table_sem, out_sem = refs
+    copies = [copied(source, weight_ref.at[i], weight_sem.at[i]) for i, source in enumerate(weights)]
+    table_copy = copied(table_hbm, table_ref, table_sem)
     _, width = own_ref.shape
     residual = own_ref[...].astype(F32)
-    for part, core in ((weights[:5], c), (weights[5:], 1 - c)):
-        for ref, away in ((part[0], 0), (part[1], 3), (part[2], 1)):
-            attended = attended_ref[((y + away) & 3) * 2 + core]
-            residual = residual + dot(attended, ref[...]).astype(BF).astype(F32)
-        attended = attended_ref[((y + 2) & 3) * 2 + core]
-        half = part[3].shape[0]
-        term = dot(attended[:, :half], part[3][...]) + dot(attended[:, half:], part[4][...])
-        residual = residual + term.astype(BF).astype(F32)
+    for i, block in enumerate(block_order()):
+        copies[i].wait()
+        residual = residual + dot(attended_ref[block], weight_ref[i]).astype(BF).astype(F32)
     residual_ref[...] = residual
     mean = jnp.mean(residual * residual, axis=1, keepdims=True)
     entering = (residual * lax.rsqrt(mean + norm_eps) * gain_ref[...].astype(F32)).astype(BF)
     step = width // QUART
     stacked = jnp.concatenate([entering[:, q * step : (q + 1) * step] for q in range(QUART)], axis=0)
-    out_ref[...] = dot(send_table_ref[...], stacked).astype(BF)
+    table_copy.wait()
+    size = COLS // STEPS
+    copies = []
+    for i in range(STEPS):
+        lines = pl.ds(i * size, size)
+        out_ref[lines, :] = dot(table_ref[lines, :], stacked).astype(BF)
+        copies.append(copied(out_ref.at[lines], out_hbm.at[lines], out_sem.at[i]))
+    for copy in copies:
+        copy.wait()
 
 
 def expert_kernel(
@@ -300,23 +313,23 @@
     hidden = expert_gate.shape[2]
     order = sorting()
 
+    attn_rows = attn_gain.astype(F32).reshape(8, 1, width)
+    head_row = head_gain.reshape(1, width)
+    moe_row = moe_gain.reshape(1, model)
     mine = tokens.reshape(rows, width)
-    from_left = shifted(mine, "y", 1)
-    from_right = shifted(mine, "y", -1)
-    far_low = shifted(from_left[: rows // 2], "y", 1)
-    far_high = shifted(from_right[rows // 2 :], "y", -1)
-    pieces = [mine, from_left, from_right, far_low, far_high]
+    first = swirled(mine, 1)
+    second = swirled(mine, -1)
+    far = swirled(first, 1)
+    pieces = [mine, first, second, far]
     pieces = pieces + [shifted(p, "c", 1) for p in pieces]
 
-    later_out, *pieces[5:] = lax.optimization_barrier((out_weight, *pieces[5:]))
-    out_left = shifted(later_out, "y", 1)
-    out_right = shifted(later_out, "y", -1)
-    out_half = out_weight.shape[0] // 2
-    out_low = shifted(out_left[:out_half], "y", 1)
-    out_high = shifted(out_right[out_half:], "y", -1)
-    projections = [out_weight, out_left, out_right, out_low, out_high]
+    later_out, *pieces[4:] = lax.optimization_barrier((out_weight, *pieces[4:]))
+    out_first = swirled(later_out, 1)
+    out_second = swirled(later_out, -1)
+    out_far = swirled(out_first, 1)
+    projections = [out_weight, out_first, out_second, out_far]
     projections = projections + [shifted(p, "c", 1) for p in projections[:3]]
-    projections = projections + [shifted(p, "c", 1) for p in projections[3:5]]
+    projections.append(shifted(out_far, "c", 1))
     gate = expert_gate.reshape(model, hidden)
     up = expert_up.reshape(model, hidden)
     down = expert_down.reshape(hidden, model)
@@ -342,50 +355,69 @@
             pltpu.VMEM((2 * rows, 128), BF),
             pltpu.HBM((own_rows, model), BF),
         ),
-        *[placed_inside(p) for p in pieces],
-        key_weight,
-        value_weight,
-        attn_gain.astype(F32).reshape(8, 1, width),
+        *[inside(p) for p in pieces],
+        outside(key_weight),
+        outside(value_weight),
+        attn_rows,
+        out_specs=[OUTSIDE, OUTSIDE, OUTSIDE, INSIDE, INSIDE],
+        scratch=[
+            pltpu.VMEM((rows, model), BF),
+            pltpu.VMEM((rows, width), BF),
+            pltpu.VMEM((rows, width), BF),
+            pltpu.VMEM((model, width), BF),
+            pltpu.VMEM((model, width), BF),
+            pltpu.SemaphoreType.DMA((2,)),
+            pltpu.SemaphoreType.DMA((3,)),
+        ],
     )
     q, local_mix = call(
         score_kernel, (pltpu.HBM((rows, width), BF), pltpu.HBM((rows, width), F32)), normed, query_weight, k, v
     )
     blocks = lax.axis_size(("x", "z"))
-    states = placed_inside(exchanged(state.reshape(blocks, 2 * rows // blocks, 128), ("x", "z")))
+    states = inside(exchanged(state.reshape(blocks, 2 * rows // blocks, 128), ("x", "z")))
     before = call(prefix_kernel, pltpu.HBM(states.x.shape, BF), states)
-    carried = placed_inside(exchanged(before, ("x", "z")).reshape(2 * rows, 128))
-    attended = call(mix_kernel, pltpu.VMEM((rows, width), BF), q, local_mix, carried, head_gain.reshape(1, width))
-    attended = placed_inside(exchanged(attended.reshape(8, own_rows, width), ("y", "c")))
+    carried = inside(exchanged(before, ("x", "z")).reshape(2 * rows, 128))
+    attended = call(mix_kernel, pltpu.VMEM((rows, width), BF), q, local_mix, carried, head_row)
+    attended = inside(exchanged(attended.reshape(8, own_rows, width), ("y", "c")))
     step = model // QUART
     residual, sending = call(
         dispatch_kernel,
         (pltpu.HBM((own_rows, model), F32), pltpu.HBM((COLS, step), BF)),
-        *projections,
+        *[outside(p) for p in projections],
         attended,
         own,
-        moe_gain.reshape(1, model),
-        send_table,
+        moe_row,
+        outside(send_table),
+        out_specs=[INSIDE, OUTSIDE],
+        scratch=[
+            pltpu.VMEM((8, width, model), BF),
+            pltpu.VMEM((COLS, QUART * own_rows), BF),
+            pltpu.VMEM((COLS, step), BF),
+            pltpu.SemaphoreType.DMA((8,)),
+            pltpu.SemaphoreType.DMA,
+            pltpu.SemaphoreType.DMA((STEPS,)),
+        ],
     )
     chips = ("x", "z", "y")
-    received = placed_inside(exchanged(sending.reshape(EXPERTS, PACK, step), chips))
-    inside, anywhere = vmem(1)[0], pl.BlockSpec(memory_space=pltpu.HBM)
-    results = pl.pallas_call(
+    received = inside(exchanged(sending.reshape(EXPERTS, PACK, step), chips))
+    results = call(
         expert_kernel,
-        out_shape=pltpu.VMEM((EXPERTS, PACK, step), BF),
-        in_specs=[inside] * 3 + [anywhere] * 6,
-        out_specs=inside,
-        scratch_shapes=[
+        pltpu.VMEM((EXPERTS, PACK, step), BF),
+        received,
+        either(jnp.asarray(order, BF)),
+        either(jnp.asarray(order.T, BF)),
+        *[outside(w) for w in (gate, up, down, other_gate, other_up, other_down)],
+        scratch=[
             pltpu.VMEM((EXPERTS * CAP, model), BF),
             pltpu.VMEM((2, model, hidden), BF),
             pltpu.VMEM((2, model, hidden), BF),
             pltpu.VMEM((2, hidden, model), BF),
             pltpu.SemaphoreType.DMA((2, 3)),
         ],
-        compiler_params=limit(36),
-        name="experts",
-    )(received.x, jnp.asarray(order, BF), jnp.asarray(order.T, BF), *[outside(w) for w in (gate, up, down, other_gate, other_up, other_down)])
-    returned = placed_inside(exchanged(results, chips).reshape(COLS, step))
-    out = call(combine_kernel, shape((own_rows, model), BF), returned, sum_table, residual)
+        mib=36,
+    )
+    returned = inside(exchanged(results, chips).reshape(COLS, step))
+    out = call(combine_kernel, shape((own_rows, model), BF), returned, either(sum_table), either(residual))
     return out.reshape(own_rows // batch, batch, model)
 
 

time: 228 us -> 238 us (1.044)
  blocking collectives: 52.5 us -> 68.2 us
  starting transfers between devices: 47.4 us -> 39 us
  waiting for transfers between devices: 75.7 us -> 81.3 us
    ppermute x0 -> x6, waiting for transfers between devices: none -> 40.1 us  [swirled(): return lax.ppermute(x, ('y', 'c'), pairs)]
    ppermute x21 -> x11, waiting for transfers between devices: 37.4 us -> 9.44 us  [shifted(): return lax.ppermute(x, axis, [(i, (i + by) % count) for i in range(count)])]
    all_to_all x1 -> x2, blocking collectives: 52.5 us -> 68.2 us  [exchanged(): return lax.all_to_all(x, axes, split_axis=0, concat_axis=0, tiled=True)]
    ppermute x0 -> x6, starting transfers between devices: none -> 10.4 us  [swirled(): return lax.ppermute(x, ('y', 'c'), pairs)]
    ppermute x21 -> x11, starting transfers between devices: 21.8 us -> 11.7 us  [shifted(): return lax.ppermute(x, axis, [(i, (i + by) % count) for i in range(count)])]
    all_to_all x4 -> x3, starting transfers between devices: 25.5 us -> 16.9 us  [exchanged(): return lax.all_to_all(x, axes, split_axis=0, concat_axis=0, tiled=True)]
    all_to_all x4 -> x3, waiting for transfers between devices: 38.3 us -> 31.8 us  [exchanged(): return lax.all_to_all(x, axes, split_axis=0, concat_axis=0, tiled=True)]
  transfers between devices with their start and end apart: 25 -> 20, of which waited for: 12 -> 11; matrix products, arithmetic and copies ran while one was open for 2% -> 2% of each run, Pallas kernels for 8% -> 8%
where the time goes in v1:
time: 238 us; the launch traced here: 236 us
  waiting for transfers between devices  81.3 us (34%)
  blocking collectives  68.2 us (29%)
  Pallas kernels  40.6 us (17%)
  starting transfers between devices  39 us (16%)
  local copies, waits for them, and re-layouts  5.84 us (2%)
    all_to_all x2, blocking collectives, exchanged(): return lax.all_to_all(x, axes, split_axis=0, concat_axis=0, tiled=True)  68.2 us
    pallas_call x8, Pallas kernels, call(): pl.pallas_call(kernel, out_shape=out_shape, in_specs=[x.spec for x in arg...  40.6 us
    ppermute x6, waiting for transfers between devices, swirled(): return lax.ppermute(x, ('y', 'c'), pairs)  40.1 us
    all_to_all x3, waiting for transfers between devices, exchanged(): return lax.all_to_all(x, axes, split_axis=0, concat_axis=0, tiled=True)  31.8 us
    all_to_all x3, starting transfers between devices, exchanged(): return lax.all_to_all(x, axes, split_axis=0, concat_axis=0, tiled=True)  16.9 us
    ppermute x11, starting transfers between devices, shifted(): return lax.ppermute(x, axis, [(i, (i + by) % count) for i in range(count)])  11.7 us
    ppermute x6, starting transfers between devices, swirled(): return lax.ppermute(x, ('y', 'c'), pairs)  10.4 us
    ppermute x11, waiting for transfers between devices, shifted(): return lax.ppermute(x, axis, [(i, (i + by) % count) for i in range(count)])  9.44 us
  transfers between devices with their start and end apart: 20, of which 11 were waited for; matrix products, arithmetic and copies ran while one was open for 2% of the time, Pallas kernels for 8%

profile of v1, /device:TPU:1, one launch (start us, length us, event | category | flops | bytes accessed | tf_op | source)
XLA Modules:
  0.0 236.4 jit_solution(16304374888546171304)
XLA Ops:
  0.0 1.0 reshape.47.refs_0_
  1.0 3.6 %collective-permute-start.1 = (bf16[512,256]{1,0:T(8,128)(2,1)S(1)}, bf16[512,256]{1,0:T(8,128)(2,1)S(1)}, u32[]{:S(2)}, u32[]{:S(2)}) collective-permute-start(bf16[512,256]{1,0:T(8,128)(2,1)S(1)} %reshape.47.refs_0_), channel_id=1, source_target_pairs={{0,2},{1,7},{2,4},{3,1},{4,6},{5,3},{6,0},{7,5},{8,10},{9,15},{10,... | collective-permute-start | bytes 786440 | tf_op jit(solution)/shard_map/ppermute | solution.py:36
  4.6 4.9 %collective-permute-done.1.refs_1_ = bf16[512,256]{1,0:T(8,128)(2,1)S(1)} collective-permute-done((bf16[512,256]{1,0:T(8,128)(2,1)S(1)}, bf16[512,256]{1,0:T(8,128)(2,1)S(1)}, u32[]{:S(2)}, u32[]{:S(2)}) %collective-permute-start.1) | collective-permute-done | bytes 262176 | tf_op jit(solution)/shard_map/ppermute | solution.py:36
  9.5 3.4 %collective-permute-start.5 = (bf16[512,256]{1,0:T(8,128)(2,1)S(1)}, bf16[512,256]{1,0:T(8,128)(2,1)S(1)}, u32[]{:S(2)}, u32[]{:S(2)}) collective-permute-start(bf16[512,256]{1,0:T(8,128)(2,1)S(1)} %collective-permute-done.1.refs_1_), channel_id=1, source_target_pairs={{0,2},{1,7},{2,4},{3,1},{4,6},{5,3},{6,0},{7,5},{8,10},{9,15},{10,... | collective-permute-start | bytes 786440 | tf_op jit(solution)/shard_map/ppermute | solution.py:36
  12.9 0.1 collective-permute-start
  13.0 0.4 collective-permute-start.2
  13.4 0.1 collective-permute-start.4
  13.5 2.7 %collective-permute-done.5.refs_3_ = bf16[512,256]{1,0:T(8,128)(2,1)S(1)} collective-permute-done((bf16[512,256]{1,0:T(8,128)(2,1)S(1)}, bf16[512,256]{1,0:T(8,128)(2,1)S(1)}, u32[]{:S(2)}, u32[]{:S(2)}) %collective-permute-start.5) | collective-permute-done | bytes 262176 | tf_op jit(solution)/shard_map/ppermute | solution.py:36
  16.2 2.5 %collective-permute-start.6 = (bf16[512,256]{1,0:T(8,128)(2,1)S(1)}, bf16[512,256]{1,0:T(8,128)(2,1)S(1)}, u32[]{:S(2)}, u32[]{:S(2)}) collective-permute-start(bf16[512,256]{1,0:T(8,128)(2,1)S(1)} %collective-permute-done.5.refs_3_), channel_id=1, source_target_pairs={{0,1},{1,0},{2,3},{3,2},{4,5},{5,4},{6,7},{7,6},{8,9},{9,8},{10,11... | collective-permute-start | bytes 786440 | tf_op jit(solution)/shard_map/ppermute | solution.py:30
  18.7 1.1 collective-permute-done.6.refs_7_
  19.9 1.5 collective-permute-start.7
  21.4 22.4 %collective-permute-done.7.refs_1_ = bf16[256,2048]{1,0:T(8,128)(2,1)S(1)} collective-permute-done((bf16[256,2048]{1,0:T(8,128)(2,1)}, bf16[256,2048]{1,0:T(8,128)(2,1)S(1)}, u32[]{:S(2)}, u32[]{:S(2)}) %collective-permute-start.7) | collective-permute-done | bytes 1048608 | tf_op jit(solution)/shard_map/ppermute | solution.py:36
  43.8 1.9 collective-permute-start.9
  45.6 1.5 collective-permute-start.10
  47.1 0.1 collective-permute-start.11
  47.2 0.4 collective-permute-start.12
  47.6 10.1 %collective-permute-done.9.refs_3_ = bf16[256,2048]{1,0:T(8,128)(2,1)S(1)} collective-permute-done((bf16[256,2048]{1,0:T(8,128)(2,1)S(1)}, bf16[256,2048]{1,0:T(8,128)(2,1)S(1)}, u32[]{:S(2)}, u32[]{:S(2)}) %collective-permute-start.9) | collective-permute-done | bytes 1048608 | tf_op jit(solution)/shard_map/ppermute | solution.py:36
  57.7 5.4 %collective-permute-start.13 = (bf16[256,2048]{1,0:T(8,128)(2,1)S(1)}, bf16[256,2048]{1,0:T(8,128)(2,1)}, u32[]{:S(2)}, u32[]{:S(2)}) collective-permute-start(bf16[256,2048]{1,0:T(8,128)(2,1)S(1)} %collective-permute-done.9.refs_3_), channel_id=1, source_target_pairs={{0,1},{1,0},{2,3},{3,2},{4,5},{5,4},{6,7},{7,6},{8,9},{9,8},{10,11... | collective-permute-start | bytes 3145736 | tf_op jit(solution)/shard_map/ppermute | solution.py:30
  63.1 1.3 reshape.63
  64.4 6.0 %shard_map.145 = (bf16[512,2048]{1,0:T(8,128)(2,1)}, bf16[512,256]{1,0:T(8,128)(2,1)}, bf16[512,256]{1,0:T(8,128)(2,1)}, bf16[1024,128]{1,0:T(8,128)(2,1)S(1)}, bf16[64,2048]{1,0:T(8,128)(2,1)}) custom-call(bf16[512,256]{1,0:T(8,128)(2,1)S(1)} %reshape.47.refs_0_, bf16[512,256]{1,0:T(8,128)(2,1)S(1)} %collective-permute-done.1.refs_1_, ...), custom_call_target="tpu_custom_call" | custom-call | tf_op jit(solution)/shard_map/pallas_call | solution.py:81
  70.4 15.6 %all_to_all.25.states_ref = bf16[16,64,128]{2,1,0:T(8,128)(2,1)S(1)} all-to-all(bf16[16,64,128]{2,1,0:T(8,128)(2,1)S(1)} %bitcast.14), channel_id=1, replica_groups=mesh['x'=4,'z'=4,'y'=4,'c'=2] {'x','z'}, dimensions={0} | all-to-all | bytes 524288 | tf_op jit(solution)/shard_map/all_to_all | solution.py:40
  86.1 0.7 shard_map.147
  86.8 3.9 %all-to-all-start.1 = ((bf16[16,64,128]{2,1,0:T(8,128)(2,1)}), bf16[16,64,128]{2,1,0:T(8,128)(2,1)S(1)}, u32[]{:S(2)}, u32[]{:S(2)}) async-start(bf16[16,64,128]{2,1,0:T(8,128)(2,1)} %shard_map.147), calls=%async_computation.1 | async-start | bytes 524288 | tf_op jit(solution)/shard_map/all_to_all | solution.py:40
  90.7 0.6 reshape.52.gain_ref
  91.3 5.2 %shard_map.146 = (bf16[512,256]{1,0:T(8,128)(2,1)}, f32[512,256]{1,0:T(8,128)}) custom-call(bf16[512,2048]{1,0:T(8,128)(2,1)} %get-tuple-element.26.normed_ref, bf16[2048,256]{1,0:T(8,128)(2,1)} %wq_ref.1, bf16[512,256]{1,0:T(8,128)(2,1)} %get-tuple-element.27.k_ref, bf16[512,256]{1,0:T(8,128)(2,1)} %get-tuple-element.28.v_ref), custom_call_target="tpu_custom_call" | custom-call | tf_op jit(solution)/shard_map/pallas_call | solution.py:81
  96.5 1.6 all-to-all-done.1
  98.0 2.3 shard_map.148
  100.4 5.9 %all-to-all-start.2 = ((bf16[8,64,256]{2,1,0:T(8,128)(2,1)}), bf16[8,64,256]{2,1,0:T(8,128)(2,1)S(1)}, u32[]{:S(2)}, u32[]{:S(2)}) async-start(bf16[8,64,256]{2,1,0:T(8,128)(2,1)} %bitcast.3), calls=%async_computation.2 | async-start | bytes 524288 | tf_op jit(solution)/shard_map/all_to_all | solution.py:40
  106.3 0.1 copy.19
  106.4 0.7 copy.20
  107.0 0.7 copy.21
  107.7 0.6 reshape.54.refs_10_
  108.3 3.7 %shard_map.149 = (bf16[3072,256]{1,0:T(8,128)(2,1)}, bf16[256,3072]{1,0:T(8,128)(2,1)}) custom-call(s32[64,8]{1,0:T(8,128)} %bitcast.23, s32[8,64]{1,0:T(8,128)} %bitcast.26, f32[64,8]{1,0:T(8,128)} %bitcast.24), custom_call_target="tpu_custom_call" | custom-call | tf_op jit(solution)/shard_map/pallas_call | solution.py:81
  112.1 0.7 all-to-all-done.2.refs_8_
  112.8 7.9 %shard_map.150 = (f32[64,2048]{1,0:T(8,128)}, bf16[3072,512]{1,0:T(8,128)(2,1)}) custom-call(bf16[256,2048]{1,0:T(8,128)(2,1)} %refs_0_.1, bf16[256,2048]{1,0:T(8,128)(2,1)} %copy-done.6, bf16[256,2048]{1,0:T(8,128)(2,1)} %copy-done.7, bf16[256,2048]{1,0:T(8,128)(2,1)} %copy-done.8, bf16[256,2048]{1,0:T(8,128)(2,1)} %collective-permute-done.10.refs_4_, ...), custom_call_target="tpu_custom_call" | custom-call | tf_op jit(solution)/shard_map/pallas_call | solution.py:81
  120.7 7.1 %all-to-all-start.3 = ((bf16[64,48,512]{2,1,0:T(8,128)(2,1)}), bf16[64,48,512]{2,1,0:T(8,128)(2,1)S(1)}, u32[]{:S(2)}, u32[]{:S(2)}) async-start(bf16[64,48,512]{2,1,0:T(8,128)(2,1)} %bitcast.15), calls=%async_computation.3 | async-start | bytes 6291456 | tf_op jit(solution)/shard_map/all_to_all | solution.py:40
  127.8 0.7 collective-permute-start.14
  128.6 0.1 collective-permute-start.15
  128.7 0.4 collective-permute-start.16
  129.1 3.5 %collective-permute-done.14.gate_b_hbm = bf16[2048,512]{1,0:T(8,128)(2,1)S(1)} collective-permute-done((bf16[2048,512]{1,0:T(8,128)(2,1)}, bf16[2048,512]{1,0:T(8,128)(2,1)S(1)}, u32[]{:S(2)}, u32[]{:S(2)}) %collective-permute-start.14) | collective-permute-done | bytes 2097184 | tf_op jit(solution)/shard_map/ppermute | solution.py:30
  132.6 3.0 %collective-permute-done.15.up_b_hbm = bf16[2048,512]{1,0:T(8,128)(2,1)S(1)} collective-permute-done((bf16[2048,512]{1,0:T(8,128)(2,1)}, bf16[2048,512]{1,0:T(8,128)(2,1)S(1)}, u32[]{:S(2)}, u32[]{:S(2)}) %collective-permute-start.15) | collective-permute-done | bytes 2097184 | tf_op jit(solution)/shard_map/ppermute | solution.py:30
  135.6 1.3 copy-done.5
  136.9 1.8 collective-permute-done.16.down_b_hbm
  138.7 29.5 %all-to-all-done.3.rows_ref = bf16[64,48,512]{2,1,0:T(8,128)(2,1)S(1)} async-done(((bf16[64,48,512]{2,1,0:T(8,128)(2,1)}), bf16[64,48,512]{2,1,0:T(8,128)(2,1)S(1)}, u32[]{:S(2)}, u32[]{:S(2)}) %all-to-all-start.3) | async-done | bytes 3145760 | tf_op jit(solution)/shard_map/all_to_all | solution.py:40
  168.2 13.8 %shard_map.151 = bf16[64,48,512]{2,1,0:T(8,128)(2,1)S(1)} custom-call(bf16[64,48,512]{2,1,0:T(8,128)(2,1)S(1)} %all-to-all-done.3.rows_ref, bf16[256,256]{1,0:T(8,128)(2,1)S(1)} %copy-done.2, bf16[256,256]{1,0:T(8,128)(2,1)S(1)} %copy-done.3, bf16[2048,512]{1,0:T(8,128)(2,1)} %bitcast.17, bf16[2048,512]{1,0:T(8,128)(2,1)} %bitcast.19, ...), custom_call_target="tpu_custom_call" | custom-call | tf_op jit(solution)/shard_map/pallas_call | solution.py:81
  182.0 52.6 %all_to_all.26 = bf16[64,48,512]{2,1,0:T(8,128)(2,1)S(1)} all-to-all(bf16[64,48,512]{2,1,0:T(8,128)(2,1)S(1)} %shard_map.151), channel_id=1, replica_groups=mesh['x'=4,'z'=4,'y'=4,'c'=2] {'x','z','y'}, dimensions={0} | all-to-all | bytes 6291456 | tf_op jit(solution)/shard_map/all_to_all | solution.py:40
  234.6 1.0 shard_map.152
  235.6 0.8 reshape.62
  (38 shorter events, 0.1 us)
Async XLA Ops:
  1.0 8.5 %collective-permute-start.1 = (bf16[512,256]{1,0:T(8,128)(2,1)S(1)}, bf16[512,256]{1,0:T(8,128)(2,1)S(1)}, u32[]{:S(2)}, u32[]{:S(2)}) collective-permute-start(bf16[512,256]{1,0:T(8,128)(2,1)S(1)} %reshape.47.refs_0_), channel_id=1, source_target_pairs={{0,2},{1,7},{2,4},{3,1},{4,6},{5,3},{6,0},{7,5},{8,10},{9,15},{10,... | collective-permute-start | bytes 786440 | tf_op jit(solution)/shard_map/ppermute | solution.py:36
  4.6 8.8 %collective-permute-start.3 = (bf16[512,256]{1,0:T(8,128)(2,1)S(1)}, bf16[512,256]{1,0:T(8,128)(2,1)S(1)}, u32[]{:S(2)}, u32[]{:S(2)}) collective-permute-start(bf16[512,256]{1,0:T(8,128)(2,1)S(1)} %reshape.47.refs_0_), channel_id=1, source_target_pairs={{0,6},{1,3},{2,0},{3,5},{4,2},{5,7},{6,4},{7,1},{8,14},{9,11},{10,... | collective-permute-start | bytes 786440 | tf_op jit(solution)/shard_map/ppermute | solution.py:36
  9.5 6.7 %collective-permute-start.5 = (bf16[512,256]{1,0:T(8,128)(2,1)S(1)}, bf16[512,256]{1,0:T(8,128)(2,1)S(1)}, u32[]{:S(2)}, u32[]{:S(2)}) collective-permute-start(bf16[512,256]{1,0:T(8,128)(2,1)S(1)} %collective-permute-done.1.refs_1_), channel_id=1, source_target_pairs={{0,2},{1,7},{2,4},{3,1},{4,6},{5,3},{6,0},{7,5},{8,10},{9,15},{10,... | collective-permute-start | bytes 786440 | tf_op jit(solution)/shard_map/ppermute | solution.py:36
  12.9 5.8 %collective-permute-start = (bf16[512,256]{1,0:T(8,128)(2,1)S(1)}, bf16[512,256]{1,0:T(8,128)(2,1)S(1)}, u32[]{:S(2)}, u32[]{:S(2)}) collective-permute-start(bf16[512,256]{1,0:T(8,128)(2,1)S(1)} %reshape.47.refs_0_), channel_id=1, source_target_pairs={{0,1},{1,0},{2,3},{3,2},{4,5},{5,4},{6,7},{7,6},{8,9},{9,8},{10,11... | collective-permute-start | bytes 786440 | tf_op jit(solution)/shard_map/ppermute | solution.py:30
  13.0 5.7 %collective-permute-start.2 = (bf16[512,256]{1,0:T(8,128)(2,1)S(1)}, bf16[512,256]{1,0:T(8,128)(2,1)S(1)}, u32[]{:S(2)}, u32[]{:S(2)}) collective-permute-start(bf16[512,256]{1,0:T(8,128)(2,1)S(1)} %collective-permute-done.1.refs_1_), channel_id=1, source_target_pairs={{0,1},{1,0},{2,3},{3,2},{4,5},{5,4},{6,7},{7,6},{8,9},{9,8},{10,11... | collective-permute-start | bytes 786440 | tf_op jit(solution)/shard_map/ppermute | solution.py:30
  13.4 5.3 %collective-permute-start.4 = (bf16[512,256]{1,0:T(8,128)(2,1)S(1)}, bf16[512,256]{1,0:T(8,128)(2,1)S(1)}, u32[]{:S(2)}, u32[]{:S(2)}) collective-permute-start(bf16[512,256]{1,0:T(8,128)(2,1)S(1)} %collective-permute-done.3.refs_2_), channel_id=1, source_target_pairs={{0,1},{1,0},{2,3},{3,2},{4,5},{5,4},{6,7},{7,6},{8,9},{9,8},{10,11... | collective-permute-start | bytes 786440 | tf_op jit(solution)/shard_map/ppermute | solution.py:30
  16.2 3.7 %collective-permute-start.6 = (bf16[512,256]{1,0:T(8,128)(2,1)S(1)}, bf16[512,256]{1,0:T(8,128)(2,1)S(1)}, u32[]{:S(2)}, u32[]{:S(2)}) collective-permute-start(bf16[512,256]{1,0:T(8,128)(2,1)S(1)} %collective-permute-done.5.refs_3_), channel_id=1, source_target_pairs={{0,1},{1,0},{2,3},{3,2},{4,5},{5,4},{6,7},{7,6},{8,9},{9,8},{10,11... | collective-permute-start | bytes 786440 | tf_op jit(solution)/shard_map/ppermute | solution.py:30
  19.9 23.9 %collective-permute-start.7 = (bf16[256,2048]{1,0:T(8,128)(2,1)}, bf16[256,2048]{1,0:T(8,128)(2,1)S(1)}, u32[]{:S(2)}, u32[]{:S(2)}) collective-permute-start(bf16[256,2048]{1,0:T(8,128)(2,1)} %refs_0_.1), channel_id=1, source_target_pairs={{0,2},{1,7},{2,4},{3,1},{4,6},{5,3},{6,0},{7,5},{8,10},{9,15},{10,... | collective-permute-start | bytes 3145736 | tf_op jit(solution)/shard_map/ppermute | solution.py:36
  21.4 25.8 %collective-permute-start.8 = (bf16[256,2048]{1,0:T(8,128)(2,1)}, bf16[256,2048]{1,0:T(8,128)(2,1)S(1)}, u32[]{:S(2)}, u32[]{:S(2)}) collective-permute-start(bf16[256,2048]{1,0:T(8,128)(2,1)} %refs_0_.1), channel_id=1, source_target_pairs={{0,6},{1,3},{2,0},{3,5},{4,2},{5,7},{6,4},{7,1},{8,14},{9,11},{10,... | collective-permute-start | bytes 3145736 | tf_op jit(solution)/shard_map/ppermute | solution.py:36
  43.8 26.6 %copy-start.6 = (bf16[256,2048]{1,0:T(8,128)(2,1)}, bf16[256,2048]{1,0:T(8,128)(2,1)S(1)}, u32[]{:S(2)}) copy-start(bf16[256,2048]{1,0:T(8,128)(2,1)S(1)} %collective-permute-done.7.refs_1_) | copy-start | bytes 3145732
  43.8 13.9 %collective-permute-start.9 = (bf16[256,2048]{1,0:T(8,128)(2,1)S(1)}, bf16[256,2048]{1,0:T(8,128)(2,1)S(1)}, u32[]{:S(2)}, u32[]{:S(2)}) collective-permute-start(bf16[256,2048]{1,0:T(8,128)(2,1)S(1)} %collective-permute-done.7.refs_1_), channel_id=1, source_target_pairs={{0,2},{1,7},{2,4},{3,1},{4,6},{5,3},{6,0},{7,5},{8,10},{9,15},{10,... | collective-permute-start | bytes 3145736 | tf_op jit(solution)/shard_map/ppermute | solution.py:36
  45.6 66.4 %collective-permute-start.10 = (bf16[256,2048]{1,0:T(8,128)(2,1)}, bf16[256,2048]{1,0:T(8,128)(2,1)}, u32[]{:S(2)}, u32[]{:S(2)}) collective-permute-start(bf16[256,2048]{1,0:T(8,128)(2,1)} %refs_0_.1), channel_id=1, source_target_pairs={{0,1},{1,0},{2,3},{3,2},{4,5},{5,4},{6,7},{7,6},{8,9},{9,8},{10,11... | collective-permute-start | bytes 3145736 | tf_op jit(solution)/shard_map/ppermute | solution.py:30
  47.1 65.7 %collective-permute-start.11 = (bf16[256,2048]{1,0:T(8,128)(2,1)S(1)}, bf16[256,2048]{1,0:T(8,128)(2,1)}, u32[]{:S(2)}, u32[]{:S(2)}) collective-permute-start(bf16[256,2048]{1,0:T(8,128)(2,1)S(1)} %collective-permute-done.7.refs_1_), channel_id=1, source_target_pairs={{0,1},{1,0},{2,3},{3,2},{4,5},{5,4},{6,7},{7,6},{8,9},{9,8},{10,11... | collective-permute-start | bytes 3145736 | tf_op jit(solution)/shard_map/ppermute | solution.py:30
  47.2 23.2 %copy-start.7 = (bf16[256,2048]{1,0:T(8,128)(2,1)}, bf16[256,2048]{1,0:T(8,128)(2,1)S(1)}, u32[]{:S(2)}) copy-start(bf16[256,2048]{1,0:T(8,128)(2,1)S(1)} %collective-permute-done.8.refs_2_) | copy-start | bytes 3145732
  47.2 65.6 %collective-permute-start.12 = (bf16[256,2048]{1,0:T(8,128)(2,1)S(1)}, bf16[256,2048]{1,0:T(8,128)(2,1)}, u32[]{:S(2)}, u32[]{:S(2)}) collective-permute-start(bf16[256,2048]{1,0:T(8,128)(2,1)S(1)} %collective-permute-done.8.refs_2_), channel_id=1, source_target_pairs={{0,1},{1,0},{2,3},{3,2},{4,5},{5,4},{6,7},{7,6},{8,9},{9,8},{10,11... | collective-permute-start | bytes 3145736 | tf_op jit(solution)/shard_map/ppermute | solution.py:30
  57.7 12.7 %copy-start.8 = (bf16[256,2048]{1,0:T(8,128)(2,1)}, bf16[256,2048]{1,0:T(8,128)(2,1)S(1)}, u32[]{:S(2)}) copy-start(bf16[256,2048]{1,0:T(8,128)(2,1)S(1)} %collective-permute-done.9.refs_3_) | copy-start | bytes 3145732
  57.7 55.1 %collective-permute-start.13 = (bf16[256,2048]{1,0:T(8,128)(2,1)S(1)}, bf16[256,2048]{1,0:T(8,128)(2,1)}, u32[]{:S(2)}, u32[]{:S(2)}) collective-permute-start(bf16[256,2048]{1,0:T(8,128)(2,1)S(1)} %collective-permute-done.9.refs_3_), channel_id=1, source_target_pairs={{0,1},{1,0},{2,3},{3,2},{4,5},{5,4},{6,7},{7,6},{8,9},{9,8},{10,11... | collective-permute-start | bytes 3145736 | tf_op jit(solution)/shard_map/ppermute | solution.py:30
  64.4 26.3 %copy-start.13 = (bf16[256]{0:T(256)(128)(2,1)S(1)}, bf16[256]{0:T(256)(128)(2,1)}, u32[]{:S(2)}) copy-start(bf16[256]{0:T(256)(128)(2,1)} %param.20) | copy-start | bytes 1540
  86.8 11.2 %all-to-all-start.1 = ((bf16[16,64,128]{2,1,0:T(8,128)(2,1)}), bf16[16,64,128]{2,1,0:T(8,128)(2,1)S(1)}, u32[]{:S(2)}, u32[]{:S(2)}) async-start(bf16[16,64,128]{2,1,0:T(8,128)(2,1)} %shard_map.147), calls=%async_computation.1 | async-start | bytes 524288 | tf_op jit(solution)/shard_map/all_to_all | solution.py:40
  91.3 15.0 %copy-start.10 = (s32[16,4,8]{0,2,1:T(8,128)S(1)}, s32[16,4,8]{0,2,1:T(8,128)}, u32[]{:S(2)}) copy-start(s32[16,4,8]{0,2,1:T(8,128)} %param.23) | copy-start | bytes 6148
  91.3 15.7 %copy-start.11 = (f32[16,4,8]{0,2,1:T(8,128)S(1)}, f32[16,4,8]{0,2,1:T(8,128)}, u32[]{:S(2)}) copy-start(f32[16,4,8]{0,2,1:T(8,128)} %param.24) | copy-start | bytes 6148
  91.3 16.4 %copy-start.12 = (bf16[2048]{0:T(1024)(128)(2,1)S(1)}, bf16[2048]{0:T(1024)(128)(2,1)}, u32[]{:S(2)}) copy-start(bf16[2048]{0:T(1024)(128)(2,1)} %param.22) | copy-start | bytes 12292
  100.4 12.4 %all-to-all-start.2 = ((bf16[8,64,256]{2,1,0:T(8,128)(2,1)}), bf16[8,64,256]{2,1,0:T(8,128)(2,1)S(1)}, u32[]{:S(2)}, u32[]{:S(2)}) async-start(bf16[8,64,256]{2,1,0:T(8,128)(2,1)} %bitcast.3), calls=%async_computation.2 | async-start | bytes 524288 | tf_op jit(solution)/shard_map/all_to_all | solution.py:40
  106.4 2.0 copy-start.9
  120.7 47.5 %copy-start.2 = (bf16[256,256]{1,0:T(8,128)(2,1)S(1)}, bf16[256,256]{1,0:T(8,128)(2,1)}, u32[]{:S(2)}) copy-start(bf16[256,256]{1,0:T(8,128)(2,1)} %constant.4.clone.order_ref) | copy-start | bytes 393220
  120.7 47.5 %copy-start.3 = (bf16[256,256]{1,0:T(8,128)(2,1)S(1)}, bf16[256,256]{1,0:T(8,128)(2,1)}, u32[]{:S(2)}) copy-start(bf16[256,256]{1,0:T(8,128)(2,1)} %constant.5.clone.back_ref) | copy-start | bytes 393220
  120.7 47.5 %all-to-all-start.3 = ((bf16[64,48,512]{2,1,0:T(8,128)(2,1)}), bf16[64,48,512]{2,1,0:T(8,128)(2,1)S(1)}, u32[]{:S(2)}, u32[]{:S(2)}) async-start(bf16[64,48,512]{2,1,0:T(8,128)(2,1)} %bitcast.15), calls=%async_computation.3 | async-start | bytes 6291456 | tf_op jit(solution)/shard_map/all_to_all | solution.py:40
  127.8 4.7 %collective-permute-start.14 = (bf16[2048,512]{1,0:T(8,128)(2,1)}, bf16[2048,512]{1,0:T(8,128)(2,1)S(1)}, u32[]{:S(2)}, u32[]{:S(2)}) collective-permute-start(bf16[2048,512]{1,0:T(8,128)(2,1)} %bitcast.16), channel_id=1, source_target_pairs={{0,1},{1,0},{2,3},{3,2},{4,5},{5,4},{6,7},{7,6},{8,9},{9,8},{10,11... | collective-permute-start | bytes 6291464 | tf_op jit(solution)/shard_map/ppermute | solution.py:30
  128.6 7.0 %collective-permute-start.15 = (bf16[2048,512]{1,0:T(8,128)(2,1)}, bf16[2048,512]{1,0:T(8,128)(2,1)S(1)}, u32[]{:S(2)}, u32[]{:S(2)}) collective-permute-start(bf16[2048,512]{1,0:T(8,128)(2,1)} %bitcast.18), channel_id=1, source_target_pairs={{0,1},{1,0},{2,3},{3,2},{4,5},{5,4},{6,7},{7,6},{8,9},{9,8},{10,11... | collective-permute-start | bytes 6291464 | tf_op jit(solution)/shard_map/ppermute | solution.py:30
  128.7 10.0 %collective-permute-start.16 = (bf16[512,2048]{1,0:T(8,128)(2,1)}, bf16[512,2048]{1,0:T(8,128)(2,1)}, u32[]{:S(2)}, u32[]{:S(2)}) collective-permute-start(bf16[512,2048]{1,0:T(8,128)(2,1)} %bitcast.20), channel_id=1, source_target_pairs={{0,1},{1,0},{2,3},{3,2},{4,5},{5,4},{6,7},{7,6},{8,9},{9,8},{10,11... | collective-permute-start | bytes 6291464 | tf_op jit(solution)/shard_map/ppermute | solution.py:30
  132.6 3.0 %copy-start.4 = (bf16[2048,512]{1,0:T(8,128)(2,1)}, bf16[2048,512]{1,0:T(8,128)(2,1)S(1)}, u32[]{:S(2)}) copy-start(bf16[2048,512]{1,0:T(8,128)(2,1)S(1)} %collective-permute-done.14.gate_b_hbm) | copy-start | bytes 6291460
  135.6 1.3 copy-start.5
  182.0 52.6 %copy-start = (bf16[256,3072]{1,0:T(8,128)(2,1)S(1)}, bf16[256,3072]{1,0:T(8,128)(2,1)}, u32[]{:S(2)}) copy-start(bf16[256,3072]{1,0:T(8,128)(2,1)} %get-tuple-element.35.table_ref) | copy-start | bytes 4718596
  182.0 52.6 %copy-start.1 = (f32[64,2048]{1,0:T(8,128)S(1)}, f32[64,2048]{1,0:T(8,128)}, u32[]{:S(2)}) copy-start(f32[64,2048]{1,0:T(8,128)} %get-tuple-element.36.residual_ref) | copy-start | bytes 1572868

commit v2 on v1

--- a/solution.py
+++ b/solution.py
@@ -16,7 +16,7 @@
 WIDE = 8
 REST = CAP - WIDE
 GROUP = 16
-STEPS = 4
+PARTS = 4
 
 norm_eps = 1e-05
 head_eps = 1e-06
@@ -88,13 +88,21 @@
     )(*[x.x for x in args])
 
 
-def route_kernel(ids_ref, ids_t_ref, weight_ref, send_ref, sum_ref):
-    rows = ids_ref.shape[0]
-    ids = ids_ref[...]
-    ids_t = ids_t_ref[...]
-    weights = weight_ref[...]
-    across = lax.broadcasted_iota(jnp.int32, (rows, EXPERTS), 1)
-    down = lax.broadcasted_iota(jnp.int32, (EXPERTS, rows), 0)
+def route_kernel(ids_ref, weight_ref, send_ref, sum_ref):
+    batch, _, span = ids_ref.shape
+    rows = batch * span
+    ids = jnp.zeros((rows, TOP), F32)
+    ids_t = jnp.zeros((TOP, rows), F32)
+    weights = jnp.zeros((rows, TOP), F32)
+    for b in range(batch):
+        row = lax.broadcasted_iota(jnp.int32, (span, rows), 1)
+        pick = jnp.where(lax.broadcasted_iota(jnp.int32, (span, rows), 0) * batch + b == row, 1.0, 0.0).astype(BF)
+        some = ids_ref[b].astype(F32).astype(BF)
+        ids = ids + dot(pick, some, ((0,), (1,)))
+        ids_t = ids_t + dot(some, pick)
+        weights = weights + dot(pick, weight_ref[b].astype(BF), ((0,), (1,)))
+    across = lax.broadcasted_iota(jnp.int32, (rows, EXPERTS), 1).astype(F32)
+    down = lax.broadcasted_iota(jnp.int32, (EXPERTS, rows), 0).astype(F32)
     named = jnp.zeros((rows, EXPERTS), F32)
     named_t = jnp.zeros((EXPERTS, rows), F32)
     weight = jnp.zeros((rows, EXPERTS), F32)
@@ -136,6 +144,17 @@
     return copy
 
 
+def copied_parts(source, target, sems):
+    size = source.shape[0] // PARTS
+    lines = [pl.ds(i * size, size) for i in range(PARTS)]
+    return [copied(source.at[line], target.at[line], sems.at[i]) for i, line in enumerate(lines)]
+
+
+def wait_all(copies):
+    for copy in copies:
+        copy.wait()
+
+
 def block_order():
     y = lax.axis_index("y")
     c = lax.axis_index("c")
@@ -145,8 +164,10 @@
 def local_kernel(*refs):
     pieces, refs = refs[:8], refs[8:]
     wk_hbm, wv_hbm, gain_ref, normed_hbm, k_hbm, v_hbm, state_ref, own_ref, refs = *refs[:8], refs[8:]
-    normed_ref, k_ref, v_ref, wk_ref, wv_ref, in_sem, out_sem = refs
-    weight_copies = [copied(wk_hbm, wk_ref, in_sem.at[0]), copied(wv_hbm, wv_ref, in_sem.at[1])]
+    normed_ref, k_ref, v_ref, wk_ref, wv_ref, gain_rows_ref, in_sem, out_sem = refs
+    k_copies = copied_parts(wk_hbm, wk_ref, in_sem.at[0])
+    v_copies = copied_parts(wv_hbm, wv_ref, in_sem.at[1])
+    gain_rows_ref[...] = gain_ref[...].astype(F32)
     rows, width = pieces[0].shape
     blocks = block_order()
     total = jnp.zeros((rows, 1), F32)
@@ -158,23 +179,23 @@
     start = pl.multiple_of((lax.axis_index("y") * 2 + lax.axis_index("c")) * own_rows, own_rows)
     for ref, block in zip(pieces, blocks):
         columns = pl.ds(pl.multiple_of(block * width, width), width)
-        normed_ref[:, columns] = (ref[...].astype(F32) * scale * gain_ref[block]).astype(BF)
+        gain = jnp.concatenate([gain_rows_ref[pl.ds(2 * block + i, 1), :] for i in range(2)], axis=1)
+        normed_ref[:, columns] = (ref[...].astype(F32) * scale * gain).astype(BF)
         own_ref[:, columns] = ref[pl.ds(start, own_rows), :]
-    out_copies = [copied(normed_ref, normed_hbm, out_sem.at[0])]
-    weight_copies[0].wait()
+    out_copies = copied_parts(normed_ref, normed_hbm, out_sem.at[0])
+    wait_all(k_copies)
     k_ref[...] = silu(dot(normed_ref[...], wk_ref[...])).astype(BF)
-    out_copies.append(copied(k_ref, k_hbm, out_sem.at[1]))
-    weight_copies[1].wait()
+    out_copies += copied_parts(k_ref, k_hbm, out_sem.at[1])
+    wait_all(v_copies)
     v_ref[...] = dot(normed_ref[...], wv_ref[...]).astype(BF)
-    out_copies.append(copied(v_ref, v_hbm, out_sem.at[2]))
+    out_copies += copied_parts(v_ref, v_hbm, out_sem.at[2])
     sequence = lax.broadcasted_iota(jnp.int32, (rows, 128), 0) & 3
     for h in range(2):
         cols = slice(h * 128, (h + 1) * 128)
         keys = k_ref[:, cols].astype(F32)
         apart = jnp.concatenate([jnp.where(sequence == b, keys, 0.0).astype(BF) for b in range(4)], axis=1)
         state_ref[h * rows : (h + 1) * rows, :] = dot(apart, v_ref[:, cols], ((0,), (0,))).astype(BF)
-    for copy in out_copies:
-        copy.wait()
+    wait_all(out_copies)
 
 
 def score_kernel(normed_ref, wq_ref, k_ref, v_ref, q_ref, local_ref):
@@ -206,47 +227,43 @@
         apart = jnp.concatenate([jnp.where(sequence == b, q, 0.0).astype(BF) for b in range(4)], axis=1)
         mixed = local_ref[:, cols] + dot(apart, carried_ref[h * rows : (h + 1) * rows, :])
         mean = jnp.mean(mixed * mixed, axis=1, keepdims=True)
-        out_ref[:, cols] = (mixed * lax.rsqrt(mean + head_eps) * gain_ref[:, cols].astype(F32)).astype(BF)
+        out_ref[:, cols] = (mixed * lax.rsqrt(mean + head_eps) * gain_ref[h : h + 1, :].astype(F32)).astype(BF)
 
 
 def dispatch_kernel(*refs):
     weights, refs = refs[:8], refs[8:]
-    attended_ref, own_ref, gain_ref, table_hbm, residual_ref, out_hbm, refs = *refs[:6], refs[6:]
-    weight_ref, table_ref, out_ref, weight_sem, table_sem, out_sem = refs
-    copies = [copied(source, weight_ref.at[i], weight_sem.at[i]) for i, source in enumerate(weights)]
-    table_copy = copied(table_hbm, table_ref, table_sem)
+    attended_ref, own_ref, gain_ref, table_hbm, residual_ref, out_ref, refs = *refs[:6], refs[6:]
+    weight_ref, table_ref, weight_sem, table_sem = refs
+    copies = [copied(source, weight_ref.at[i], weight_sem.at[i]) for i, source in enumerate(weights[:7])]
+    table_copies = copied_parts(table_hbm, table_ref, table_sem)
     _, width = own_ref.shape
     residual = own_ref[...].astype(F32)
     for i, block in enumerate(block_order()):
-        copies[i].wait()
-        residual = residual + dot(attended_ref[block], weight_ref[i]).astype(BF).astype(F32)
+        if i < 7:
+            copies[i].wait()
+        weight = weight_ref[i] if i < 7 else weights[7][...]
+        residual = residual + dot(attended_ref[block], weight).astype(BF).astype(F32)
     residual_ref[...] = residual
     mean = jnp.mean(residual * residual, axis=1, keepdims=True)
-    entering = (residual * lax.rsqrt(mean + norm_eps) * gain_ref[...].astype(F32)).astype(BF)
+    gain = gain_ref[...].astype(F32)
+    gain = jnp.concatenate([gain[i : i + 1, :] for i in range(gain.shape[0])], axis=1)
+    entering = (residual * lax.rsqrt(mean + norm_eps) * gain).astype(BF)
     step = width // QUART
     stacked = jnp.concatenate([entering[:, q * step : (q + 1) * step] for q in range(QUART)], axis=0)
-    table_copy.wait()
-    size = COLS // STEPS
-    copies = []
-    for i in range(STEPS):
-        lines = pl.ds(i * size, size)
-        out_ref[lines, :] = dot(table_ref[lines, :], stacked).astype(BF)
-        copies.append(copied(out_ref.at[lines], out_hbm.at[lines], out_sem.at[i]))
-    for copy in copies:
-        copy.wait()
+    wait_all(table_copies)
+    out_ref[...] = dot(table_ref[...], stacked).astype(BF)
 
 
 def expert_kernel(
     rows_ref, order_ref, back_ref, gate_hbm, up_hbm, down_hbm, gate_b_hbm, up_b_hbm, down_b_hbm, out_ref,
     x_ref, gate_ref, up_ref, down_ref, weight_sem,
 ):
+    targets = (gate_ref, up_ref, down_ref)
+    given = ((gate_hbm, up_hbm, down_hbm), (gate_b_hbm, up_b_hbm, down_b_hbm))
     copies = [
-        pltpu.make_async_copy(source, target.at[half], weight_sem.at[half, i])
-        for half, given in enumerate(((gate_hbm, up_hbm, down_hbm), (gate_b_hbm, up_b_hbm, down_b_hbm)))
-        for i, (source, target) in enumerate(zip(given, (gate_ref, up_ref, down_ref)))
+        [copied_parts(source, targets[i].at[half], weight_sem.at[half, i]) for i, source in enumerate(given[half])]
+        for half in range(2)
     ]
-    for copy in copies:
-        copy.start()
     sources, _, step = rows_ref.shape
     head = sources * WIDE
     part = GROUP * REST
@@ -264,12 +281,11 @@
         halves = []
         for half in range(2):
             if first:
-                copies[3 * half].wait()
-                copies[3 * half + 1].wait()
+                wait_all(copies[half][0] + copies[half][1])
             gated = dot(x_ref[lines, :], gate_ref[half])
             active = (silu(gated) * dot(x_ref[lines, :], up_ref[half])).astype(BF)
             if first:
-                copies[3 * half + 2].wait()
+                wait_all(copies[half][2])
             halves.append(dot(active, down_ref[half]).astype(BF))
         x_ref[lines, :] = (halves[0].astype(F32) + halves[1].astype(F32)).astype(BF)
     for q in range(QUART):
@@ -313,9 +329,9 @@
     hidden = expert_gate.shape[2]
     order = sorting()
 
-    attn_rows = attn_gain.astype(F32).reshape(8, 1, width)
-    head_row = head_gain.reshape(1, width)
-    moe_row = moe_gain.reshape(1, model)
+    attn_rows = attn_gain.reshape(-1, 128)
+    head_rows = head_gain.reshape(-1, 128)
+    moe_rows = moe_gain.reshape(-1, 128)
     mine = tokens.reshape(rows, width)
     first = swirled(mine, 1)
     second = swirled(mine, -1)
@@ -337,13 +353,11 @@
     other_up = shifted(up, "c", 1)
     other_down = shifted(down, "c", 1)
 
-    ids = route_ids.reshape(own_rows, TOP)
     send_table, sum_table = call(
         route_kernel,
         (pltpu.HBM((COLS, QUART * own_rows), BF), pltpu.HBM((QUART * own_rows, COLS), BF)),
-        ids,
-        ids.T,
-        route_weight.reshape(own_rows, TOP),
+        route_ids.transpose(1, 2, 0),
+        route_weight.transpose(1, 2, 0),
     )
 
     normed, k, v, state, own = call(
@@ -366,8 +380,9 @@
             pltpu.VMEM((rows, width), BF),
             pltpu.VMEM((model, width), BF),
             pltpu.VMEM((model, width), BF),
-            pltpu.SemaphoreType.DMA((2,)),
-            pltpu.SemaphoreType.DMA((3,)),
+            pltpu.VMEM(attn_rows.shape, F32),
+            pltpu.SemaphoreType.DMA((2, PARTS)),
+            pltpu.SemaphoreType.DMA((3, PARTS)),
         ],
     )
     q, local_mix = call(
@@ -377,25 +392,23 @@
     states = inside(exchanged(state.reshape(blocks, 2 * rows // blocks, 128), ("x", "z")))
     before = call(prefix_kernel, pltpu.HBM(states.x.shape, BF), states)
     carried = inside(exchanged(before, ("x", "z")).reshape(2 * rows, 128))
-    attended = call(mix_kernel, pltpu.VMEM((rows, width), BF), q, local_mix, carried, head_row)
+    attended = call(mix_kernel, pltpu.VMEM((rows, width), BF), q, local_mix, carried, head_rows)
     attended = inside(exchanged(attended.reshape(8, own_rows, width), ("y", "c")))
     step = model // QUART
     residual, sending = call(
         dispatch_kernel,
-        (pltpu.HBM((own_rows, model), F32), pltpu.HBM((COLS, step), BF)),
-        *[outside(p) for p in projections],
+        (pltpu.HBM((own_rows, model), F32), pltpu.VMEM((COLS, step), BF)),
+        *[outside(p) for p in projections[:7]],
+        inside(projections[7]),
         attended,
         own,
-        moe_row,
+        moe_rows,
         outside(send_table),
-        out_specs=[INSIDE, OUTSIDE],
         scratch=[
-            pltpu.VMEM((8, width, model), BF),
+            pltpu.VMEM((7, width, model), BF),
             pltpu.VMEM((COLS, QUART * own_rows), BF),
-            pltpu.VMEM((COLS, step), BF),
-            pltpu.SemaphoreType.DMA((8,)),
-            pltpu.SemaphoreType.DMA,
-            pltpu.SemaphoreType.DMA((STEPS,)),
+            pltpu.SemaphoreType.DMA((7,)),
+            pltpu.SemaphoreType.DMA((PARTS,)),
         ],
     )
     chips = ("x", "z", "y")
@@ -412,7 +425,7 @@
             pltpu.VMEM((2, model, hidden), BF),
             pltpu.VMEM((2, model, hidden), BF),
             pltpu.VMEM((2, hidden, model), BF),
-            pltpu.SemaphoreType.DMA((2, 3)),
+            pltpu.SemaphoreType.DMA((2, 3, PARTS)),
         ],
         mib=36,
     )

time: 238 us -> 233 us (0.979)
  transfers between devices with their start and end apart: 20 -> 20, of which waited for: 11 -> 11; matrix products, arithmetic and copies ran while one was open for 2% -> 0% of each run, Pallas kernels for 8% -> 8%
where the time goes in v2:
time: 233 us; the launch traced here: 231 us
  waiting for transfers between devices  80.8 us (35%)
  blocking collectives  68.2 us (29%)
  Pallas kernels  39.3 us (17%)
  starting transfers between devices  37.7 us (16%)
  local copies, waits for them, and re-layouts  4.79 us (2%)
    all_to_all x2, blocking collectives, exchanged(): return lax.all_to_all(x, axes, split_axis=0, concat_axis=0, tiled=True)  68.2 us
    ppermute x6, waiting for transfers between devices, swirled(): return lax.ppermute(x, ('y', 'c'), pairs)  40.2 us
    pallas_call x8, Pallas kernels, call(): pl.pallas_call(kernel, out_shape=out_shape, in_specs=[x.spec for x in arg...  39.3 us
    all_to_all x3, waiting for transfers between devices, exchanged(): return lax.all_to_all(x, axes, split_axis=0, concat_axis=0, tiled=True)  31.1 us
    all_to_all x3, starting transfers between devices, exchanged(): return lax.all_to_all(x, axes, split_axis=0, concat_axis=0, tiled=True)  15 us
    ppermute x11, starting transfers between devices, shifted(): return lax.ppermute(x, axis, [(i, (i + by) % count) for i in range(count)])  12.4 us
    ppermute x6, starting transfers between devices, swirled(): return lax.ppermute(x, ('y', 'c'), pairs)  10.4 us
    ppermute x11, waiting for transfers between devices, shifted(): return lax.ppermute(x, axis, [(i, (i + by) % count) for i in range(count)])  9.46 us
  transfers between devices with their start and end apart: 20, of which 11 were waited for; matrix products, arithmetic and copies ran while one was open for 0% of the time, Pallas kernels for 8%

profile of v2, /device:TPU:1, one launch (start us, length us, event | category | flops | bytes accessed | tf_op | source)
XLA Modules:
  0.0 230.9 jit_solution(1956093315049007443)
XLA Ops:
  0.0 1.0 reshape.39.refs_0_
  1.0 3.6 %collective-permute-start.1 = (bf16[512,256]{1,0:T(8,128)(2,1)S(1)}, bf16[512,256]{1,0:T(8,128)(2,1)S(1)}, u32[]{:S(2)}, u32[]{:S(2)}) collective-permute-start(bf16[512,256]{1,0:T(8,128)(2,1)S(1)} %reshape.39.refs_0_), channel_id=1, source_target_pairs={{0,2},{1,7},{2,4},{3,1},{4,6},{5,3},{6,0},{7,5},{8,10},{9,15},{10,... | collective-permute-start | bytes 786440 | tf_op jit(solution)/shard_map/ppermute | solution.py:36
  4.6 4.9 %collective-permute-done.1.refs_1_ = bf16[512,256]{1,0:T(8,128)(2,1)S(1)} collective-permute-done((bf16[512,256]{1,0:T(8,128)(2,1)S(1)}, bf16[512,256]{1,0:T(8,128)(2,1)S(1)}, u32[]{:S(2)}, u32[]{:S(2)}) %collective-permute-start.1) | collective-permute-done | bytes 262176 | tf_op jit(solution)/shard_map/ppermute | solution.py:36
  9.5 3.4 %collective-permute-start.5 = (bf16[512,256]{1,0:T(8,128)(2,1)S(1)}, bf16[512,256]{1,0:T(8,128)(2,1)S(1)}, u32[]{:S(2)}, u32[]{:S(2)}) collective-permute-start(bf16[512,256]{1,0:T(8,128)(2,1)S(1)} %collective-permute-done.1.refs_1_), channel_id=1, source_target_pairs={{0,2},{1,7},{2,4},{3,1},{4,6},{5,3},{6,0},{7,5},{8,10},{9,15},{10,... | collective-permute-start | bytes 786440 | tf_op jit(solution)/shard_map/ppermute | solution.py:36
  12.9 0.1 collective-permute-start
  13.0 0.4 collective-permute-start.2
  13.4 0.0 collective-permute-done.3.refs_2_
  13.4 0.1 collective-permute-start.4
  13.5 2.7 %collective-permute-done.5.refs_3_ = bf16[512,256]{1,0:T(8,128)(2,1)S(1)} collective-permute-done((bf16[512,256]{1,0:T(8,128)(2,1)S(1)}, bf16[512,256]{1,0:T(8,128)(2,1)S(1)}, u32[]{:S(2)}, u32[]{:S(2)}) %collective-permute-start.5) | collective-permute-done | bytes 262176 | tf_op jit(solution)/shard_map/ppermute | solution.py:36
  16.2 2.5 %collective-permute-start.6 = (bf16[512,256]{1,0:T(8,128)(2,1)S(1)}, bf16[512,256]{1,0:T(8,128)(2,1)S(1)}, u32[]{:S(2)}, u32[]{:S(2)}) collective-permute-start(bf16[512,256]{1,0:T(8,128)(2,1)S(1)} %collective-permute-done.5.refs_3_), channel_id=1, source_target_pairs={{0,1},{1,0},{2,3},{3,2},{4,5},{5,4},{6,7},{7,6},{8,9},{9,8},{10,11... | collective-permute-start | bytes 786440 | tf_op jit(solution)/shard_map/ppermute | solution.py:30
  18.7 0.0 collective-permute-done.2.refs_5_
  18.7 0.0 collective-permute-done.4.refs_6_
  18.7 1.1 collective-permute-done.6.refs_7_
  19.9 1.5 collective-permute-start.7
  21.4 0.0 collective-permute-start.8
  21.4 22.4 %collective-permute-done.7.refs_1_ = bf16[256,2048]{1,0:T(8,128)(2,1)S(1)} collective-permute-done((bf16[256,2048]{1,0:T(8,128)(2,1)}, bf16[256,2048]{1,0:T(8,128)(2,1)S(1)}, u32[]{:S(2)}, u32[]{:S(2)}) %collective-permute-start.7) | collective-permute-done | bytes 1048608 | tf_op jit(solution)/shard_map/ppermute | solution.py:36
  43.8 1.9 collective-permute-start.9
  45.6 1.5 collective-permute-start.10
  47.1 0.1 collective-permute-start.11
  47.2 0.0 collective-permute-done.8.refs_2_
  47.2 0.4 collective-permute-start.12
  47.6 10.2 %collective-permute-done.9.refs_3_ = bf16[256,2048]{1,0:T(8,128)(2,1)} collective-permute-done((bf16[256,2048]{1,0:T(8,128)(2,1)S(1)}, bf16[256,2048]{1,0:T(8,128)(2,1)}, u32[]{:S(2)}, u32[]{:S(2)}) %collective-permute-start.9) | collective-permute-done | bytes 1048608 | tf_op jit(solution)/shard_map/ppermute | solution.py:36
  57.8 5.4 %collective-permute-start.13 = (bf16[256,2048]{1,0:T(8,128)(2,1)}, bf16[256,2048]{1,0:T(8,128)(2,1)S(1)}, u32[]{:S(2)}, u32[]{:S(2)}) collective-permute-start(bf16[256,2048]{1,0:T(8,128)(2,1)} %collective-permute-done.9.refs_3_), channel_id=1, source_target_pairs={{0,1},{1,0},{2,3},{3,2},{4,5},{5,4},{6,7},{7,6},{8,9},{9,8},{10,11... | collective-permute-start | bytes 3145736 | tf_op jit(solution)/shard_map/ppermute | solution.py:30
  63.2 6.1 %shard_map.145 = (bf16[512,2048]{1,0:T(8,128)(2,1)}, bf16[512,256]{1,0:T(8,128)(2,1)}, bf16[512,256]{1,0:T(8,128)(2,1)}, bf16[1024,128]{1,0:T(8,128)(2,1)S(1)}, bf16[64,2048]{1,0:T(8,128)(2,1)}) custom-call(bf16[512,256]{1,0:T(8,128)(2,1)S(1)} %reshape.39.refs_0_, bf16[512,256]{1,0:T(8,128)(2,1)S(1)} %collective-permute-done.1.refs_1_, ...), custom_call_target="tpu_custom_call" | custom-call | tf_op jit(solution)/shard_map/pallas_call | solution.py:81
  69.4 15.6 %all_to_all.25.states_ref = bf16[16,64,128]{2,1,0:T(8,128)(2,1)S(1)} all-to-all(bf16[16,64,128]{2,1,0:T(8,128)(2,1)S(1)} %bitcast.16), channel_id=1, replica_groups=mesh['x'=4,'z'=4,'y'=4,'c'=2] {'x','z'}, dimensions={0} | all-to-all | bytes 524288 | tf_op jit(solution)/shard_map/all_to_all | solution.py:40
  85.0 0.7 shard_map.147
  85.7 3.9 %all-to-all-start.1 = ((bf16[16,64,128]{2,1,0:T(8,128)(2,1)}), bf16[16,64,128]{2,1,0:T(8,128)(2,1)S(1)}, u32[]{:S(2)}, u32[]{:S(2)}) async-start(bf16[16,64,128]{2,1,0:T(8,128)(2,1)} %shard_map.147), calls=%async_computation.1 | async-start | bytes 524288 | tf_op jit(solution)/shard_map/all_to_all | solution.py:40
  89.6 5.1 %shard_map.146 = (bf16[512,256]{1,0:T(8,128)(2,1)}, f32[512,256]{1,0:T(8,128)}) custom-call(bf16[512,2048]{1,0:T(8,128)(2,1)} %get-tuple-element.26.normed_ref, bf16[2048,256]{1,0:T(8,128)(2,1)} %wq_ref.1, bf16[512,256]{1,0:T(8,128)(2,1)} %get-tuple-element.27.k_ref, bf16[512,256]{1,0:T(8,128)(2,1)} %get-tuple-element.28.v_ref), custom_call_target="tpu_custom_call" | custom-call | tf_op jit(solution)/shard_map/pallas_call | solution.py:81
  94.7 2.2 all-to-all-done.1
  96.9 2.3 %shard_map.148 = bf16[512,256]{1,0:T(8,128)(2,1)} custom-call(bf16[512,256]{1,0:T(8,128)(2,1)} %get-tuple-element.29.q_ref, f32[512,256]{1,0:T(8,128)} %get-tuple-element.30.local_ref, bf16[1024,128]{1,0:T(8,128)(2,1)S(1)} %bitcast.15, bf16[2,128]{1,0:T(2,128)(2,1)} %bitcast.27), custom_call_target="tpu_custom_call" | custom-call | tf_op jit(solution)/shard_map/pallas_call | solution.py:81
  99.3 5.9 %all-to-all-start.2 = ((bf16[8,64,256]{2,1,0:T(8,128)(2,1)}), bf16[8,64,256]{2,1,0:T(8,128)(2,1)S(1)}, u32[]{:S(2)}, u32[]{:S(2)}) async-start(bf16[8,64,256]{2,1,0:T(8,128)(2,1)} %bitcast.4), calls=%async_computation.2 | async-start | bytes 524288 | tf_op jit(solution)/shard_map/all_to_all | solution.py:40
  105.2 4.0 %shard_map.149 = (bf16[3072,256]{1,0:T(8,128)(2,1)}, bf16[256,3072]{1,0:T(8,128)(2,1)}) custom-call(s32[4,8,16]{2,1,0:T(8,128)} %bitcast.23, f32[4,8,16]{2,1,0:T(8,128)} %bitcast.24), custom_call_target="tpu_custom_call" | custom-call | tf_op jit(solution)/shard_map/pallas_call | solution.py:81
  109.3 2.4 %all-to-all-done.2.refs_8_ = bf16[8,64,256]{2,1,0:T(8,128)(2,1)S(1)} async-done(((bf16[8,64,256]{2,1,0:T(8,128)(2,1)}), bf16[8,64,256]{2,1,0:T(8,128)(2,1)S(1)}, u32[]{:S(2)}, u32[]{:S(2)}) %all-to-all-start.2) | async-done | bytes 262176 | tf_op jit(solution)/shard_map/all_to_all | solution.py:40
  111.7 6.1 %shard_map.150 = (f32[64,2048]{1,0:T(8,128)}, bf16[3072,512]{1,0:T(8,128)(2,1)S(1)}) custom-call(bf16[256,2048]{1,0:T(8,128)(2,1)} %refs_0_.1, bf16[256,2048]{1,0:T(8,128)(2,1)} %copy-done.7, bf16[256,2048]{1,0:T(8,128)(2,1)} %copy-done.8, bf16[256,2048]{1,0:T(8,128)(2,1)} %collective-permute-done.9.refs_3_, ...), custom_call_target="tpu_custom_call" | custom-call | tf_op jit(solution)/shard_map/pallas_call | solution.py:81
  117.8 1.6 copy-done
  119.5 5.2 %all-to-all-start.3 = ((bf16[64,48,512]{2,1,0:T(8,128)(2,1)}), bf16[64,48,512]{2,1,0:T(8,128)(2,1)S(1)}, u32[]{:S(2)}, u32[]{:S(2)}) async-start(bf16[64,48,512]{2,1,0:T(8,128)(2,1)} %bitcast.14), calls=%async_computation.3 | async-start | bytes 6291456 | tf_op jit(solution)/shard_map/all_to_all | solution.py:40
  124.7 1.4 collective-permute-start.14
  126.1 0.1 collective-permute-start.15
  126.2 0.4 collective-permute-start.16
  126.6 3.5 %collective-permute-done.14.gate_b_hbm = bf16[2048,512]{1,0:T(8,128)(2,1)S(1)} collective-permute-done((bf16[2048,512]{1,0:T(8,128)(2,1)}, bf16[2048,512]{1,0:T(8,128)(2,1)S(1)}, u32[]{:S(2)}, u32[]{:S(2)}) %collective-permute-start.14) | collective-permute-done | bytes 2097184 | tf_op jit(solution)/shard_map/ppermute | solution.py:30
  130.1 3.0 %collective-permute-done.15.up_b_hbm = bf16[2048,512]{1,0:T(8,128)(2,1)S(1)} collective-permute-done((bf16[2048,512]{1,0:T(8,128)(2,1)}, bf16[2048,512]{1,0:T(8,128)(2,1)S(1)}, u32[]{:S(2)}, u32[]{:S(2)}) %collective-permute-start.15) | collective-permute-done | bytes 2097184 | tf_op jit(solution)/shard_map/ppermute | solution.py:30
  133.1 1.3 copy-done.6
  134.4 1.8 collective-permute-done.16.down_b_hbm
  136.2 26.5 %all-to-all-done.3.rows_ref = bf16[64,48,512]{2,1,0:T(8,128)(2,1)S(1)} async-done(((bf16[64,48,512]{2,1,0:T(8,128)(2,1)}), bf16[64,48,512]{2,1,0:T(8,128)(2,1)S(1)}, u32[]{:S(2)}, u32[]{:S(2)}) %all-to-all-start.3) | async-done | bytes 3145760 | tf_op jit(solution)/shard_map/all_to_all | solution.py:40
  162.7 13.9 %shard_map.151 = bf16[64,48,512]{2,1,0:T(8,128)(2,1)S(1)} custom-call(bf16[64,48,512]{2,1,0:T(8,128)(2,1)S(1)} %all-to-all-done.3.rows_ref, bf16[256,256]{1,0:T(8,128)(2,1)S(1)} %copy-done.3, bf16[256,256]{1,0:T(8,128)(2,1)S(1)} %copy-done.4, bf16[2048,512]{1,0:T(8,128)(2,1)} %bitcast.18, bf16[2048,512]{1,0:T(8,128)(2,1)} %bitcast.20, ...), custom_call_target="tpu_custom_call" | custom-call | tf_op jit(solution)/shard_map/pallas_call | solution.py:81
  176.6 52.6 %all_to_all.26 = bf16[64,48,512]{2,1,0:T(8,128)(2,1)S(1)} all-to-all(bf16[64,48,512]{2,1,0:T(8,128)(2,1)S(1)} %shard_map.151), channel_id=1, replica_groups=mesh['x'=4,'z'=4,'y'=4,'c'=2] {'x','z','y'}, dimensions={0} | all-to-all | bytes 6291456 | tf_op jit(solution)/shard_map/all_to_all | solution.py:40
  229.1 1.0 shard_map.152
  230.1 0.8 reshape.51
  (22 shorter events, 0.0 us)
Async XLA Ops:
  1.0 8.5 %collective-permute-start.1 = (bf16[512,256]{1,0:T(8,128)(2,1)S(1)}, bf16[512,256]{1,0:T(8,128)(2,1)S(1)}, u32[]{:S(2)}, u32[]{:S(2)}) collective-permute-start(bf16[512,256]{1,0:T(8,128)(2,1)S(1)} %reshape.39.refs_0_), channel_id=1, source_target_pairs={{0,2},{1,7},{2,4},{3,1},{4,6},{5,3},{6,0},{7,5},{8,10},{9,15},{10,... | collective-permute-start | bytes 786440 | tf_op jit(solution)/shard_map/ppermute | solution.py:36
  4.6 8.8 %collective-permute-start.3 = (bf16[512,256]{1,0:T(8,128)(2,1)S(1)}, bf16[512,256]{1,0:T(8,128)(2,1)S(1)}, u32[]{:S(2)}, u32[]{:S(2)}) collective-permute-start(bf16[512,256]{1,0:T(8,128)(2,1)S(1)} %reshape.39.refs_0_), channel_id=1, source_target_pairs={{0,6},{1,3},{2,0},{3,5},{4,2},{5,7},{6,4},{7,1},{8,14},{9,11},{10,... | collective-permute-start | bytes 786440 | tf_op jit(solution)/shard_map/ppermute | solution.py:36
  9.5 6.7 %collective-permute-start.5 = (bf16[512,256]{1,0:T(8,128)(2,1)S(1)}, bf16[512,256]{1,0:T(8,128)(2,1)S(1)}, u32[]{:S(2)}, u32[]{:S(2)}) collective-permute-start(bf16[512,256]{1,0:T(8,128)(2,1)S(1)} %collective-permute-done.1.refs_1_), channel_id=1, source_target_pairs={{0,2},{1,7},{2,4},{3,1},{4,6},{5,3},{6,0},{7,5},{8,10},{9,15},{10,... | collective-permute-start | bytes 786440 | tf_op jit(solution)/shard_map/ppermute | solution.py:36
  12.9 5.8 %collective-permute-start = (bf16[512,256]{1,0:T(8,128)(2,1)S(1)}, bf16[512,256]{1,0:T(8,128)(2,1)S(1)}, u32[]{:S(2)}, u32[]{:S(2)}) collective-permute-start(bf16[512,256]{1,0:T(8,128)(2,1)S(1)} %reshape.39.refs_0_), channel_id=1, source_target_pairs={{0,1},{1,0},{2,3},{3,2},{4,5},{5,4},{6,7},{7,6},{8,9},{9,8},{10,11... | collective-permute-start | bytes 786440 | tf_op jit(solution)/shard_map/ppermute | solution.py:30
  13.0 5.7 %collective-permute-start.2 = (bf16[512,256]{1,0:T(8,128)(2,1)S(1)}, bf16[512,256]{1,0:T(8,128)(2,1)S(1)}, u32[]{:S(2)}, u32[]{:S(2)}) collective-permute-start(bf16[512,256]{1,0:T(8,128)(2,1)S(1)} %collective-permute-done.1.refs_1_), channel_id=1, source_target_pairs={{0,1},{1,0},{2,3},{3,2},{4,5},{5,4},{6,7},{7,6},{8,9},{9,8},{10,11... | collective-permute-start | bytes 786440 | tf_op jit(solution)/shard_map/ppermute | solution.py:30
  13.4 5.3 %collective-permute-start.4 = (bf16[512,256]{1,0:T(8,128)(2,1)S(1)}, bf16[512,256]{1,0:T(8,128)(2,1)S(1)}, u32[]{:S(2)}, u32[]{:S(2)}) collective-permute-start(bf16[512,256]{1,0:T(8,128)(2,1)S(1)} %collective-permute-done.3.refs_2_), channel_id=1, source_target_pairs={{0,1},{1,0},{2,3},{3,2},{4,5},{5,4},{6,7},{7,6},{8,9},{9,8},{10,11... | collective-permute-start | bytes 786440 | tf_op jit(solution)/shard_map/ppermute | solution.py:30
  16.2 3.7 %collective-permute-start.6 = (bf16[512,256]{1,0:T(8,128)(2,1)S(1)}, bf16[512,256]{1,0:T(8,128)(2,1)S(1)}, u32[]{:S(2)}, u32[]{:S(2)}) collective-permute-start(bf16[512,256]{1,0:T(8,128)(2,1)S(1)} %collective-permute-done.5.refs_3_), channel_id=1, source_target_pairs={{0,1},{1,0},{2,3},{3,2},{4,5},{5,4},{6,7},{7,6},{8,9},{9,8},{10,11... | collective-permute-start | bytes 786440 | tf_op jit(solution)/shard_map/ppermute | solution.py:30
  19.9 23.9 %collective-permute-start.7 = (bf16[256,2048]{1,0:T(8,128)(2,1)}, bf16[256,2048]{1,0:T(8,128)(2,1)S(1)}, u32[]{:S(2)}, u32[]{:S(2)}) collective-permute-start(bf16[256,2048]{1,0:T(8,128)(2,1)} %refs_0_.1), channel_id=1, source_target_pairs={{0,2},{1,7},{2,4},{3,1},{4,6},{5,3},{6,0},{7,5},{8,10},{9,15},{10,... | collective-permute-start | bytes 3145736 | tf_op jit(solution)/shard_map/ppermute | solution.py:36
  21.4 25.8 %collective-permute-start.8 = (bf16[256,2048]{1,0:T(8,128)(2,1)}, bf16[256,2048]{1,0:T(8,128)(2,1)S(1)}, u32[]{:S(2)}, u32[]{:S(2)}) collective-permute-start(bf16[256,2048]{1,0:T(8,128)(2,1)} %refs_0_.1), channel_id=1, source_target_pairs={{0,6},{1,3},{2,0},{3,5},{4,2},{5,7},{6,4},{7,1},{8,14},{9,11},{10,... | collective-permute-start | bytes 3145736 | tf_op jit(solution)/shard_map/ppermute | solution.py:36
  43.8 25.6 %copy-start.7 = (bf16[256,2048]{1,0:T(8,128)(2,1)}, bf16[256,2048]{1,0:T(8,128)(2,1)S(1)}, u32[]{:S(2)}) copy-start(bf16[256,2048]{1,0:T(8,128)(2,1)S(1)} %collective-permute-done.7.refs_1_) | copy-start | bytes 3145732
  43.8 14.0 %collective-permute-start.9 = (bf16[256,2048]{1,0:T(8,128)(2,1)S(1)}, bf16[256,2048]{1,0:T(8,128)(2,1)}, u32[]{:S(2)}, u32[]{:S(2)}) collective-permute-start(bf16[256,2048]{1,0:T(8,128)(2,1)S(1)} %collective-permute-done.7.refs_1_), channel_id=1, source_target_pairs={{0,2},{1,7},{2,4},{3,1},{4,6},{5,3},{6,0},{7,5},{8,10},{9,15},{10,... | collective-permute-start | bytes 3145736 | tf_op jit(solution)/shard_map/ppermute | solution.py:36
  45.6 63.6 %collective-permute-start.10 = (bf16[256,2048]{1,0:T(8,128)(2,1)}, bf16[256,2048]{1,0:T(8,128)(2,1)}, u32[]{:S(2)}, u32[]{:S(2)}) collective-permute-start(bf16[256,2048]{1,0:T(8,128)(2,1)} %refs_0_.1), channel_id=1, source_target_pairs={{0,1},{1,0},{2,3},{3,2},{4,5},{5,4},{6,7},{7,6},{8,9},{9,8},{10,11... | collective-permute-start | bytes 3145736 | tf_op jit(solution)/shard_map/ppermute | solution.py:30
  47.1 64.6 %collective-permute-start.11 = (bf16[256,2048]{1,0:T(8,128)(2,1)S(1)}, bf16[256,2048]{1,0:T(8,128)(2,1)}, u32[]{:S(2)}, u32[]{:S(2)}) collective-permute-start(bf16[256,2048]{1,0:T(8,128)(2,1)S(1)} %collective-permute-done.7.refs_1_), channel_id=1, source_target_pairs={{0,1},{1,0},{2,3},{3,2},{4,5},{5,4},{6,7},{7,6},{8,9},{9,8},{10,11... | collective-permute-start | bytes 3145736 | tf_op jit(solution)/shard_map/ppermute | solution.py:30
  47.2 22.2 %copy-start.8 = (bf16[256,2048]{1,0:T(8,128)(2,1)}, bf16[256,2048]{1,0:T(8,128)(2,1)S(1)}, u32[]{:S(2)}) copy-start(bf16[256,2048]{1,0:T(8,128)(2,1)S(1)} %collective-permute-done.8.refs_2_) | copy-start | bytes 3145732
  47.2 64.5 %collective-permute-start.12 = (bf16[256,2048]{1,0:T(8,128)(2,1)S(1)}, bf16[256,2048]{1,0:T(8,128)(2,1)}, u32[]{:S(2)}, u32[]{:S(2)}) collective-permute-start(bf16[256,2048]{1,0:T(8,128)(2,1)S(1)} %collective-permute-done.8.refs_2_), channel_id=1, source_target_pairs={{0,1},{1,0},{2,3},{3,2},{4,5},{5,4},{6,7},{7,6},{8,9},{9,8},{10,11... | collective-permute-start | bytes 3145736 | tf_op jit(solution)/shard_map/ppermute | solution.py:30
  57.8 53.9 %collective-permute-start.13 = (bf16[256,2048]{1,0:T(8,128)(2,1)}, bf16[256,2048]{1,0:T(8,128)(2,1)S(1)}, u32[]{:S(2)}, u32[]{:S(2)}) collective-permute-start(bf16[256,2048]{1,0:T(8,128)(2,1)} %collective-permute-done.9.refs_3_), channel_id=1, source_target_pairs={{0,1},{1,0},{2,3},{3,2},{4,5},{5,4},{6,7},{7,6},{8,9},{9,8},{10,11... | collective-permute-start | bytes 3145736 | tf_op jit(solution)/shard_map/ppermute | solution.py:30
  85.7 11.2 %all-to-all-start.1 = ((bf16[16,64,128]{2,1,0:T(8,128)(2,1)}), bf16[16,64,128]{2,1,0:T(8,128)(2,1)S(1)}, u32[]{:S(2)}, u32[]{:S(2)}) async-start(bf16[16,64,128]{2,1,0:T(8,128)(2,1)} %shard_map.147), calls=%async_computation.1 | async-start | bytes 524288 | tf_op jit(solution)/shard_map/all_to_all | solution.py:40
  99.3 12.4 %all-to-all-start.2 = ((bf16[8,64,256]{2,1,0:T(8,128)(2,1)}), bf16[8,64,256]{2,1,0:T(8,128)(2,1)S(1)}, u32[]{:S(2)}, u32[]{:S(2)}) async-start(bf16[8,64,256]{2,1,0:T(8,128)(2,1)} %bitcast.4), calls=%async_computation.2 | async-start | bytes 524288 | tf_op jit(solution)/shard_map/all_to_all | solution.py:40
  117.8 1.6 copy-start
  119.5 43.2 %copy-start.3 = (bf16[256,256]{1,0:T(8,128)(2,1)S(1)}, bf16[256,256]{1,0:T(8,128)(2,1)}, u32[]{:S(2)}) copy-start(bf16[256,256]{1,0:T(8,128)(2,1)} %constant.4.clone.order_ref) | copy-start | bytes 393220
  119.5 43.2 %copy-start.4 = (bf16[256,256]{1,0:T(8,128)(2,1)S(1)}, bf16[256,256]{1,0:T(8,128)(2,1)}, u32[]{:S(2)}) copy-start(bf16[256,256]{1,0:T(8,128)(2,1)} %constant.5.clone.back_ref) | copy-start | bytes 393220
  119.5 43.2 %all-to-all-start.3 = ((bf16[64,48,512]{2,1,0:T(8,128)(2,1)}), bf16[64,48,512]{2,1,0:T(8,128)(2,1)S(1)}, u32[]{:S(2)}, u32[]{:S(2)}) async-start(bf16[64,48,512]{2,1,0:T(8,128)(2,1)} %bitcast.14), calls=%async_computation.3 | async-start | bytes 6291456 | tf_op jit(solution)/shard_map/all_to_all | solution.py:40
  124.7 5.4 %collective-permute-start.14 = (bf16[2048,512]{1,0:T(8,128)(2,1)}, bf16[2048,512]{1,0:T(8,128)(2,1)S(1)}, u32[]{:S(2)}, u32[]{:S(2)}) collective-permute-start(bf16[2048,512]{1,0:T(8,128)(2,1)} %bitcast.17), channel_id=1, source_target_pairs={{0,1},{1,0},{2,3},{3,2},{4,5},{5,4},{6,7},{7,6},{8,9},{9,8},{10,11... | collective-permute-start | bytes 6291464 | tf_op jit(solution)/shard_map/ppermute | solution.py:30
  126.1 7.0 %collective-permute-start.15 = (bf16[2048,512]{1,0:T(8,128)(2,1)}, bf16[2048,512]{1,0:T(8,128)(2,1)S(1)}, u32[]{:S(2)}, u32[]{:S(2)}) collective-permute-start(bf16[2048,512]{1,0:T(8,128)(2,1)} %bitcast.19), channel_id=1, source_target_pairs={{0,1},{1,0},{2,3},{3,2},{4,5},{5,4},{6,7},{7,6},{8,9},{9,8},{10,11... | collective-permute-start | bytes 6291464 | tf_op jit(solution)/shard_map/ppermute | solution.py:30
  126.2 10.0 %collective-permute-start.16 = (bf16[512,2048]{1,0:T(8,128)(2,1)}, bf16[512,2048]{1,0:T(8,128)(2,1)}, u32[]{:S(2)}, u32[]{:S(2)}) collective-permute-start(bf16[512,2048]{1,0:T(8,128)(2,1)} %bitcast.21), channel_id=1, source_target_pairs={{0,1},{1,0},{2,3},{3,2},{4,5},{5,4},{6,7},{7,6},{8,9},{9,8},{10,11... | collective-permute-start | bytes 6291464 | tf_op jit(solution)/shard_map/ppermute | solution.py:30
  130.1 3.0 %copy-start.5 = (bf16[2048,512]{1,0:T(8,128)(2,1)}, bf16[2048,512]{1,0:T(8,128)(2,1)S(1)}, u32[]{:S(2)}) copy-start(bf16[2048,512]{1,0:T(8,128)(2,1)S(1)} %collective-permute-done.14.gate_b_hbm) | copy-start | bytes 6291460
  133.1 1.3 copy-start.6
  176.5 52.6 %copy-start.1 = (bf16[256,3072]{1,0:T(8,128)(2,1)S(1)}, bf16[256,3072]{1,0:T(8,128)(2,1)}, u32[]{:S(2)}) copy-start(bf16[256,3072]{1,0:T(8,128)(2,1)} %get-tuple-element.35.table_ref) | copy-start | bytes 4718596
  176.5 52.6 %copy-start.2 = (f32[64,2048]{1,0:T(8,128)S(1)}, f32[64,2048]{1,0:T(8,128)}, u32[]{:S(2)}) copy-start(f32[64,2048]{1,0:T(8,128)} %get-tuple-element.36.residual_ref) | copy-start | bytes 1572868

commit v3 on v2

--- a/solution.py
+++ b/solution.py
@@ -163,10 +163,11 @@
 
 def local_kernel(*refs):
     pieces, refs = refs[:8], refs[8:]
-    wk_hbm, wv_hbm, gain_ref, normed_hbm, k_hbm, v_hbm, state_ref, own_ref, refs = *refs[:8], refs[8:]
-    normed_ref, k_ref, v_ref, wk_ref, wv_ref, gain_rows_ref, in_sem, out_sem = refs
+    wk_hbm, wv_hbm, wq_hbm, gain_ref, k_hbm, v_hbm, q_hbm, state_ref, own_ref, refs = *refs[:9], refs[9:]
+    normed_ref, k_ref, v_ref, q_ref, wk_ref, wv_ref, wq_ref, gain_rows_ref, in_sem, out_sem = refs
     k_copies = copied_parts(wk_hbm, wk_ref, in_sem.at[0])
     v_copies = copied_parts(wv_hbm, wv_ref, in_sem.at[1])
+    q_copies = copied_parts(wq_hbm, wq_ref, in_sem.at[2])
     gain_rows_ref[...] = gain_ref[...].astype(F32)
     rows, width = pieces[0].shape
     blocks = block_order()
@@ -182,13 +183,15 @@
         gain = jnp.concatenate([gain_rows_ref[pl.ds(2 * block + i, 1), :] for i in range(2)], axis=1)
         normed_ref[:, columns] = (ref[...].astype(F32) * scale * gain).astype(BF)
         own_ref[:, columns] = ref[pl.ds(start, own_rows), :]
-    out_copies = copied_parts(normed_ref, normed_hbm, out_sem.at[0])
     wait_all(k_copies)
     k_ref[...] = silu(dot(normed_ref[...], wk_ref[...])).astype(BF)
-    out_copies += copied_parts(k_ref, k_hbm, out_sem.at[1])
+    out_copies = copied_parts(k_ref, k_hbm, out_sem.at[0])
     wait_all(v_copies)
     v_ref[...] = dot(normed_ref[...], wv_ref[...]).astype(BF)
-    out_copies += copied_parts(v_ref, v_hbm, out_sem.at[2])
+    out_copies += copied_parts(v_ref, v_hbm, out_sem.at[1])
+    wait_all(q_copies)
+    q_ref[...] = silu(dot(normed_ref[...], wq_ref[...])).astype(BF)
+    out_copies += copied_parts(q_ref, q_hbm, out_sem.at[2])
     sequence = lax.broadcasted_iota(jnp.int32, (rows, 128), 0) & 3
     for h in range(2):
         cols = slice(h * 128, (h + 1) * 128)
@@ -198,16 +201,14 @@
     wait_all(out_copies)
 
 
-def score_kernel(normed_ref, wq_ref, k_ref, v_ref, q_ref, local_ref):
-    rows = normed_ref.shape[0]
-    q = silu(dot(normed_ref[...], wq_ref[...])).astype(BF)
-    q_ref[...] = q
+def score_kernel(q_ref, k_ref, v_ref, local_ref):
+    rows = q_ref.shape[0]
     i0 = lax.broadcasted_iota(jnp.int32, (rows, rows), 0)
     i1 = lax.broadcasted_iota(jnp.int32, (rows, rows), 1)
     seen = (((i0 ^ i1) & 3) == 0) & (i1 <= i0)
     for h in range(2):
         cols = slice(h * 128, (h + 1) * 128)
-        scores = jnp.where(seen, dot(q[:, cols], k_ref[:, cols], ((1,), (1,))), 0.0).astype(BF)
+        scores = jnp.where(seen, dot(q_ref[:, cols], k_ref[:, cols], ((1,), (1,))), 0.0).astype(BF)
         local_ref[:, cols] = dot(scores, v_ref[:, cols])
 
 
@@ -234,15 +235,16 @@
     weights, refs = refs[:8], refs[8:]
     attended_ref, own_ref, gain_ref, table_hbm, residual_ref, out_ref, refs = *refs[:6], refs[6:]
     weight_ref, table_ref, weight_sem, table_sem = refs
-    copies = [copied(source, weight_ref.at[i], weight_sem.at[i]) for i, source in enumerate(weights[:7])]
+    copies = [copied_parts(source, weight_ref.at[i], weight_sem.at[i]) for i, source in enumerate(weights[:7])]
     table_copies = copied_parts(table_hbm, table_ref, table_sem)
     _, width = own_ref.shape
     residual = own_ref[...].astype(F32)
-    for i, block in enumerate(block_order()):
+    blocks = block_order()
+    for i in (7, 0, 1, 2, 3, 4, 5, 6):
         if i < 7:
-            copies[i].wait()
+            wait_all(copies[i])
         weight = weight_ref[i] if i < 7 else weights[7][...]
-        residual = residual + dot(attended_ref[block], weight).astype(BF).astype(F32)
+        residual = residual + dot(attended_ref[blocks[i]], weight).astype(BF).astype(F32)
     residual_ref[...] = residual
     mean = jnp.mean(residual * residual, axis=1, keepdims=True)
     gain = gain_ref[...].astype(F32)
@@ -360,10 +362,10 @@
         route_weight.transpose(1, 2, 0),
     )
 
-    normed, k, v, state, own = call(
+    k, v, q, state, own = call(
         local_kernel,
         (
-            pltpu.HBM((rows, model), BF),
+            pltpu.HBM((rows, width), BF),
             pltpu.HBM((rows, width), BF),
             pltpu.HBM((rows, width), BF),
             pltpu.VMEM((2 * rows, 128), BF),
@@ -372,22 +374,23 @@
         *[inside(p) for p in pieces],
         outside(key_weight),
         outside(value_weight),
+        outside(query_weight),
         attn_rows,
         out_specs=[OUTSIDE, OUTSIDE, OUTSIDE, INSIDE, INSIDE],
         scratch=[
             pltpu.VMEM((rows, model), BF),
             pltpu.VMEM((rows, width), BF),
             pltpu.VMEM((rows, width), BF),
+            pltpu.VMEM((rows, width), BF),
+            pltpu.VMEM((model, width), BF),
             pltpu.VMEM((model, width), BF),
             pltpu.VMEM((model, width), BF),
             pltpu.VMEM(attn_rows.shape, F32),
-            pltpu.SemaphoreType.DMA((2, PARTS)),
+            pltpu.SemaphoreType.DMA((3, PARTS)),
             pltpu.SemaphoreType.DMA((3, PARTS)),
         ],
     )
-    q, local_mix = call(
-        score_kernel, (pltpu.HBM((rows, width), BF), pltpu.HBM((rows, width), F32)), normed, query_weight, k, v
-    )
+    local_mix = call(score_kernel, pltpu.HBM((rows, width), F32), q, k, v)
     blocks = lax.axis_size(("x", "z"))
     states = inside(exchanged(state.reshape(blocks, 2 * rows // blocks, 128), ("x", "z")))
     before = call(prefix_kernel, pltpu.HBM(states.x.shape, BF), states)
@@ -407,7 +410,7 @@
         scratch=[
             pltpu.VMEM((7, width, model), BF),
             pltpu.VMEM((COLS, QUART * own_rows), BF),
-            pltpu.SemaphoreType.DMA((7,)),
+            pltpu.SemaphoreType.DMA((7, PARTS)),
             pltpu.SemaphoreType.DMA((PARTS,)),
         ],
     )

time: 233 us -> 235 us (level)
  waiting for transfers between devices: 80.8 us -> 83.2 us
    all_to_all x3, waiting for transfers between devices: 31.1 us -> 33.6 us  [exchanged(): return lax.all_to_all(x, axes, split_axis=0, concat_axis=0, tiled=True)]
where the time goes in v3:
time: 235 us; the launch traced here: 232 us
  waiting for transfers between devices  83.2 us (35%)
  blocking collectives  68.2 us (29%)
  Pallas kernels  38.6 us (16%)
  starting transfers between devices  37.4 us (16%)
  local copies, waits for them, and re-layouts  4.8 us (2%)
    all_to_all x2, blocking collectives, exchanged(): return lax.all_to_all(x, axes, split_axis=0, concat_axis=0, tiled=True)  68.2 us
    ppermute x6, waiting for transfers between devices, swirled(): return lax.ppermute(x, ('y', 'c'), pairs)  40.2 us
    pallas_call x8, Pallas kernels, call(): pl.pallas_call(kernel, out_shape=out_shape, in_specs=[x.spec for x in arg...  38.6 us
    all_to_all x3, waiting for transfers between devices, exchanged(): return lax.all_to_all(x, axes, split_axis=0, concat_axis=0, tiled=True)  33.6 us
    all_to_all x3, starting transfers between devices, exchanged(): return lax.all_to_all(x, axes, split_axis=0, concat_axis=0, tiled=True)  14.7 us
    ppermute x11, starting transfers between devices, shifted(): return lax.ppermute(x, axis, [(i, (i + by) % count) for i in range(count)])  12.4 us
    ppermute x6, starting transfers between devices, swirled(): return lax.ppermute(x, ('y', 'c'), pairs)  10.4 us
    ppermute x11, waiting for transfers between devices, shifted(): return lax.ppermute(x, axis, [(i, (i + by) % count) for i in range(count)])  9.45 us
  transfers between devices with their start and end apart: 20, of which 11 were waited for; matrix products, arithmetic and copies ran while one was open for 0% of the time, Pallas kernels for 8%

profile of v3, /device:TPU:1, one launch (start us, length us, event | category | flops | bytes accessed | tf_op | source)
XLA Modules:
  0.0 232.4 jit_solution(15928657144640334970)
XLA Ops:
  0.0 1.0 reshape.39.refs_0_
  1.0 3.6 %collective-permute-start.1 = (bf16[512,256]{1,0:T(8,128)(2,1)S(1)}, bf16[512,256]{1,0:T(8,128)(2,1)S(1)}, u32[]{:S(2)}, u32[]{:S(2)}) collective-permute-start(bf16[512,256]{1,0:T(8,128)(2,1)S(1)} %reshape.39.refs_0_), channel_id=1, source_target_pairs={{0,2},{1,7},{2,4},{3,1},{4,6},{5,3},{6,0},{7,5},{8,10},{9,15},{10,... | collective-permute-start | bytes 786440 | tf_op jit(solution)/shard_map/ppermute | solution.py:36
  4.6 4.9 %collective-permute-done.1.refs_1_ = bf16[512,256]{1,0:T(8,128)(2,1)S(1)} collective-permute-done((bf16[512,256]{1,0:T(8,128)(2,1)S(1)}, bf16[512,256]{1,0:T(8,128)(2,1)S(1)}, u32[]{:S(2)}, u32[]{:S(2)}) %collective-permute-start.1) | collective-permute-done | bytes 262176 | tf_op jit(solution)/shard_map/ppermute | solution.py:36
  9.5 3.4 %collective-permute-start.5 = (bf16[512,256]{1,0:T(8,128)(2,1)S(1)}, bf16[512,256]{1,0:T(8,128)(2,1)S(1)}, u32[]{:S(2)}, u32[]{:S(2)}) collective-permute-start(bf16[512,256]{1,0:T(8,128)(2,1)S(1)} %collective-permute-done.1.refs_1_), channel_id=1, source_target_pairs={{0,2},{1,7},{2,4},{3,1},{4,6},{5,3},{6,0},{7,5},{8,10},{9,15},{10,... | collective-permute-start | bytes 786440 | tf_op jit(solution)/shard_map/ppermute | solution.py:36
  12.9 0.1 collective-permute-start
  13.0 0.4 collective-permute-start.2
  13.4 0.0 collective-permute-done.3.refs_2_
  13.4 0.1 collective-permute-start.4
  13.5 2.7 %collective-permute-done.5.refs_3_ = bf16[512,256]{1,0:T(8,128)(2,1)S(1)} collective-permute-done((bf16[512,256]{1,0:T(8,128)(2,1)S(1)}, bf16[512,256]{1,0:T(8,128)(2,1)S(1)}, u32[]{:S(2)}, u32[]{:S(2)}) %collective-permute-start.5) | collective-permute-done | bytes 262176 | tf_op jit(solution)/shard_map/ppermute | solution.py:36
  16.2 2.5 %collective-permute-start.6 = (bf16[512,256]{1,0:T(8,128)(2,1)S(1)}, bf16[512,256]{1,0:T(8,128)(2,1)S(1)}, u32[]{:S(2)}, u32[]{:S(2)}) collective-permute-start(bf16[512,256]{1,0:T(8,128)(2,1)S(1)} %collective-permute-done.5.refs_3_), channel_id=1, source_target_pairs={{0,1},{1,0},{2,3},{3,2},{4,5},{5,4},{6,7},{7,6},{8,9},{9,8},{10,11... | collective-permute-start | bytes 786440 | tf_op jit(solution)/shard_map/ppermute | solution.py:30
  18.7 0.0 collective-permute-done.2.refs_5_
  18.7 0.0 collective-permute-done.4.refs_6_
  18.7 1.1 collective-permute-done.6.refs_7_
  19.9 1.5 collective-permute-start.7
  21.4 0.0 collective-permute-start.8
  21.4 22.4 %collective-permute-done.7.refs_1_ = bf16[256,2048]{1,0:T(8,128)(2,1)S(1)} collective-permute-done((bf16[256,2048]{1,0:T(8,128)(2,1)}, bf16[256,2048]{1,0:T(8,128)(2,1)S(1)}, u32[]{:S(2)}, u32[]{:S(2)}) %collective-permute-start.7) | collective-permute-done | bytes 1048608 | tf_op jit(solution)/shard_map/ppermute | solution.py:36
  43.8 1.9 collective-permute-start.9
  45.6 1.5 collective-permute-start.10
  47.1 0.1 collective-permute-start.11
  47.2 0.0 collective-permute-done.8.refs_2_
  47.2 0.4 collective-permute-start.12
  47.6 10.2 %collective-permute-done.9.refs_3_ = bf16[256,2048]{1,0:T(8,128)(2,1)} collective-permute-done((bf16[256,2048]{1,0:T(8,128)(2,1)S(1)}, bf16[256,2048]{1,0:T(8,128)(2,1)}, u32[]{:S(2)}, u32[]{:S(2)}) %collective-permute-start.9) | collective-permute-done | bytes 1048608 | tf_op jit(solution)/shard_map/ppermute | solution.py:36
  57.8 5.4 %collective-permute-start.13 = (bf16[256,2048]{1,0:T(8,128)(2,1)}, bf16[256,2048]{1,0:T(8,128)(2,1)S(1)}, u32[]{:S(2)}, u32[]{:S(2)}) collective-permute-start(bf16[256,2048]{1,0:T(8,128)(2,1)} %collective-permute-done.9.refs_3_), channel_id=1, source_target_pairs={{0,1},{1,0},{2,3},{3,2},{4,5},{5,4},{6,7},{7,6},{8,9},{9,8},{10,11... | collective-permute-start | bytes 3145736 | tf_op jit(solution)/shard_map/ppermute | solution.py:30
  63.2 7.8 %shard_map.145 = (bf16[512,256]{1,0:T(8,128)(2,1)}, bf16[512,256]{1,0:T(8,128)(2,1)}, bf16[512,256]{1,0:T(8,128)(2,1)}, bf16[1024,128]{1,0:T(8,128)(2,1)S(1)}, bf16[64,2048]{1,0:T(8,128)(2,1)}) custom-call(bf16[512,256]{1,0:T(8,128)(2,1)S(1)} %reshape.39.refs_0_, bf16[512,256]{1,0:T(8,128)(2,1)S(1)} %collective-permute-done.1.refs_1_, ...), custom_call_target="tpu_custom_call" | custom-call | tf_op jit(solution)/shard_map/pallas_call | solution.py:81
  71.0 15.6 %all_to_all.25.states_ref = bf16[16,64,128]{2,1,0:T(8,128)(2,1)S(1)} all-to-all(bf16[16,64,128]{2,1,0:T(8,128)(2,1)S(1)} %bitcast.16), channel_id=1, replica_groups=mesh['x'=4,'z'=4,'y'=4,'c'=2] {'x','z'}, dimensions={0} | all-to-all | bytes 524288 | tf_op jit(solution)/shard_map/all_to_all | solution.py:40
  86.6 0.7 shard_map.147
  87.4 3.9 %all-to-all-start.1 = ((bf16[16,64,128]{2,1,0:T(8,128)(2,1)}), bf16[16,64,128]{2,1,0:T(8,128)(2,1)S(1)}, u32[]{:S(2)}, u32[]{:S(2)}) async-start(bf16[16,64,128]{2,1,0:T(8,128)(2,1)} %shard_map.147), calls=%async_computation.1 | async-start | bytes 524288 | tf_op jit(solution)/shard_map/all_to_all | solution.py:40
  91.3 2.7 %shard_map.146.local_ref = f32[512,256]{1,0:T(8,128)} custom-call(bf16[512,256]{1,0:T(8,128)(2,1)} %get-tuple-element.24.q_ref, bf16[512,256]{1,0:T(8,128)(2,1)} %get-tuple-element.25.k_ref, bf16[512,256]{1,0:T(8,128)(2,1)} %get-tuple-element.26.v_ref), custom_call_target="tpu_custom_call" | custom-call | tf_op jit(solution)/shard_map/pallas_call | solution.py:81
  94.0 4.6 %all-to-all-done.1 = bf16[16,64,128]{2,1,0:T(8,128)(2,1)S(1)} async-done(((bf16[16,64,128]{2,1,0:T(8,128)(2,1)}), bf16[16,64,128]{2,1,0:T(8,128)(2,1)S(1)}, u32[]{:S(2)}, u32[]{:S(2)}) %all-to-all-start.1) | async-done | bytes 262176 | tf_op jit(solution)/shard_map/all_to_all | solution.py:40
  98.6 2.3 %shard_map.148 = bf16[512,256]{1,0:T(8,128)(2,1)} custom-call(bf16[512,256]{1,0:T(8,128)(2,1)} %get-tuple-element.24.q_ref, f32[512,256]{1,0:T(8,128)} %shard_map.146.local_ref, bf16[1024,128]{1,0:T(8,128)(2,1)S(1)} %bitcast.15, bf16[2,128]{1,0:T(2,128)(2,1)} %bitcast.27), custom_call_target="tpu_custom_call" | custom-call | tf_op jit(solution)/shard_map/pallas_call | solution.py:81
  101.0 5.9 %all-to-all-start.2 = ((bf16[8,64,256]{2,1,0:T(8,128)(2,1)}), bf16[8,64,256]{2,1,0:T(8,128)(2,1)S(1)}, u32[]{:S(2)}, u32[]{:S(2)}) async-start(bf16[8,64,256]{2,1,0:T(8,128)(2,1)} %bitcast.4), calls=%async_computation.2 | async-start | bytes 524288 | tf_op jit(solution)/shard_map/all_to_all | solution.py:40
  106.8 4.1 %shard_map.149 = (bf16[3072,256]{1,0:T(8,128)(2,1)}, bf16[256,3072]{1,0:T(8,128)(2,1)}) custom-call(s32[4,8,16]{2,1,0:T(8,128)} %bitcast.23, f32[4,8,16]{2,1,0:T(8,128)} %bitcast.24), custom_call_target="tpu_custom_call" | custom-call | tf_op jit(solution)/shard_map/pallas_call | solution.py:81
  110.9 2.4 %all-to-all-done.2.refs_8_ = bf16[8,64,256]{2,1,0:T(8,128)(2,1)S(1)} async-done(((bf16[8,64,256]{2,1,0:T(8,128)(2,1)}), bf16[8,64,256]{2,1,0:T(8,128)(2,1)S(1)}, u32[]{:S(2)}, u32[]{:S(2)}) %all-to-all-start.2) | async-done | bytes 262176 | tf_op jit(solution)/shard_map/all_to_all | solution.py:40
  113.4 6.2 %shard_map.150 = (f32[64,2048]{1,0:T(8,128)}, bf16[3072,512]{1,0:T(8,128)(2,1)S(1)}) custom-call(bf16[256,2048]{1,0:T(8,128)(2,1)} %refs_0_.1, bf16[256,2048]{1,0:T(8,128)(2,1)} %copy-done.7, bf16[256,2048]{1,0:T(8,128)(2,1)} %copy-done.8, bf16[256,2048]{1,0:T(8,128)(2,1)} %collective-permute-done.9.refs_3_, ...), custom_call_target="tpu_custom_call" | custom-call | tf_op jit(solution)/shard_map/pallas_call | solution.py:81
  119.6 1.6 copy-done
  121.2 5.0 %all-to-all-start.3 = ((bf16[64,48,512]{2,1,0:T(8,128)(2,1)}), bf16[64,48,512]{2,1,0:T(8,128)(2,1)S(1)}, u32[]{:S(2)}, u32[]{:S(2)}) async-start(bf16[64,48,512]{2,1,0:T(8,128)(2,1)} %bitcast.14), calls=%async_computation.3 | async-start | bytes 6291456 | tf_op jit(solution)/shard_map/all_to_all | solution.py:40
  126.2 1.4 collective-permute-start.14
  127.6 0.1 collective-permute-start.15
  127.7 0.4 collective-permute-start.16
  128.1 3.5 %collective-permute-done.14.gate_b_hbm = bf16[2048,512]{1,0:T(8,128)(2,1)S(1)} collective-permute-done((bf16[2048,512]{1,0:T(8,128)(2,1)}, bf16[2048,512]{1,0:T(8,128)(2,1)S(1)}, u32[]{:S(2)}, u32[]{:S(2)}) %collective-permute-start.14) | collective-permute-done | bytes 2097184 | tf_op jit(solution)/shard_map/ppermute | solution.py:30
  131.6 3.0 %collective-permute-done.15.up_b_hbm = bf16[2048,512]{1,0:T(8,128)(2,1)S(1)} collective-permute-done((bf16[2048,512]{1,0:T(8,128)(2,1)}, bf16[2048,512]{1,0:T(8,128)(2,1)S(1)}, u32[]{:S(2)}, u32[]{:S(2)}) %collective-permute-start.15) | collective-permute-done | bytes 2097184 | tf_op jit(solution)/shard_map/ppermute | solution.py:30
  134.6 1.3 copy-done.6
  135.9 1.8 collective-permute-done.16.down_b_hbm
  137.7 26.5 %all-to-all-done.3.rows_ref = bf16[64,48,512]{2,1,0:T(8,128)(2,1)S(1)} async-done(((bf16[64,48,512]{2,1,0:T(8,128)(2,1)}), bf16[64,48,512]{2,1,0:T(8,128)(2,1)S(1)}, u32[]{:S(2)}, u32[]{:S(2)}) %all-to-all-start.3) | async-done | bytes 3145760 | tf_op jit(solution)/shard_map/all_to_all | solution.py:40
  164.2 13.8 %shard_map.151 = bf16[64,48,512]{2,1,0:T(8,128)(2,1)S(1)} custom-call(bf16[64,48,512]{2,1,0:T(8,128)(2,1)S(1)} %all-to-all-done.3.rows_ref, bf16[256,256]{1,0:T(8,128)(2,1)S(1)} %copy-done.3, bf16[256,256]{1,0:T(8,128)(2,1)S(1)} %copy-done.4, bf16[2048,512]{1,0:T(8,128)(2,1)} %bitcast.18, bf16[2048,512]{1,0:T(8,128)(2,1)} %bitcast.20, ...), custom_call_target="tpu_custom_call" | custom-call | tf_op jit(solution)/shard_map/pallas_call | solution.py:81
  178.1 52.6 %all_to_all.26 = bf16[64,48,512]{2,1,0:T(8,128)(2,1)S(1)} all-to-all(bf16[64,48,512]{2,1,0:T(8,128)(2,1)S(1)} %shard_map.151), channel_id=1, replica_groups=mesh['x'=4,'z'=4,'y'=4,'c'=2] {'x','z','y'}, dimensions={0} | all-to-all | bytes 6291456 | tf_op jit(solution)/shard_map/all_to_all | solution.py:40
  230.7 1.0 shard_map.152
  231.6 0.8 reshape.51
  (22 shorter events, 0.0 us)
Async XLA Ops:
  1.0 8.5 %collective-permute-start.1 = (bf16[512,256]{1,0:T(8,128)(2,1)S(1)}, bf16[512,256]{1,0:T(8,128)(2,1)S(1)}, u32[]{:S(2)}, u32[]{:S(2)}) collective-permute-start(bf16[512,256]{1,0:T(8,128)(2,1)S(1)} %reshape.39.refs_0_), channel_id=1, source_target_pairs={{0,2},{1,7},{2,4},{3,1},{4,6},{5,3},{6,0},{7,5},{8,10},{9,15},{10,... | collective-permute-start | bytes 786440 | tf_op jit(solution)/shard_map/ppermute | solution.py:36
  4.6 8.8 %collective-permute-start.3 = (bf16[512,256]{1,0:T(8,128)(2,1)S(1)}, bf16[512,256]{1,0:T(8,128)(2,1)S(1)}, u32[]{:S(2)}, u32[]{:S(2)}) collective-permute-start(bf16[512,256]{1,0:T(8,128)(2,1)S(1)} %reshape.39.refs_0_), channel_id=1, source_target_pairs={{0,6},{1,3},{2,0},{3,5},{4,2},{5,7},{6,4},{7,1},{8,14},{9,11},{10,... | collective-permute-start | bytes 786440 | tf_op jit(solution)/shard_map/ppermute | solution.py:36
  9.5 6.7 %collective-permute-start.5 = (bf16[512,256]{1,0:T(8,128)(2,1)S(1)}, bf16[512,256]{1,0:T(8,128)(2,1)S(1)}, u32[]{:S(2)}, u32[]{:S(2)}) collective-permute-start(bf16[512,256]{1,0:T(8,128)(2,1)S(1)} %collective-permute-done.1.refs_1_), channel_id=1, source_target_pairs={{0,2},{1,7},{2,4},{3,1},{4,6},{5,3},{6,0},{7,5},{8,10},{9,15},{10,... | collective-permute-start | bytes 786440 | tf_op jit(solution)/shard_map/ppermute | solution.py:36
  12.9 5.8 %collective-permute-start = (bf16[512,256]{1,0:T(8,128)(2,1)S(1)}, bf16[512,256]{1,0:T(8,128)(2,1)S(1)}, u32[]{:S(2)}, u32[]{:S(2)}) collective-permute-start(bf16[512,256]{1,0:T(8,128)(2,1)S(1)} %reshape.39.refs_0_), channel_id=1, source_target_pairs={{0,1},{1,0},{2,3},{3,2},{4,5},{5,4},{6,7},{7,6},{8,9},{9,8},{10,11... | collective-permute-start | bytes 786440 | tf_op jit(solution)/shard_map/ppermute | solution.py:30
  13.0 5.7 %collective-permute-start.2 = (bf16[512,256]{1,0:T(8,128)(2,1)S(1)}, bf16[512,256]{1,0:T(8,128)(2,1)S(1)}, u32[]{:S(2)}, u32[]{:S(2)}) collective-permute-start(bf16[512,256]{1,0:T(8,128)(2,1)S(1)} %collective-permute-done.1.refs_1_), channel_id=1, source_target_pairs={{0,1},{1,0},{2,3},{3,2},{4,5},{5,4},{6,7},{7,6},{8,9},{9,8},{10,11... | collective-permute-start | bytes 786440 | tf_op jit(solution)/shard_map/ppermute | solution.py:30
  13.4 5.3 %collective-permute-start.4 = (bf16[512,256]{1,0:T(8,128)(2,1)S(1)}, bf16[512,256]{1,0:T(8,128)(2,1)S(1)}, u32[]{:S(2)}, u32[]{:S(2)}) collective-permute-start(bf16[512,256]{1,0:T(8,128)(2,1)S(1)} %collective-permute-done.3.refs_2_), channel_id=1, source_target_pairs={{0,1},{1,0},{2,3},{3,2},{4,5},{5,4},{6,7},{7,6},{8,9},{9,8},{10,11... | collective-permute-start | bytes 786440 | tf_op jit(solution)/shard_map/ppermute | solution.py:30
  16.2 3.7 %collective-permute-start.6 = (bf16[512,256]{1,0:T(8,128)(2,1)S(1)}, bf16[512,256]{1,0:T(8,128)(2,1)S(1)}, u32[]{:S(2)}, u32[]{:S(2)}) collective-permute-start(bf16[512,256]{1,0:T(8,128)(2,1)S(1)} %collective-permute-done.5.refs_3_), channel_id=1, source_target_pairs={{0,1},{1,0},{2,3},{3,2},{4,5},{5,4},{6,7},{7,6},{8,9},{9,8},{10,11... | collective-permute-start | bytes 786440 | tf_op jit(solution)/shard_map/ppermute | solution.py:30
  19.9 23.9 %collective-permute-start.7 = (bf16[256,2048]{1,0:T(8,128)(2,1)}, bf16[256,2048]{1,0:T(8,128)(2,1)S(1)}, u32[]{:S(2)}, u32[]{:S(2)}) collective-permute-start(bf16[256,2048]{1,0:T(8,128)(2,1)} %refs_0_.1), channel_id=1, source_target_pairs={{0,2},{1,7},{2,4},{3,1},{4,6},{5,3},{6,0},{7,5},{8,10},{9,15},{10,... | collective-permute-start | bytes 3145736 | tf_op jit(solution)/shard_map/ppermute | solution.py:36
  21.4 25.8 %collective-permute-start.8 = (bf16[256,2048]{1,0:T(8,128)(2,1)}, bf16[256,2048]{1,0:T(8,128)(2,1)S(1)}, u32[]{:S(2)}, u32[]{:S(2)}) collective-permute-start(bf16[256,2048]{1,0:T(8,128)(2,1)} %refs_0_.1), channel_id=1, source_target_pairs={{0,6},{1,3},{2,0},{3,5},{4,2},{5,7},{6,4},{7,1},{8,14},{9,11},{10,... | collective-permute-start | bytes 3145736 | tf_op jit(solution)/shard_map/ppermute | solution.py:36
  43.8 27.2 %copy-start.7 = (bf16[256,2048]{1,0:T(8,128)(2,1)}, bf16[256,2048]{1,0:T(8,128)(2,1)S(1)}, u32[]{:S(2)}) copy-start(bf16[256,2048]{1,0:T(8,128)(2,1)S(1)} %collective-permute-done.7.refs_1_) | copy-start | bytes 3145732
  43.8 14.0 %collective-permute-start.9 = (bf16[256,2048]{1,0:T(8,128)(2,1)S(1)}, bf16[256,2048]{1,0:T(8,128)(2,1)}, u32[]{:S(2)}, u32[]{:S(2)}) collective-permute-start(bf16[256,2048]{1,0:T(8,128)(2,1)S(1)} %collective-permute-done.7.refs_1_), channel_id=1, source_target_pairs={{0,2},{1,7},{2,4},{3,1},{4,6},{5,3},{6,0},{7,5},{8,10},{9,15},{10,... | collective-permute-start | bytes 3145736 | tf_op jit(solution)/shard_map/ppermute | solution.py:36
  45.6 65.3 %collective-permute-start.10 = (bf16[256,2048]{1,0:T(8,128)(2,1)}, bf16[256,2048]{1,0:T(8,128)(2,1)}, u32[]{:S(2)}, u32[]{:S(2)}) collective-permute-start(bf16[256,2048]{1,0:T(8,128)(2,1)} %refs_0_.1), channel_id=1, source_target_pairs={{0,1},{1,0},{2,3},{3,2},{4,5},{5,4},{6,7},{7,6},{8,9},{9,8},{10,11... | collective-permute-start | bytes 3145736 | tf_op jit(solution)/shard_map/ppermute | solution.py:30
  47.1 66.3 %collective-permute-start.11 = (bf16[256,2048]{1,0:T(8,128)(2,1)S(1)}, bf16[256,2048]{1,0:T(8,128)(2,1)}, u32[]{:S(2)}, u32[]{:S(2)}) collective-permute-start(bf16[256,2048]{1,0:T(8,128)(2,1)S(1)} %collective-permute-done.7.refs_1_), channel_id=1, source_target_pairs={{0,1},{1,0},{2,3},{3,2},{4,5},{5,4},{6,7},{7,6},{8,9},{9,8},{10,11... | collective-permute-start | bytes 3145736 | tf_op jit(solution)/shard_map/ppermute | solution.py:30
  47.2 23.8 %copy-start.8 = (bf16[256,2048]{1,0:T(8,128)(2,1)}, bf16[256,2048]{1,0:T(8,128)(2,1)S(1)}, u32[]{:S(2)}) copy-start(bf16[256,2048]{1,0:T(8,128)(2,1)S(1)} %collective-permute-done.8.refs_2_) | copy-start | bytes 3145732
  47.2 66.2 %collective-permute-start.12 = (bf16[256,2048]{1,0:T(8,128)(2,1)S(1)}, bf16[256,2048]{1,0:T(8,128)(2,1)}, u32[]{:S(2)}, u32[]{:S(2)}) collective-permute-start(bf16[256,2048]{1,0:T(8,128)(2,1)S(1)} %collective-permute-done.8.refs_2_), channel_id=1, source_target_pairs={{0,1},{1,0},{2,3},{3,2},{4,5},{5,4},{6,7},{7,6},{8,9},{9,8},{10,11... | collective-permute-start | bytes 3145736 | tf_op jit(solution)/shard_map/ppermute | solution.py:30
  57.8 55.5 %collective-permute-start.13 = (bf16[256,2048]{1,0:T(8,128)(2,1)}, bf16[256,2048]{1,0:T(8,128)(2,1)S(1)}, u32[]{:S(2)}, u32[]{:S(2)}) collective-permute-start(bf16[256,2048]{1,0:T(8,128)(2,1)} %collective-permute-done.9.refs_3_), channel_id=1, source_target_pairs={{0,1},{1,0},{2,3},{3,2},{4,5},{5,4},{6,7},{7,6},{8,9},{9,8},{10,11... | collective-permute-start | bytes 3145736 | tf_op jit(solution)/shard_map/ppermute | solution.py:30
  87.4 11.2 %all-to-all-start.1 = ((bf16[16,64,128]{2,1,0:T(8,128)(2,1)}), bf16[16,64,128]{2,1,0:T(8,128)(2,1)S(1)}, u32[]{:S(2)}, u32[]{:S(2)}) async-start(bf16[16,64,128]{2,1,0:T(8,128)(2,1)} %shard_map.147), calls=%async_computation.1 | async-start | bytes 524288 | tf_op jit(solution)/shard_map/all_to_all | solution.py:40
  101.0 12.4 %all-to-all-start.2 = ((bf16[8,64,256]{2,1,0:T(8,128)(2,1)}), bf16[8,64,256]{2,1,0:T(8,128)(2,1)S(1)}, u32[]{:S(2)}, u32[]{:S(2)}) async-start(bf16[8,64,256]{2,1,0:T(8,128)(2,1)} %bitcast.4), calls=%async_computation.2 | async-start | bytes 524288 | tf_op jit(solution)/shard_map/all_to_all | solution.py:40
  119.6 1.6 copy-start
  121.2 43.0 %copy-start.3 = (bf16[256,256]{1,0:T(8,128)(2,1)S(1)}, bf16[256,256]{1,0:T(8,128)(2,1)}, u32[]{:S(2)}) copy-start(bf16[256,256]{1,0:T(8,128)(2,1)} %constant.4.clone.order_ref) | copy-start | bytes 393220
  121.2 43.0 %copy-start.4 = (bf16[256,256]{1,0:T(8,128)(2,1)S(1)}, bf16[256,256]{1,0:T(8,128)(2,1)}, u32[]{:S(2)}) copy-start(bf16[256,256]{1,0:T(8,128)(2,1)} %constant.5.clone.back_ref) | copy-start | bytes 393220
  121.2 43.0 %all-to-all-start.3 = ((bf16[64,48,512]{2,1,0:T(8,128)(2,1)}), bf16[64,48,512]{2,1,0:T(8,128)(2,1)S(1)}, u32[]{:S(2)}, u32[]{:S(2)}) async-start(bf16[64,48,512]{2,1,0:T(8,128)(2,1)} %bitcast.14), calls=%async_computation.3 | async-start | bytes 6291456 | tf_op jit(solution)/shard_map/all_to_all | solution.py:40
  126.2 5.4 %collective-permute-start.14 = (bf16[2048,512]{1,0:T(8,128)(2,1)}, bf16[2048,512]{1,0:T(8,128)(2,1)S(1)}, u32[]{:S(2)}, u32[]{:S(2)}) collective-permute-start(bf16[2048,512]{1,0:T(8,128)(2,1)} %bitcast.17), channel_id=1, source_target_pairs={{0,1},{1,0},{2,3},{3,2},{4,5},{5,4},{6,7},{7,6},{8,9},{9,8},{10,11... | collective-permute-start | bytes 6291464 | tf_op jit(solution)/shard_map/ppermute | solution.py:30
  127.6 7.0 %collective-permute-start.15 = (bf16[2048,512]{1,0:T(8,128)(2,1)}, bf16[2048,512]{1,0:T(8,128)(2,1)S(1)}, u32[]{:S(2)}, u32[]{:S(2)}) collective-permute-start(bf16[2048,512]{1,0:T(8,128)(2,1)} %bitcast.19), channel_id=1, source_target_pairs={{0,1},{1,0},{2,3},{3,2},{4,5},{5,4},{6,7},{7,6},{8,9},{9,8},{10,11... | collective-permute-start | bytes 6291464 | tf_op jit(solution)/shard_map/ppermute | solution.py:30
  127.7 10.0 %collective-permute-start.16 = (bf16[512,2048]{1,0:T(8,128)(2,1)}, bf16[512,2048]{1,0:T(8,128)(2,1)}, u32[]{:S(2)}, u32[]{:S(2)}) collective-permute-start(bf16[512,2048]{1,0:T(8,128)(2,1)} %bitcast.21), channel_id=1, source_target_pairs={{0,1},{1,0},{2,3},{3,2},{4,5},{5,4},{6,7},{7,6},{8,9},{9,8},{10,11... | collective-permute-start | bytes 6291464 | tf_op jit(solution)/shard_map/ppermute | solution.py:30
  131.6 3.0 %copy-start.5 = (bf16[2048,512]{1,0:T(8,128)(2,1)}, bf16[2048,512]{1,0:T(8,128)(2,1)S(1)}, u32[]{:S(2)}) copy-start(bf16[2048,512]{1,0:T(8,128)(2,1)S(1)} %collective-permute-done.14.gate_b_hbm) | copy-start | bytes 6291460
  134.6 1.3 copy-start.6
  178.1 52.6 %copy-start.1 = (bf16[256,3072]{1,0:T(8,128)(2,1)S(1)}, bf16[256,3072]{1,0:T(8,128)(2,1)}, u32[]{:S(2)}) copy-start(bf16[256,3072]{1,0:T(8,128)(2,1)} %get-tuple-element.31.table_ref) | copy-start | bytes 4718596
  178.1 52.6 %copy-start.2 = (f32[64,2048]{1,0:T(8,128)S(1)}, f32[64,2048]{1,0:T(8,128)}, u32[]{:S(2)}) copy-start(f32[64,2048]{1,0:T(8,128)} %get-tuple-element.32.residual_ref) | copy-start | bytes 1572868

commit v4 on v2

--- a/solution.py
+++ b/solution.py
@@ -16,7 +16,6 @@
 WIDE = 8
 REST = CAP - WIDE
 GROUP = 16
-PARTS = 4
 
 norm_eps = 1e-05
 head_eps = 1e-06
@@ -144,12 +143,6 @@
     return copy
 
 
-def copied_parts(source, target, sems):
-    size = source.shape[0] // PARTS
-    lines = [pl.ds(i * size, size) for i in range(PARTS)]
-    return [copied(source.at[line], target.at[line], sems.at[i]) for i, line in enumerate(lines)]
-
-
 def wait_all(copies):
     for copy in copies:
         copy.wait()
@@ -161,12 +154,15 @@
     return [((y + away) & 3) * 2 + core for core in (c, 1 - c) for away in (0, 3 - 2 * core, 1 + 2 * core, 2)]
 
 
+def load_kernel(*refs):
+    count = len(refs) // 2
+    copies = [copied(refs[i], refs[count + i], refs[-1].at[i]) for i in range(count)]
+    wait_all(copies)
+
+
 def local_kernel(*refs):
     pieces, refs = refs[:8], refs[8:]
-    wk_hbm, wv_hbm, gain_ref, normed_hbm, k_hbm, v_hbm, state_ref, own_ref, refs = *refs[:8], refs[8:]
-    normed_ref, k_ref, v_ref, wk_ref, wv_ref, gain_rows_ref, in_sem, out_sem = refs
-    k_copies = copied_parts(wk_hbm, wk_ref, in_sem.at[0])
-    v_copies = copied_parts(wv_hbm, wv_ref, in_sem.at[1])
+    wk_ref, wv_ref, wq_ref, gain_ref, q_ref, local_ref, state_ref, own_ref, normed_ref, gain_rows_ref = refs
     gain_rows_ref[...] = gain_ref[...].astype(F32)
     rows, width = pieces[0].shape
     blocks = block_order()
@@ -182,33 +178,21 @@
         gain = jnp.concatenate([gain_rows_ref[pl.ds(2 * block + i, 1), :] for i in range(2)], axis=1)
         normed_ref[:, columns] = (ref[...].astype(F32) * scale * gain).astype(BF)
         own_ref[:, columns] = ref[pl.ds(start, own_rows), :]
-    out_copies = copied_parts(normed_ref, normed_hbm, out_sem.at[0])
-    wait_all(k_copies)
-    k_ref[...] = silu(dot(normed_ref[...], wk_ref[...])).astype(BF)
-    out_copies += copied_parts(k_ref, k_hbm, out_sem.at[1])
-    wait_all(v_copies)
-    v_ref[...] = dot(normed_ref[...], wv_ref[...]).astype(BF)
-    out_copies += copied_parts(v_ref, v_hbm, out_sem.at[2])
-    sequence = lax.broadcasted_iota(jnp.int32, (rows, 128), 0) & 3
-    for h in range(2):
-        cols = slice(h * 128, (h + 1) * 128)
-        keys = k_ref[:, cols].astype(F32)
-        apart = jnp.concatenate([jnp.where(sequence == b, keys, 0.0).astype(BF) for b in range(4)], axis=1)
-        state_ref[h * rows : (h + 1) * rows, :] = dot(apart, v_ref[:, cols], ((0,), (0,))).astype(BF)
-    wait_all(out_copies)
-
-
-def score_kernel(normed_ref, wq_ref, k_ref, v_ref, q_ref, local_ref):
-    rows = normed_ref.shape[0]
+    k = silu(dot(normed_ref[...], wk_ref[...])).astype(BF)
+    v = dot(normed_ref[...], wv_ref[...]).astype(BF)
     q = silu(dot(normed_ref[...], wq_ref[...])).astype(BF)
     q_ref[...] = q
     i0 = lax.broadcasted_iota(jnp.int32, (rows, rows), 0)
     i1 = lax.broadcasted_iota(jnp.int32, (rows, rows), 1)
     seen = (((i0 ^ i1) & 3) == 0) & (i1 <= i0)
+    sequence = lax.broadcasted_iota(jnp.int32, (rows, 128), 0) & 3
     for h in range(2):
         cols = slice(h * 128, (h + 1) * 128)
-        scores = jnp.where(seen, dot(q[:, cols], k_ref[:, cols], ((1,), (1,))), 0.0).astype(BF)
-        local_ref[:, cols] = dot(scores, v_ref[:, cols])
+        keys = k[:, cols].astype(F32)
+        apart = jnp.concatenate([jnp.where(sequence == b, keys, 0.0).astype(BF) for b in range(4)], axis=1)
+        state_ref[h * rows : (h + 1) * rows, :] = dot(apart, v[:, cols], ((0,), (0,))).astype(BF)
+        scores = jnp.where(seen, dot(q[:, cols], k[:, cols], ((1,), (1,))), 0.0).astype(BF)
+        local_ref[:, cols] = dot(scores, v[:, cols])
 
 
 def prefix_kernel(states_ref, before_ref):
@@ -232,17 +216,11 @@
 
 def dispatch_kernel(*refs):
     weights, refs = refs[:8], refs[8:]
-    attended_ref, own_ref, gain_ref, table_hbm, residual_ref, out_ref, refs = *refs[:6], refs[6:]
-    weight_ref, table_ref, weight_sem, table_sem = refs
-    copies = [copied(source, weight_ref.at[i], weight_sem.at[i]) for i, source in enumerate(weights[:7])]
-    table_copies = copied_parts(table_hbm, table_ref, table_sem)
+    attended_ref, own_ref, gain_ref, table_ref, residual_ref, out_ref = refs
     _, width = own_ref.shape
     residual = own_ref[...].astype(F32)
-    for i, block in enumerate(block_order()):
-        if i < 7:
-            copies[i].wait()
-        weight = weight_ref[i] if i < 7 else weights[7][...]
-        residual = residual + dot(attended_ref[block], weight).astype(BF).astype(F32)
+    for ref, block in zip(weights, block_order()):
+        residual = residual + dot(attended_ref[block], ref[...]).astype(BF).astype(F32)
     residual_ref[...] = residual
     mean = jnp.mean(residual * residual, axis=1, keepdims=True)
     gain = gain_ref[...].astype(F32)
@@ -250,20 +228,12 @@
     entering = (residual * lax.rsqrt(mean + norm_eps) * gain).astype(BF)
     step = width // QUART
     stacked = jnp.concatenate([entering[:, q * step : (q + 1) * step] for q in range(QUART)], axis=0)
-    wait_all(table_copies)
     out_ref[...] = dot(table_ref[...], stacked).astype(BF)
 
 
 def expert_kernel(
-    rows_ref, order_ref, back_ref, gate_hbm, up_hbm, down_hbm, gate_b_hbm, up_b_hbm, down_b_hbm, out_ref,
-    x_ref, gate_ref, up_ref, down_ref, weight_sem,
+    rows_ref, order_ref, back_ref, gate_ref, up_ref, down_ref, gate_b_ref, up_b_ref, down_b_ref, out_ref, x_ref
 ):
-    targets = (gate_ref, up_ref, down_ref)
-    given = ((gate_hbm, up_hbm, down_hbm), (gate_b_hbm, up_b_hbm, down_b_hbm))
-    copies = [
-        [copied_parts(source, targets[i].at[half], weight_sem.at[half, i]) for i, source in enumerate(given[half])]
-        for half in range(2)
-    ]
     sources, _, step = rows_ref.shape
     head = sources * WIDE
     part = GROUP * REST
@@ -277,16 +247,12 @@
         for q in range(QUART):
             at = head + g * part
             x_ref[at : at + part, q * step : (q + 1) * step] = rest[q * part : (q + 1) * part]
-    for first, lines in ((True, slice(0, head)), (False, slice(head, sources * CAP))):
+    for lines in (slice(0, head), slice(head, sources * CAP)):
         halves = []
-        for half in range(2):
-            if first:
-                wait_all(copies[half][0] + copies[half][1])
-            gated = dot(x_ref[lines, :], gate_ref[half])
-            active = (silu(gated) * dot(x_ref[lines, :], up_ref[half])).astype(BF)
-            if first:
-                wait_all(copies[half][2])
-            halves.append(dot(active, down_ref[half]).astype(BF))
+        for gate, up, down in ((gate_ref, up_ref, down_ref), (gate_b_ref, up_b_ref, down_b_ref)):
+            gated = dot(x_ref[lines, :], gate[...])
+            active = (silu(gated) * dot(x_ref[lines, :], up[...])).astype(BF)
+            halves.append(dot(active, down[...]).astype(BF))
         x_ref[lines, :] = (halves[0].astype(F32) + halves[1].astype(F32)).astype(BF)
     for q in range(QUART):
         for i in range(sources):
@@ -332,6 +298,13 @@
     attn_rows = attn_gain.reshape(-1, 128)
     head_rows = head_gain.reshape(-1, 128)
     moe_rows = moe_gain.reshape(-1, 128)
+    near_weights = call(
+        load_kernel,
+        [pltpu.VMEM(w.shape, BF) for w in (key_weight, value_weight, query_weight, out_weight)],
+        *[outside(w) for w in (key_weight, value_weight, query_weight, out_weight)],
+        scratch=[pltpu.SemaphoreType.DMA((4,))],
+        mib=4,
+    )
     mine = tokens.reshape(rows, width)
     first = swirled(mine, 1)
     second = swirled(mine, -1)
@@ -343,8 +316,8 @@
     out_first = swirled(later_out, 1)
     out_second = swirled(later_out, -1)
     out_far = swirled(out_first, 1)
-    projections = [out_weight, out_first, out_second, out_far]
-    projections = projections + [shifted(p, "c", 1) for p in projections[:3]]
+    projections = [near_weights[3], out_first, out_second, out_far]
+    projections = projections + [shifted(p, "c", 1) for p in (out_weight, out_first, out_second)]
     projections.append(shifted(out_far, "c", 1))
     gate = expert_gate.reshape(model, hidden)
     up = expert_up.reshape(model, hidden)
@@ -355,61 +328,40 @@
 
     send_table, sum_table = call(
         route_kernel,
-        (pltpu.HBM((COLS, QUART * own_rows), BF), pltpu.HBM((QUART * own_rows, COLS), BF)),
+        (pltpu.VMEM((COLS, QUART * own_rows), BF), pltpu.HBM((QUART * own_rows, COLS), BF)),
         route_ids.transpose(1, 2, 0),
         route_weight.transpose(1, 2, 0),
     )
 
-    normed, k, v, state, own = call(
+    q, local_mix, state, own = call(
         local_kernel,
         (
-            pltpu.HBM((rows, model), BF),
-            pltpu.HBM((rows, width), BF),
-            pltpu.HBM((rows, width), BF),
+            pltpu.VMEM((rows, width), BF),
+            pltpu.VMEM((rows, width), F32),
             pltpu.VMEM((2 * rows, 128), BF),
-            pltpu.HBM((own_rows, model), BF),
+            pltpu.VMEM((own_rows, model), BF),
         ),
         *[inside(p) for p in pieces],
-        outside(key_weight),
-        outside(value_weight),
+        *[inside(w) for w in near_weights[:3]],
         attn_rows,
-        out_specs=[OUTSIDE, OUTSIDE, OUTSIDE, INSIDE, INSIDE],
-        scratch=[
-            pltpu.VMEM((rows, model), BF),
-            pltpu.VMEM((rows, width), BF),
-            pltpu.VMEM((rows, width), BF),
-            pltpu.VMEM((model, width), BF),
-            pltpu.VMEM((model, width), BF),
-            pltpu.VMEM(attn_rows.shape, F32),
-            pltpu.SemaphoreType.DMA((2, PARTS)),
-            pltpu.SemaphoreType.DMA((3, PARTS)),
-        ],
-    )
-    q, local_mix = call(
-        score_kernel, (pltpu.HBM((rows, width), BF), pltpu.HBM((rows, width), F32)), normed, query_weight, k, v
+        scratch=[pltpu.VMEM((rows, model), BF), pltpu.VMEM(attn_rows.shape, F32)],
+        mib=20,
     )
     blocks = lax.axis_size(("x", "z"))
     states = inside(exchanged(state.reshape(blocks, 2 * rows // blocks, 128), ("x", "z")))
-    before = call(prefix_kernel, pltpu.HBM(states.x.shape, BF), states)
+    before = call(prefix_kernel, pltpu.VMEM(states.x.shape, BF), states)
     carried = inside(exchanged(before, ("x", "z")).reshape(2 * rows, 128))
-    attended = call(mix_kernel, pltpu.VMEM((rows, width), BF), q, local_mix, carried, head_rows)
+    attended = call(mix_kernel, pltpu.VMEM((rows, width), BF), inside(q), inside(local_mix), carried, head_rows)
     attended = inside(exchanged(attended.reshape(8, own_rows, width), ("y", "c")))
     step = model // QUART
     residual, sending = call(
         dispatch_kernel,
         (pltpu.HBM((own_rows, model), F32), pltpu.VMEM((COLS, step), BF)),
-        *[outside(p) for p in projections[:7]],
-        inside(projections[7]),
+        *[inside(p) for p in projections],
         attended,
-        own,
+        inside(own),
         moe_rows,
-        outside(send_table),
-        scratch=[
-            pltpu.VMEM((7, width, model), BF),
-            pltpu.VMEM((COLS, QUART * own_rows), BF),
-            pltpu.SemaphoreType.DMA((7,)),
-            pltpu.SemaphoreType.DMA((PARTS,)),
-        ],
+        inside(send_table),
     )
     chips = ("x", "z", "y")
     received = inside(exchanged(sending.reshape(EXPERTS, PACK, step), chips))
@@ -419,15 +371,9 @@
         received,
         either(jnp.asarray(order, BF)),
         either(jnp.asarray(order.T, BF)),
-        *[outside(w) for w in (gate, up, down, other_gate, other_up, other_down)],
-        scratch=[
-            pltpu.VMEM((EXPERTS * CAP, model), BF),
-            pltpu.VMEM((2, model, hidden), BF),
-            pltpu.VMEM((2, model, hidden), BF),
-            pltpu.VMEM((2, hidden, model), BF),
-            pltpu.SemaphoreType.DMA((2, 3, PARTS)),
-        ],
-        mib=36,
+        *[inside(w) for w in (gate, up, down, other_gate, other_up, other_down)],
+        scratch=[pltpu.VMEM((EXPERTS * CAP, model), BF)],
+        mib=20,
     )
     returned = inside(exchanged(results, chips).reshape(COLS, step))
     out = call(combine_kernel, shape((own_rows, model), BF), returned, either(sum_table), either(residual))

time: 233 us -> 242 us (1.039)
  local copies, waits for them, and re-layouts: 4.79 us -> 19.2 us
  blocking collectives: 68.2 us -> 79.3 us
  Pallas kernels: 39.3 us -> 30.6 us
  starting transfers between devices: 37.7 us -> 33.3 us
  waiting for transfers between devices: 80.8 us -> 76.5 us
    unnamed x18 -> x32, local copies, waits for them, and re-layouts: 2.97 us -> 17.4 us
    all_to_all x2 -> x3, blocking collectives: 68.2 us -> 79.3 us  [exchanged(): return lax.all_to_all(x, axes, split_axis=0, concat_axis=0, tiled=True)]
    pallas_call x8, Pallas kernels: 39.3 us -> 30.6 us  [call(): pl.pallas_call(kernel, out_shape=out_shape, in_specs=[x.spec for x in arg...]
    all_to_all x3 -> x2, starting transfers between devices: 15 us -> 10.9 us  [exchanged(): return lax.all_to_all(x, axes, split_axis=0, concat_axis=0, tiled=True)]
    all_to_all x3 -> x2, waiting for transfers between devices: 31.1 us -> 28 us  [exchanged(): return lax.all_to_all(x, axes, split_axis=0, concat_axis=0, tiled=True)]
  transfers between devices with their start and end apart: 20 -> 19, of which waited for: 11 -> 10; matrix products, arithmetic and copies ran while one was open for 0% -> 0% of each run, Pallas kernels for 8% -> 6%
where the time goes in v4:
time: 242 us; the launch traced here: 239 us
  blocking collectives  79.3 us (33%)
  waiting for transfers between devices  76.5 us (32%)
  starting transfers between devices  33.3 us (14%)
  Pallas kernels  30.6 us (13%)
  local copies, waits for them, and re-layouts  19.2 us (8%)
    all_to_all x3, blocking collectives, exchanged(): return lax.all_to_all(x, axes, split_axis=0, concat_axis=0, tiled=True)  79.3 us
    ppermute x6, waiting for transfers between devices, swirled(): return lax.ppermute(x, ('y', 'c'), pairs)  40.5 us
    pallas_call x8, Pallas kernels, call(): pl.pallas_call(kernel, out_shape=out_shape, in_specs=[x.spec for x in arg...  30.6 us
    all_to_all x2, waiting for transfers between devices, exchanged(): return lax.all_to_all(x, axes, split_axis=0, concat_axis=0, tiled=True)  28 us
    unnamed x32, local copies, waits for them, and re-layouts  17.4 us
    ppermute x11, starting transfers between devices, shifted(): return lax.ppermute(x, axis, [(i, (i + by) % count) for i in range(count)])  12.1 us
    all_to_all x2, starting transfers between devices, exchanged(): return lax.all_to_all(x, axes, split_axis=0, concat_axis=0, tiled=True)  10.9 us
    ppermute x6, starting transfers between devices, swirled(): return lax.ppermute(x, ('y', 'c'), pairs)  10.4 us
  transfers between devices with their start and end apart: 19, of which 10 were waited for; matrix products, arithmetic and copies ran while one was open for 0% of the time, Pallas kernels for 6%

profile of v4, /device:TPU:1, one launch (start us, length us, event | category | flops | bytes accessed | tf_op | source)
XLA Modules:
  0.0 239.0 jit_solution(4843298319545785478)
XLA Ops:
  0.0 1.0 reshape.39.refs_0_
  1.0 3.6 %collective-permute-start.1 = (bf16[512,256]{1,0:T(8,128)(2,1)S(1)}, bf16[512,256]{1,0:T(8,128)(2,1)S(1)}, u32[]{:S(2)}, u32[]{:S(2)}) collective-permute-start(bf16[512,256]{1,0:T(8,128)(2,1)S(1)} %reshape.39.refs_0_), channel_id=1, source_target_pairs={{0,2},{1,7},{2,4},{3,1},{4,6},{5,3},{6,0},{7,5},{8,10},{9,15},{10,... | collective-permute-start | bytes 786440 | tf_op jit(solution)/shard_map/ppermute | solution.py:35
  4.6 4.9 %collective-permute-done.1.refs_1_ = bf16[512,256]{1,0:T(8,128)(2,1)S(1)} collective-permute-done((bf16[512,256]{1,0:T(8,128)(2,1)S(1)}, bf16[512,256]{1,0:T(8,128)(2,1)S(1)}, u32[]{:S(2)}, u32[]{:S(2)}) %collective-permute-start.1) | collective-permute-done | bytes 262176 | tf_op jit(solution)/shard_map/ppermute | solution.py:35
  9.5 3.4 %collective-permute-start.5 = (bf16[512,256]{1,0:T(8,128)(2,1)S(1)}, bf16[512,256]{1,0:T(8,128)(2,1)S(1)}, u32[]{:S(2)}, u32[]{:S(2)}) collective-permute-start(bf16[512,256]{1,0:T(8,128)(2,1)S(1)} %collective-permute-done.1.refs_1_), channel_id=1, source_target_pairs={{0,2},{1,7},{2,4},{3,1},{4,6},{5,3},{6,0},{7,5},{8,10},{9,15},{10,... | collective-permute-start | bytes 786440 | tf_op jit(solution)/shard_map/ppermute | solution.py:35
  13.0 0.4 collective-permute-start.2
  13.4 0.1 collective-permute-start.4
  13.5 2.7 %collective-permute-done.5.refs_3_ = bf16[512,256]{1,0:T(8,128)(2,1)S(1)} collective-permute-done((bf16[512,256]{1,0:T(8,128)(2,1)S(1)}, bf16[512,256]{1,0:T(8,128)(2,1)S(1)}, u32[]{:S(2)}, u32[]{:S(2)}) %collective-permute-start.5) | collective-permute-done | bytes 262176 | tf_op jit(solution)/shard_map/ppermute | solution.py:35
  16.2 2.5 %collective-permute-start.6 = (bf16[512,256]{1,0:T(8,128)(2,1)S(1)}, bf16[512,256]{1,0:T(8,128)(2,1)S(1)}, u32[]{:S(2)}, u32[]{:S(2)}) collective-permute-start(bf16[512,256]{1,0:T(8,128)(2,1)S(1)} %collective-permute-done.5.refs_3_), channel_id=1, source_target_pairs={{0,1},{1,0},{2,3},{3,2},{4,5},{5,4},{6,7},{7,6},{8,9},{9,8},{10,11... | collective-permute-start | bytes 786440 | tf_op jit(solution)/shard_map/ppermute | solution.py:29
  18.7 1.1 collective-permute-done.6.refs_7_
  19.9 1.5 collective-permute-start.7
  21.4 22.5 %collective-permute-done.7.refs_1_ = bf16[256,2048]{1,0:T(8,128)(2,1)S(1)} collective-permute-done((bf16[256,2048]{1,0:T(8,128)(2,1)}, bf16[256,2048]{1,0:T(8,128)(2,1)S(1)}, u32[]{:S(2)}, u32[]{:S(2)}) %collective-permute-start.7) | collective-permute-done | bytes 1048608 | tf_op jit(solution)/shard_map/ppermute | solution.py:35
  43.9 1.9 collective-permute-start.9
  45.7 1.4 collective-permute-start.10
  47.1 0.5 collective-permute-start.12
  47.6 10.3 %collective-permute-done.9.refs_3_ = bf16[256,2048]{1,0:T(8,128)(2,1)} collective-permute-done((bf16[256,2048]{1,0:T(8,128)(2,1)S(1)}, bf16[256,2048]{1,0:T(8,128)(2,1)}, u32[]{:S(2)}, u32[]{:S(2)}) %collective-permute-start.9) | collective-permute-done | bytes 1048608 | tf_op jit(solution)/shard_map/ppermute | solution.py:35
  57.9 5.3 %collective-permute-start.13 = (bf16[256,2048]{1,0:T(8,128)(2,1)}, bf16[256,2048]{1,0:T(8,128)(2,1)}, u32[]{:S(2)}, u32[]{:S(2)}) collective-permute-start(bf16[256,2048]{1,0:T(8,128)(2,1)} %collective-permute-done.9.refs_3_), channel_id=1, source_target_pairs={{0,1},{1,0},{2,3},{3,2},{4,5},{5,4},{6,7},{7,6},{8,9},{9,8},{10,11... | collective-permute-start | bytes 3145736 | tf_op jit(solution)/shard_map/ppermute | solution.py:29
  63.2 2.2 shard_map.145
  65.4 1.0 copy-done.11
  66.4 5.4 %shard_map.146 = (bf16[512,256]{1,0:T(8,128)(2,1)S(1)}, f32[512,256]{1,0:T(8,128)S(1)}, bf16[1024,128]{1,0:T(8,128)(2,1)S(1)}, bf16[64,2048]{1,0:T(8,128)(2,1)S(1)}) custom-call(bf16[512,256]{1,0:T(8,128)(2,1)S(1)} %reshape.39.refs_0_, bf16[512,256]{1,0:T(8,128)(2,1)S(1)} %collective-permute-done.1.refs_1_, ...), custom_call_target="tpu_custom_call" | custom-call | tf_op jit(solution)/shard_map/pallas_call | solution.py:80
  71.8 15.6 %all_to_all.25.states_ref = bf16[16,64,128]{2,1,0:T(8,128)(2,1)S(1)} all-to-all(bf16[16,64,128]{2,1,0:T(8,128)(2,1)S(1)} %bitcast.22), channel_id=1, replica_groups=mesh['x'=4,'z'=4,'y'=4,'c'=2] {'x','z'}, dimensions={0} | all-to-all | bytes 524288 | tf_op jit(solution)/shard_map/all_to_all | solution.py:39
  87.5 11.0 %all_to_all.26 = bf16[16,64,128]{2,1,0:T(8,128)(2,1)S(1)} all-to-all(bf16[16,64,128]{2,1,0:T(8,128)(2,1)S(1)} %shard_map.147), channel_id=1, replica_groups=mesh['x'=4,'z'=4,'y'=4,'c'=2] {'x','z'}, dimensions={0} | all-to-all | bytes 524288 | tf_op jit(solution)/shard_map/all_to_all | solution.py:39
  98.5 1.9 shard_map.148
  100.4 5.9 %all-to-all-start.2 = ((bf16[8,64,256]{2,1,0:T(8,128)(2,1)}), bf16[8,64,256]{2,1,0:T(8,128)(2,1)S(1)}, u32[]{:S(2)}, u32[]{:S(2)}) async-start(bf16[8,64,256]{2,1,0:T(8,128)(2,1)} %bitcast.4), calls=%async_computation.2 | async-start | bytes 524288 | tf_op jit(solution)/shard_map/all_to_all | solution.py:39
  106.3 3.7 %shard_map.149 = (bf16[3072,256]{1,0:T(8,128)(2,1)S(1)}, bf16[256,3072]{1,0:T(8,128)(2,1)}) custom-call(s32[4,8,16]{2,1,0:T(8,128)} %bitcast.23, f32[4,8,16]{2,1,0:T(8,128)} %bitcast.24), custom_call_target="tpu_custom_call" | custom-call | tf_op jit(solution)/shard_map/pallas_call | solution.py:80
  110.0 2.8 %all-to-all-done.2.refs_8_ = bf16[8,64,256]{2,1,0:T(8,128)(2,1)S(1)} async-done(((bf16[8,64,256]{2,1,0:T(8,128)(2,1)}), bf16[8,64,256]{2,1,0:T(8,128)(2,1)S(1)}, u32[]{:S(2)}, u32[]{:S(2)}) %all-to-all-start.2) | async-done | bytes 262176 | tf_op jit(solution)/shard_map/all_to_all | solution.py:39
  112.8 1.2 copy-done.12
  114.0 5.5 %shard_map.150 = (f32[64,2048]{1,0:T(8,128)}, bf16[3072,512]{1,0:T(8,128)(2,1)S(1)}) custom-call(bf16[256,2048]{1,0:T(8,128)(2,1)S(1)} %copy-done.12, bf16[256,2048]{1,0:T(8,128)(2,1)S(1)} %collective-permute-done.7.refs_1_, bf16[256,2048]{1,0:T(8,128)(2,1)} %collective-permute-done.8.refs_2_, bf16[256,2048]{1,0:T(8,128)(2,1)} %collective-permute-done.9.refs_3_, ...), custom_call_target="tpu_custom_call" | custom-call | tf_op jit(solution)/shard_map/pallas_call | solution.py:80
  119.5 1.6 copy-done
  121.1 5.0 %all-to-all-start.3 = ((bf16[64,48,512]{2,1,0:T(8,128)(2,1)}), bf16[64,48,512]{2,1,0:T(8,128)(2,1)S(1)}, u32[]{:S(2)}, u32[]{:S(2)}) async-start(bf16[64,48,512]{2,1,0:T(8,128)(2,1)} %bitcast.14), calls=%async_computation.3 | async-start | bytes 6291456 | tf_op jit(solution)/shard_map/all_to_all | solution.py:39
  126.1 1.4 collective-permute-start.14
  127.6 0.4 collective-permute-start.16
  128.0 3.5 %collective-permute-done.14.gate_b_ref = bf16[2048,512]{1,0:T(8,128)(2,1)S(1)} collective-permute-done((bf16[2048,512]{1,0:T(8,128)(2,1)}, bf16[2048,512]{1,0:T(8,128)(2,1)S(1)}, u32[]{:S(2)}, u32[]{:S(2)}) %collective-permute-start.14) | collective-permute-done | bytes 2097184 | tf_op jit(solution)/shard_map/ppermute | solution.py:29
  131.5 1.3 copy-done.4
  132.8 1.7 collective-permute-done.15.up_b_ref
  134.5 1.3 copy-done.6
  135.8 1.7 collective-permute-done.16.down_b_ref
  137.5 1.4 copy-done.8
  138.9 25.2 %all-to-all-done.3.rows_ref = bf16[64,48,512]{2,1,0:T(8,128)(2,1)S(1)} async-done(((bf16[64,48,512]{2,1,0:T(8,128)(2,1)}), bf16[64,48,512]{2,1,0:T(8,128)(2,1)S(1)}, u32[]{:S(2)}, u32[]{:S(2)}) %all-to-all-start.3) | async-done | bytes 3145760 | tf_op jit(solution)/shard_map/all_to_all | solution.py:39
  164.1 1.6 copy-done.1
  165.7 1.6 copy-done.2
  167.3 1.6 copy-done.3
  168.9 1.6 copy-done.5
  170.5 1.6 copy-done.7
  172.1 1.6 copy-done.9
  173.7 10.9 %shard_map.151 = bf16[64,48,512]{2,1,0:T(8,128)(2,1)S(1)} custom-call(bf16[64,48,512]{2,1,0:T(8,128)(2,1)S(1)} %all-to-all-done.3.rows_ref, bf16[256,256]{1,0:T(8,128)(2,1)S(1)} %copy-done.14, bf16[256,256]{1,0:T(8,128)(2,1)S(1)} %copy-done.15, bf16[2048,512]{1,0:T(8,128)(2,1)S(1)} %bitcast.16, bf16[2048,512]{1,0:T(8,128)(2,1)S(1)} %bitcast.18, ...), custom_call_target="tpu_custom_call" | custom-call | tf_op jit(solution)/shard_map/pallas_call | solution.py:80
  184.6 52.6 %all_to_all.27 = bf16[64,48,512]{2,1,0:T(8,128)(2,1)S(1)} all-to-all(bf16[64,48,512]{2,1,0:T(8,128)(2,1)S(1)} %shard_map.151), channel_id=1, replica_groups=mesh['x'=4,'z'=4,'y'=4,'c'=2] {'x','z','y'}, dimensions={0} | all-to-all | bytes 6291456 | tf_op jit(solution)/shard_map/all_to_all | solution.py:39
  237.2 1.0 shard_map.152
  238.2 0.8 reshape.51
  (35 shorter events, 0.4 us)
Async XLA Ops:
  1.0 8.5 %collective-permute-start.1 = (bf16[512,256]{1,0:T(8,128)(2,1)S(1)}, bf16[512,256]{1,0:T(8,128)(2,1)S(1)}, u32[]{:S(2)}, u32[]{:S(2)}) collective-permute-start(bf16[512,256]{1,0:T(8,128)(2,1)S(1)} %reshape.39.refs_0_), channel_id=1, source_target_pairs={{0,2},{1,7},{2,4},{3,1},{4,6},{5,3},{6,0},{7,5},{8,10},{9,15},{10,... | collective-permute-start | bytes 786440 | tf_op jit(solution)/shard_map/ppermute | solution.py:35
  4.6 8.8 %collective-permute-start.3 = (bf16[512,256]{1,0:T(8,128)(2,1)S(1)}, bf16[512,256]{1,0:T(8,128)(2,1)S(1)}, u32[]{:S(2)}, u32[]{:S(2)}) collective-permute-start(bf16[512,256]{1,0:T(8,128)(2,1)S(1)} %reshape.39.refs_0_), channel_id=1, source_target_pairs={{0,6},{1,3},{2,0},{3,5},{4,2},{5,7},{6,4},{7,1},{8,14},{9,11},{10,... | collective-permute-start | bytes 786440 | tf_op jit(solution)/shard_map/ppermute | solution.py:35
  9.5 6.7 %collective-permute-start.5 = (bf16[512,256]{1,0:T(8,128)(2,1)S(1)}, bf16[512,256]{1,0:T(8,128)(2,1)S(1)}, u32[]{:S(2)}, u32[]{:S(2)}) collective-permute-start(bf16[512,256]{1,0:T(8,128)(2,1)S(1)} %collective-permute-done.1.refs_1_), channel_id=1, source_target_pairs={{0,2},{1,7},{2,4},{3,1},{4,6},{5,3},{6,0},{7,5},{8,10},{9,15},{10,... | collective-permute-start | bytes 786440 | tf_op jit(solution)/shard_map/ppermute | solution.py:35
  12.9 5.8 %collective-permute-start = (bf16[512,256]{1,0:T(8,128)(2,1)S(1)}, bf16[512,256]{1,0:T(8,128)(2,1)S(1)}, u32[]{:S(2)}, u32[]{:S(2)}) collective-permute-start(bf16[512,256]{1,0:T(8,128)(2,1)S(1)} %reshape.39.refs_0_), channel_id=1, source_target_pairs={{0,1},{1,0},{2,3},{3,2},{4,5},{5,4},{6,7},{7,6},{8,9},{9,8},{10,11... | collective-permute-start | bytes 786440 | tf_op jit(solution)/shard_map/ppermute | solution.py:29
  13.0 5.7 %collective-permute-start.2 = (bf16[512,256]{1,0:T(8,128)(2,1)S(1)}, bf16[512,256]{1,0:T(8,128)(2,1)S(1)}, u32[]{:S(2)}, u32[]{:S(2)}) collective-permute-start(bf16[512,256]{1,0:T(8,128)(2,1)S(1)} %collective-permute-done.1.refs_1_), channel_id=1, source_target_pairs={{0,1},{1,0},{2,3},{3,2},{4,5},{5,4},{6,7},{7,6},{8,9},{9,8},{10,11... | collective-permute-start | bytes 786440 | tf_op jit(solution)/shard_map/ppermute | solution.py:29
  13.4 5.3 %collective-permute-start.4 = (bf16[512,256]{1,0:T(8,128)(2,1)S(1)}, bf16[512,256]{1,0:T(8,128)(2,1)S(1)}, u32[]{:S(2)}, u32[]{:S(2)}) collective-permute-start(bf16[512,256]{1,0:T(8,128)(2,1)S(1)} %collective-permute-done.3.refs_2_), channel_id=1, source_target_pairs={{0,1},{1,0},{2,3},{3,2},{4,5},{5,4},{6,7},{7,6},{8,9},{9,8},{10,11... | collective-permute-start | bytes 786440 | tf_op jit(solution)/shard_map/ppermute | solution.py:29
  16.2 3.7 %collective-permute-start.6 = (bf16[512,256]{1,0:T(8,128)(2,1)S(1)}, bf16[512,256]{1,0:T(8,128)(2,1)S(1)}, u32[]{:S(2)}, u32[]{:S(2)}) collective-permute-start(bf16[512,256]{1,0:T(8,128)(2,1)S(1)} %collective-permute-done.5.refs_3_), channel_id=1, source_target_pairs={{0,1},{1,0},{2,3},{3,2},{4,5},{5,4},{6,7},{7,6},{8,9},{9,8},{10,11... | collective-permute-start | bytes 786440 | tf_op jit(solution)/shard_map/ppermute | solution.py:29
  19.9 24.0 %collective-permute-start.7 = (bf16[256,2048]{1,0:T(8,128)(2,1)}, bf16[256,2048]{1,0:T(8,128)(2,1)S(1)}, u32[]{:S(2)}, u32[]{:S(2)}) collective-permute-start(bf16[256,2048]{1,0:T(8,128)(2,1)} %refs_3_.1), channel_id=1, source_target_pairs={{0,2},{1,7},{2,4},{3,1},{4,6},{5,3},{6,0},{7,5},{8,10},{9,15},{10,... | collective-permute-start | bytes 3145736 | tf_op jit(solution)/shard_map/ppermute | solution.py:35
  21.4 25.8 %collective-permute-start.8 = (bf16[256,2048]{1,0:T(8,128)(2,1)}, bf16[256,2048]{1,0:T(8,128)(2,1)}, u32[]{:S(2)}, u32[]{:S(2)}) collective-permute-start(bf16[256,2048]{1,0:T(8,128)(2,1)} %refs_3_.1), channel_id=1, source_target_pairs={{0,6},{1,3},{2,0},{3,5},{4,2},{5,7},{6,4},{7,1},{8,14},{9,11},{10,... | collective-permute-start | bytes 3145736 | tf_op jit(solution)/shard_map/ppermute | solution.py:35
  43.9 14.0 %collective-permute-start.9 = (bf16[256,2048]{1,0:T(8,128)(2,1)S(1)}, bf16[256,2048]{1,0:T(8,128)(2,1)}, u32[]{:S(2)}, u32[]{:S(2)}) collective-permute-start(bf16[256,2048]{1,0:T(8,128)(2,1)S(1)} %collective-permute-done.7.refs_1_), channel_id=1, source_target_pairs={{0,2},{1,7},{2,4},{3,1},{4,6},{5,3},{6,0},{7,5},{8,10},{9,15},{10,... | collective-permute-start | bytes 3145736 | tf_op jit(solution)/shard_map/ppermute | solution.py:35
  45.7 64.3 %collective-permute-start.10 = (bf16[256,2048]{1,0:T(8,128)(2,1)}, bf16[256,2048]{1,0:T(8,128)(2,1)}, u32[]{:S(2)}, u32[]{:S(2)}) collective-permute-start(bf16[256,2048]{1,0:T(8,128)(2,1)} %refs_3_.1), channel_id=1, source_target_pairs={{0,1},{1,0},{2,3},{3,2},{4,5},{5,4},{6,7},{7,6},{8,9},{9,8},{10,11... | collective-permute-start | bytes 3145736 | tf_op jit(solution)/shard_map/ppermute | solution.py:29
  47.1 65.7 %collective-permute-start.11 = (bf16[256,2048]{1,0:T(8,128)(2,1)S(1)}, bf16[256,2048]{1,0:T(8,128)(2,1)}, u32[]{:S(2)}, u32[]{:S(2)}) collective-permute-start(bf16[256,2048]{1,0:T(8,128)(2,1)S(1)} %collective-permute-done.7.refs_1_), channel_id=1, source_target_pairs={{0,1},{1,0},{2,3},{3,2},{4,5},{5,4},{6,7},{7,6},{8,9},{9,8},{10,11... | collective-permute-start | bytes 3145736 | tf_op jit(solution)/shard_map/ppermute | solution.py:29
  47.1 65.7 %collective-permute-start.12 = (bf16[256,2048]{1,0:T(8,128)(2,1)}, bf16[256,2048]{1,0:T(8,128)(2,1)}, u32[]{:S(2)}, u32[]{:S(2)}) collective-permute-start(bf16[256,2048]{1,0:T(8,128)(2,1)} %collective-permute-done.8.refs_2_), channel_id=1, source_target_pairs={{0,1},{1,0},{2,3},{3,2},{4,5},{5,4},{6,7},{7,6},{8,9},{9,8},{10,11... | collective-permute-start | bytes 3145736 | tf_op jit(solution)/shard_map/ppermute | solution.py:29
  57.9 54.9 %collective-permute-start.13 = (bf16[256,2048]{1,0:T(8,128)(2,1)}, bf16[256,2048]{1,0:T(8,128)(2,1)}, u32[]{:S(2)}, u32[]{:S(2)}) collective-permute-start(bf16[256,2048]{1,0:T(8,128)(2,1)} %collective-permute-done.9.refs_3_), channel_id=1, source_target_pairs={{0,1},{1,0},{2,3},{3,2},{4,5},{5,4},{6,7},{7,6},{8,9},{9,8},{10,11... | collective-permute-start | bytes 3145736 | tf_op jit(solution)/shard_map/ppermute | solution.py:29
  65.4 1.0 copy-start.11
  100.4 12.4 %all-to-all-start.2 = ((bf16[8,64,256]{2,1,0:T(8,128)(2,1)}), bf16[8,64,256]{2,1,0:T(8,128)(2,1)S(1)}, u32[]{:S(2)}, u32[]{:S(2)}) async-start(bf16[8,64,256]{2,1,0:T(8,128)(2,1)} %bitcast.4), calls=%async_computation.2 | async-start | bytes 524288 | tf_op jit(solution)/shard_map/all_to_all | solution.py:39
  112.8 1.2 copy-start.12
  119.5 1.6 copy-start
  121.1 43.0 %copy-start.14 = (bf16[256,256]{1,0:T(8,128)(2,1)S(1)}, bf16[256,256]{1,0:T(8,128)(2,1)}, u32[]{:S(2)}) copy-start(bf16[256,256]{1,0:T(8,128)(2,1)} %constant.4.clone.order_ref) | copy-start | bytes 393220
  121.1 43.0 %copy-start.15 = (bf16[256,256]{1,0:T(8,128)(2,1)S(1)}, bf16[256,256]{1,0:T(8,128)(2,1)}, u32[]{:S(2)}) copy-start(bf16[256,256]{1,0:T(8,128)(2,1)} %constant.5.clone.back_ref) | copy-start | bytes 393220
  121.1 43.0 %all-to-all-start.3 = ((bf16[64,48,512]{2,1,0:T(8,128)(2,1)}), bf16[64,48,512]{2,1,0:T(8,128)(2,1)S(1)}, u32[]{:S(2)}, u32[]{:S(2)}) async-start(bf16[64,48,512]{2,1,0:T(8,128)(2,1)} %bitcast.14), calls=%async_computation.3 | async-start | bytes 6291456 | tf_op jit(solution)/shard_map/all_to_all | solution.py:39
  126.1 5.4 %collective-permute-start.14 = (bf16[2048,512]{1,0:T(8,128)(2,1)}, bf16[2048,512]{1,0:T(8,128)(2,1)S(1)}, u32[]{:S(2)}, u32[]{:S(2)}) collective-permute-start(bf16[2048,512]{1,0:T(8,128)(2,1)} %bitcast.15), channel_id=1, source_target_pairs={{0,1},{1,0},{2,3},{3,2},{4,5},{5,4},{6,7},{7,6},{8,9},{9,8},{10,11... | collective-permute-start | bytes 6291464 | tf_op jit(solution)/shard_map/ppermute | solution.py:29
  127.5 7.0 %collective-permute-start.15 = (bf16[2048,512]{1,0:T(8,128)(2,1)}, bf16[2048,512]{1,0:T(8,128)(2,1)S(1)}, u32[]{:S(2)}, u32[]{:S(2)}) collective-permute-start(bf16[2048,512]{1,0:T(8,128)(2,1)} %bitcast.17), channel_id=1, source_target_pairs={{0,1},{1,0},{2,3},{3,2},{4,5},{5,4},{6,7},{7,6},{8,9},{9,8},{10,11... | collective-permute-start | bytes 6291464 | tf_op jit(solution)/shard_map/ppermute | solution.py:29
  127.6 9.9 %collective-permute-start.16 = (bf16[512,2048]{1,0:T(8,128)(2,1)}, bf16[512,2048]{1,0:T(8,128)(2,1)S(1)}, u32[]{:S(2)}, u32[]{:S(2)}) collective-permute-start(bf16[512,2048]{1,0:T(8,128)(2,1)} %bitcast.19), channel_id=1, source_target_pairs={{0,1},{1,0},{2,3},{3,2},{4,5},{5,4},{6,7},{7,6},{8,9},{9,8},{10,11... | collective-permute-start | bytes 6291464 | tf_op jit(solution)/shard_map/ppermute | solution.py:29
  131.5 1.3 copy-start.4
  134.5 1.3 copy-start.6
  137.5 1.4 copy-start.8
  164.1 1.6 copy-start.1
  165.7 1.6 copy-start.2
  167.3 1.6 copy-start.3
  168.9 1.6 copy-start.5
  170.5 1.6 copy-start.7
  172.1 1.6 copy-start.9
  184.6 52.6 %copy-start.10 = (bf16[256,3072]{1,0:T(8,128)(2,1)S(1)}, bf16[256,3072]{1,0:T(8,128)(2,1)}, u32[]{:S(2)}) copy-start(bf16[256,3072]{1,0:T(8,128)(2,1)} %get-tuple-element.37.table_ref) | copy-start | bytes 4718596
  184.6 52.6 %copy-start.13 = (f32[64,2048]{1,0:T(8,128)S(1)}, f32[64,2048]{1,0:T(8,128)}, u32[]{:S(2)}) copy-start(f32[64,2048]{1,0:T(8,128)} %get-tuple-element.38.residual_ref) | copy-start | bytes 1572868

commit v5 on v4

--- a/solution.py
+++ b/solution.py
@@ -310,11 +310,11 @@
     second = swirled(mine, -1)
     far = swirled(first, 1)
     pieces = [mine, first, second, far]
-    pieces = pieces + [shifted(p, "c", 1) for p in pieces]
-
-    later_out, *pieces[4:] = lax.optimization_barrier((out_weight, *pieces[4:]))
-    out_first = swirled(later_out, 1)
-    out_second = swirled(later_out, -1)
+    pieces = pieces + [shifted(mine, "c", 1)]
+    pieces = pieces + [shifted(p, "c", 1) for p in (first, second, far)]
+
+    out_first = swirled(out_weight, 1)
+    out_second = swirled(out_weight, -1)
     out_far = swirled(out_first, 1)
     projections = [near_weights[3], out_first, out_second, out_far]
     projections = projections + [shifted(p, "c", 1) for p in (out_weight, out_first, out_second)]

time: 242 us -> 239 us (0.988)
    ppermute x11, starting transfers between devices: 12.1 us -> 8.71 us  [shifted(): return lax.ppermute(x, axis, [(i, (i + by) % count) for i in range(count)])]
    ppermute x6, waiting for transfers between devices: 40.5 us -> 37.9 us  [swirled(): return lax.ppermute(x, ('y', 'c'), pairs)]
  transfers between devices with their start and end apart: 19 -> 19, of which waited for: 10 -> 9; matrix products, arithmetic and copies ran while one was open for 0% -> 0% of each run, Pallas kernels for 6% -> 6%
where the time goes in v5:
time: 239 us; the launch traced here: 236 us
  blocking collectives  78.6 us (33%)
  waiting for transfers between devices  75.9 us (32%)
  starting transfers between devices  31.6 us (13%)
  Pallas kernels  30.6 us (13%)
  local copies, waits for them, and re-layouts  19.2 us (8%)
    all_to_all x3, blocking collectives, exchanged(): return lax.all_to_all(x, axes, split_axis=0, concat_axis=0, tiled=True)  78.6 us
    ppermute x6, waiting for transfers between devices, swirled(): return lax.ppermute(x, ('y', 'c'), pairs)  37.9 us
    pallas_call x8, Pallas kernels, call(): pl.pallas_call(kernel, out_shape=out_shape, in_specs=[x.spec for x in arg...  30.6 us
    all_to_all x2, waiting for transfers between devices, exchanged(): return lax.all_to_all(x, axes, split_axis=0, concat_axis=0, tiled=True)  28 us
    unnamed x32, local copies, waits for them, and re-layouts  17.4 us
    ppermute x6, starting transfers between devices, swirled(): return lax.ppermute(x, ('y', 'c'), pairs)  11.6 us
    all_to_all x2, starting transfers between devices, exchanged(): return lax.all_to_all(x, axes, split_axis=0, concat_axis=0, tiled=True)  11.3 us
    ppermute x11, waiting for transfers between devices, shifted(): return lax.ppermute(x, axis, [(i, (i + by) % count) for i in range(count)])  10 us
  transfers between devices with their start and end apart: 19, of which 9 were waited for; matrix products, arithmetic and copies ran while one was open for 0% of the time, Pallas kernels for 6%

profile of v5, /device:TPU:1, one launch (start us, length us, event | category | flops | bytes accessed | tf_op | source)
XLA Modules:
  0.0 236.1 jit_solution(8122993370379768708)
XLA Ops:
  0.0 3.6 %collective-permute-start = (bf16[256,2048]{1,0:T(8,128)(2,1)}, bf16[256,2048]{1,0:T(8,128)(2,1)S(1)}, u32[]{:S(2)}, u32[]{:S(2)}) collective-permute-start(bf16[256,2048]{1,0:T(8,128)(2,1)} %refs_3_.1), channel_id=1, source_target_pairs={{0,2},{1,7},{2,4},{3,1},{4,6},{5,3},{6,0},{7,5},{8,10},{9,15},{10,... | collective-permute-start | bytes 3145736 | tf_op jit(solution)/shard_map/ppermute | solution.py:35
  3.6 22.0 %collective-permute-done.refs_1_ = bf16[256,2048]{1,0:T(8,128)(2,1)S(1)} collective-permute-done((bf16[256,2048]{1,0:T(8,128)(2,1)}, bf16[256,2048]{1,0:T(8,128)(2,1)S(1)}, u32[]{:S(2)}, u32[]{:S(2)}) %collective-permute-start) | collective-permute-done | bytes 1048608 | tf_op jit(solution)/shard_map/ppermute | solution.py:35
  25.6 3.4 %collective-permute-start.2 = (bf16[256,2048]{1,0:T(8,128)(2,1)S(1)}, bf16[256,2048]{1,0:T(8,128)(2,1)}, u32[]{:S(2)}, u32[]{:S(2)}) collective-permute-start(bf16[256,2048]{1,0:T(8,128)(2,1)S(1)} %collective-permute-done.refs_1_), channel_id=1, source_target_pairs={{0,2},{1,7},{2,4},{3,1},{4,6},{5,3},{6,0},{7,5},{8,10},{9,15},{10,... | collective-permute-start | bytes 3145736 | tf_op jit(solution)/shard_map/ppermute | solution.py:35
  29.0 1.0 reshape.39.refs_0_
  30.1 1.5 collective-permute-start.8
  31.6 1.7 collective-permute-start.10
  33.3 13.1 %collective-permute-done.7.refs_1_ = bf16[512,256]{1,0:T(8,128)(2,1)S(1)} collective-permute-done((bf16[512,256]{1,0:T(8,128)(2,1)S(1)}, bf16[512,256]{1,0:T(8,128)(2,1)S(1)}, u32[]{:S(2)}, u32[]{:S(2)}) %collective-permute-start.7) | collective-permute-done | bytes 262176 | tf_op jit(solution)/shard_map/ppermute | solution.py:35
  46.4 3.1 %collective-permute-start.9 = (bf16[512,256]{1,0:T(8,128)(2,1)S(1)}, bf16[512,256]{1,0:T(8,128)(2,1)S(1)}, u32[]{:S(2)}, u32[]{:S(2)}) collective-permute-start(bf16[512,256]{1,0:T(8,128)(2,1)S(1)} %collective-permute-done.7.refs_1_), channel_id=1, source_target_pairs={{0,2},{1,7},{2,4},{3,1},{4,6},{5,3},{6,0},{7,5},{8,10},{9,15},{10,... | collective-permute-start | bytes 786440 | tf_op jit(solution)/shard_map/ppermute | solution.py:35
  49.5 0.5 collective-permute-start.12
  50.0 2.8 %collective-permute-done.9.refs_3_ = bf16[512,256]{1,0:T(8,128)(2,1)S(1)} collective-permute-done((bf16[512,256]{1,0:T(8,128)(2,1)S(1)}, bf16[512,256]{1,0:T(8,128)(2,1)S(1)}, u32[]{:S(2)}, u32[]{:S(2)}) %collective-permute-start.9) | collective-permute-done | bytes 262176 | tf_op jit(solution)/shard_map/ppermute | solution.py:35
  52.8 3.5 %collective-permute-start.3 = (bf16[256,2048]{1,0:T(8,128)(2,1)}, bf16[256,2048]{1,0:T(8,128)(2,1)}, u32[]{:S(2)}, u32[]{:S(2)}) collective-permute-start(bf16[256,2048]{1,0:T(8,128)(2,1)} %refs_3_.1), channel_id=1, source_target_pairs={{0,1},{1,0},{2,3},{3,2},{4,5},{5,4},{6,7},{7,6},{8,9},{9,8},{10,11... | collective-permute-start | bytes 3145736 | tf_op jit(solution)/shard_map/ppermute | solution.py:29
  56.3 0.5 collective-permute-start.5
  56.9 0.1 collective-permute-start.6
  56.9 0.4 collective-permute-start.13
  57.4 2.2 shard_map.145
  59.6 1.0 copy-done.11
  60.6 3.1 %collective-permute-done.13.refs_7_ = bf16[512,256]{1,0:T(8,128)(2,1)S(1)} collective-permute-done((bf16[512,256]{1,0:T(8,128)(2,1)S(1)}, bf16[512,256]{1,0:T(8,128)(2,1)S(1)}, u32[]{:S(2)}, u32[]{:S(2)}) %collective-permute-start.13) | collective-permute-done | bytes 262176 | tf_op jit(solution)/shard_map/ppermute | solution.py:29
  63.7 5.4 %shard_map.146 = (bf16[512,256]{1,0:T(8,128)(2,1)S(1)}, f32[512,256]{1,0:T(8,128)S(1)}, bf16[1024,128]{1,0:T(8,128)(2,1)S(1)}, bf16[64,2048]{1,0:T(8,128)(2,1)S(1)}) custom-call(bf16[512,256]{1,0:T(8,128)(2,1)S(1)} %reshape.39.refs_0_, bf16[512,256]{1,0:T(8,128)(2,1)S(1)} %collective-permute-done.7.refs_1_, ...), custom_call_target="tpu_custom_call" | custom-call | tf_op jit(solution)/shard_map/pallas_call | solution.py:80
  69.1 15.2 %all_to_all.25.states_ref = bf16[16,64,128]{2,1,0:T(8,128)(2,1)S(1)} all-to-all(bf16[16,64,128]{2,1,0:T(8,128)(2,1)S(1)} %bitcast.22), channel_id=1, replica_groups=mesh['x'=4,'z'=4,'y'=4,'c'=2] {'x','z'}, dimensions={0} | all-to-all | bytes 524288 | tf_op jit(solution)/shard_map/all_to_all | solution.py:39
  84.4 10.9 %all_to_all.26 = bf16[16,64,128]{2,1,0:T(8,128)(2,1)S(1)} all-to-all(bf16[16,64,128]{2,1,0:T(8,128)(2,1)S(1)} %shard_map.147), channel_id=1, replica_groups=mesh['x'=4,'z'=4,'y'=4,'c'=2] {'x','z'}, dimensions={0} | all-to-all | bytes 524288 | tf_op jit(solution)/shard_map/all_to_all | solution.py:39
  95.2 1.9 shard_map.148
  97.1 6.3 %all-to-all-start.2 = ((bf16[8,64,256]{2,1,0:T(8,128)(2,1)}), bf16[8,64,256]{2,1,0:T(8,128)(2,1)S(1)}, u32[]{:S(2)}, u32[]{:S(2)}) async-start(bf16[8,64,256]{2,1,0:T(8,128)(2,1)} %bitcast.4), calls=%async_computation.2 | async-start | bytes 524288 | tf_op jit(solution)/shard_map/all_to_all | solution.py:39
  103.3 3.7 %shard_map.149 = (bf16[3072,256]{1,0:T(8,128)(2,1)S(1)}, bf16[256,3072]{1,0:T(8,128)(2,1)}) custom-call(s32[4,8,16]{2,1,0:T(8,128)} %bitcast.23, f32[4,8,16]{2,1,0:T(8,128)} %bitcast.24), custom_call_target="tpu_custom_call" | custom-call | tf_op jit(solution)/shard_map/pallas_call | solution.py:80
  107.1 2.8 %all-to-all-done.2.refs_8_ = bf16[8,64,256]{2,1,0:T(8,128)(2,1)S(1)} async-done(((bf16[8,64,256]{2,1,0:T(8,128)(2,1)}), bf16[8,64,256]{2,1,0:T(8,128)(2,1)S(1)}, u32[]{:S(2)}, u32[]{:S(2)}) %all-to-all-start.2) | async-done | bytes 262176 | tf_op jit(solution)/shard_map/all_to_all | solution.py:39
  109.9 1.2 copy-done.12
  111.1 5.5 %shard_map.150 = (f32[64,2048]{1,0:T(8,128)}, bf16[3072,512]{1,0:T(8,128)(2,1)S(1)}) custom-call(bf16[256,2048]{1,0:T(8,128)(2,1)S(1)} %copy-done.12, bf16[256,2048]{1,0:T(8,128)(2,1)S(1)} %collective-permute-done.refs_1_, bf16[256,2048]{1,0:T(8,128)(2,1)} %collective-permute-done.1.refs_2_, bf16[256,2048]{1,0:T(8,128)(2,1)} %collective-permute-done.2.refs_3_, ...), custom_call_target="tpu_custom_call" | custom-call | tf_op jit(solution)/shard_map/pallas_call | solution.py:80
  116.6 1.6 copy-done
  118.2 5.0 %all-to-all-start.3 = ((bf16[64,48,512]{2,1,0:T(8,128)(2,1)}), bf16[64,48,512]{2,1,0:T(8,128)(2,1)S(1)}, u32[]{:S(2)}, u32[]{:S(2)}) async-start(bf16[64,48,512]{2,1,0:T(8,128)(2,1)} %bitcast.14), calls=%async_computation.3 | async-start | bytes 6291456 | tf_op jit(solution)/shard_map/all_to_all | solution.py:39
  123.2 1.4 collective-permute-start.14
  124.6 0.1 collective-permute-start.15
  124.7 0.4 collective-permute-start.16
  125.1 3.5 %collective-permute-done.14.gate_b_ref = bf16[2048,512]{1,0:T(8,128)(2,1)S(1)} collective-permute-done((bf16[2048,512]{1,0:T(8,128)(2,1)}, bf16[2048,512]{1,0:T(8,128)(2,1)S(1)}, u32[]{:S(2)}, u32[]{:S(2)}) %collective-permute-start.14) | collective-permute-done | bytes 2097184 | tf_op jit(solution)/shard_map/ppermute | solution.py:29
  128.6 1.3 copy-done.4
  129.9 1.7 collective-permute-done.15.up_b_ref
  131.6 1.3 copy-done.6
  132.9 1.7 collective-permute-done.16.down_b_ref
  134.6 1.4 copy-done.8
  136.0 25.2 %all-to-all-done.3.rows_ref = bf16[64,48,512]{2,1,0:T(8,128)(2,1)S(1)} async-done(((bf16[64,48,512]{2,1,0:T(8,128)(2,1)}), bf16[64,48,512]{2,1,0:T(8,128)(2,1)S(1)}, u32[]{:S(2)}, u32[]{:S(2)}) %all-to-all-start.3) | async-done | bytes 3145760 | tf_op jit(solution)/shard_map/all_to_all | solution.py:39
  161.2 1.6 copy-done.1
  162.8 1.6 copy-done.2
  164.4 1.6 copy-done.3
  166.0 1.6 copy-done.5
  167.6 1.6 copy-done.7
  169.2 1.6 copy-done.9
  170.8 10.9 %shard_map.151 = bf16[64,48,512]{2,1,0:T(8,128)(2,1)S(1)} custom-call(bf16[64,48,512]{2,1,0:T(8,128)(2,1)S(1)} %all-to-all-done.3.rows_ref, bf16[256,256]{1,0:T(8,128)(2,1)S(1)} %copy-done.14, bf16[256,256]{1,0:T(8,128)(2,1)S(1)} %copy-done.15, bf16[2048,512]{1,0:T(8,128)(2,1)S(1)} %bitcast.16, bf16[2048,512]{1,0:T(8,128)(2,1)S(1)} %bitcast.18, ...), custom_call_target="tpu_custom_call" | custom-call | tf_op jit(solution)/shard_map/pallas_call | solution.py:80
  181.7 52.6 %all_to_all.27 = bf16[64,48,512]{2,1,0:T(8,128)(2,1)S(1)} all-to-all(bf16[64,48,512]{2,1,0:T(8,128)(2,1)S(1)} %shard_map.151), channel_id=1, replica_groups=mesh['x'=4,'z'=4,'y'=4,'c'=2] {'x','z','y'}, dimensions={0} | all-to-all | bytes 6291456 | tf_op jit(solution)/shard_map/all_to_all | solution.py:39
  234.3 1.0 shard_map.152
  235.3 0.8 reshape.51
  (35 shorter events, 0.2 us)
Async XLA Ops:
  0.0 25.6 %collective-permute-start = (bf16[256,2048]{1,0:T(8,128)(2,1)}, bf16[256,2048]{1,0:T(8,128)(2,1)S(1)}, u32[]{:S(2)}, u32[]{:S(2)}) collective-permute-start(bf16[256,2048]{1,0:T(8,128)(2,1)} %refs_3_.1), channel_id=1, source_target_pairs={{0,2},{1,7},{2,4},{3,1},{4,6},{5,3},{6,0},{7,5},{8,10},{9,15},{10,... | collective-permute-start | bytes 3145736 | tf_op jit(solution)/shard_map/ppermute | solution.py:35
  3.6 52.8 %collective-permute-start.1 = (bf16[256,2048]{1,0:T(8,128)(2,1)}, bf16[256,2048]{1,0:T(8,128)(2,1)}, u32[]{:S(2)}, u32[]{:S(2)}) collective-permute-start(bf16[256,2048]{1,0:T(8,128)(2,1)} %refs_3_.1), channel_id=1, source_target_pairs={{0,6},{1,3},{2,0},{3,5},{4,2},{5,7},{6,4},{7,1},{8,14},{9,11},{10,... | collective-permute-start | bytes 3145736 | tf_op jit(solution)/shard_map/ppermute | solution.py:35
  25.6 31.3 %collective-permute-start.2 = (bf16[256,2048]{1,0:T(8,128)(2,1)S(1)}, bf16[256,2048]{1,0:T(8,128)(2,1)}, u32[]{:S(2)}, u32[]{:S(2)}) collective-permute-start(bf16[256,2048]{1,0:T(8,128)(2,1)S(1)} %collective-permute-done.refs_1_), channel_id=1, source_target_pairs={{0,2},{1,7},{2,4},{3,1},{4,6},{5,3},{6,0},{7,5},{8,10},{9,15},{10,... | collective-permute-start | bytes 3145736 | tf_op jit(solution)/shard_map/ppermute | solution.py:35
  30.0 16.3 %collective-permute-start.7 = (bf16[512,256]{1,0:T(8,128)(2,1)S(1)}, bf16[512,256]{1,0:T(8,128)(2,1)S(1)}, u32[]{:S(2)}, u32[]{:S(2)}) collective-permute-start(bf16[512,256]{1,0:T(8,128)(2,1)S(1)} %reshape.39.refs_0_), channel_id=1, source_target_pairs={{0,2},{1,7},{2,4},{3,1},{4,6},{5,3},{6,0},{7,5},{8,10},{9,15},{10,... | collective-permute-start | bytes 786440 | tf_op jit(solution)/shard_map/ppermute | solution.py:35
  30.1 19.4 %collective-permute-start.8 = (bf16[512,256]{1,0:T(8,128)(2,1)S(1)}, bf16[512,256]{1,0:T(8,128)(2,1)S(1)}, u32[]{:S(2)}, u32[]{:S(2)}) collective-permute-start(bf16[512,256]{1,0:T(8,128)(2,1)S(1)} %reshape.39.refs_0_), channel_id=1, source_target_pairs={{0,6},{1,3},{2,0},{3,5},{4,2},{5,7},{6,4},{7,1},{8,14},{9,11},{10,... | collective-permute-start | bytes 786440 | tf_op jit(solution)/shard_map/ppermute | solution.py:35
  31.6 17.9 %collective-permute-start.10 = (bf16[512,256]{1,0:T(8,128)(2,1)S(1)}, bf16[512,256]{1,0:T(8,128)(2,1)S(1)}, u32[]{:S(2)}, u32[]{:S(2)}) collective-permute-start(bf16[512,256]{1,0:T(8,128)(2,1)S(1)} %reshape.39.refs_0_), channel_id=1, source_target_pairs={{0,1},{1,0},{2,3},{3,2},{4,5},{5,4},{6,7},{7,6},{8,9},{9,8},{10,11... | collective-permute-start | bytes 786440 | tf_op jit(solution)/shard_map/ppermute | solution.py:29
  46.4 6.4 %collective-permute-start.9 = (bf16[512,256]{1,0:T(8,128)(2,1)S(1)}, bf16[512,256]{1,0:T(8,128)(2,1)S(1)}, u32[]{:S(2)}, u32[]{:S(2)}) collective-permute-start(bf16[512,256]{1,0:T(8,128)(2,1)S(1)} %collective-permute-done.7.refs_1_), channel_id=1, source_target_pairs={{0,2},{1,7},{2,4},{3,1},{4,6},{5,3},{6,0},{7,5},{8,10},{9,15},{10,... | collective-permute-start | bytes 786440 | tf_op jit(solution)/shard_map/ppermute | solution.py:35
  49.5 6.9 %collective-permute-start.11 = (bf16[512,256]{1,0:T(8,128)(2,1)S(1)}, bf16[512,256]{1,0:T(8,128)(2,1)S(1)}, u32[]{:S(2)}, u32[]{:S(2)}) collective-permute-start(bf16[512,256]{1,0:T(8,128)(2,1)S(1)} %collective-permute-done.7.refs_1_), channel_id=1, source_target_pairs={{0,1},{1,0},{2,3},{3,2},{4,5},{5,4},{6,7},{7,6},{8,9},{9,8},{10,11... | collective-permute-start | bytes 786440 | tf_op jit(solution)/shard_map/ppermute | solution.py:29
  49.5 7.4 %collective-permute-start.12 = (bf16[512,256]{1,0:T(8,128)(2,1)S(1)}, bf16[512,256]{1,0:T(8,128)(2,1)S(1)}, u32[]{:S(2)}, u32[]{:S(2)}) collective-permute-start(bf16[512,256]{1,0:T(8,128)(2,1)S(1)} %collective-permute-done.8.refs_2_), channel_id=1, source_target_pairs={{0,1},{1,0},{2,3},{3,2},{4,5},{5,4},{6,7},{7,6},{8,9},{9,8},{10,11... | collective-permute-start | bytes 786440 | tf_op jit(solution)/shard_map/ppermute | solution.py:29
  52.8 54.3 %collective-permute-start.3 = (bf16[256,2048]{1,0:T(8,128)(2,1)}, bf16[256,2048]{1,0:T(8,128)(2,1)}, u32[]{:S(2)}, u32[]{:S(2)}) collective-permute-start(bf16[256,2048]{1,0:T(8,128)(2,1)} %refs_3_.1), channel_id=1, source_target_pairs={{0,1},{1,0},{2,3},{3,2},{4,5},{5,4},{6,7},{7,6},{8,9},{9,8},{10,11... | collective-permute-start | bytes 3145736 | tf_op jit(solution)/shard_map/ppermute | solution.py:29
  56.3 53.5 %collective-permute-start.4 = (bf16[256,2048]{1,0:T(8,128)(2,1)S(1)}, bf16[256,2048]{1,0:T(8,128)(2,1)}, u32[]{:S(2)}, u32[]{:S(2)}) collective-permute-start(bf16[256,2048]{1,0:T(8,128)(2,1)S(1)} %collective-permute-done.refs_1_), channel_id=1, source_target_pairs={{0,1},{1,0},{2,3},{3,2},{4,5},{5,4},{6,7},{7,6},{8,9},{9,8},{10,11... | collective-permute-start | bytes 3145736 | tf_op jit(solution)/shard_map/ppermute | solution.py:29
  56.3 53.5 %collective-permute-start.5 = (bf16[256,2048]{1,0:T(8,128)(2,1)}, bf16[256,2048]{1,0:T(8,128)(2,1)}, u32[]{:S(2)}, u32[]{:S(2)}) collective-permute-start(bf16[256,2048]{1,0:T(8,128)(2,1)} %collective-permute-done.1.refs_2_), channel_id=1, source_target_pairs={{0,1},{1,0},{2,3},{3,2},{4,5},{5,4},{6,7},{7,6},{8,9},{9,8},{10,11... | collective-permute-start | bytes 3145736 | tf_op jit(solution)/shard_map/ppermute | solution.py:29
  56.9 53.0 %collective-permute-start.6 = (bf16[256,2048]{1,0:T(8,128)(2,1)}, bf16[256,2048]{1,0:T(8,128)(2,1)}, u32[]{:S(2)}, u32[]{:S(2)}) collective-permute-start(bf16[256,2048]{1,0:T(8,128)(2,1)} %collective-permute-done.2.refs_3_), channel_id=1, source_target_pairs={{0,1},{1,0},{2,3},{3,2},{4,5},{5,4},{6,7},{7,6},{8,9},{9,8},{10,11... | collective-permute-start | bytes 3145736 | tf_op jit(solution)/shard_map/ppermute | solution.py:29
  56.9 6.8 %collective-permute-start.13 = (bf16[512,256]{1,0:T(8,128)(2,1)S(1)}, bf16[512,256]{1,0:T(8,128)(2,1)S(1)}, u32[]{:S(2)}, u32[]{:S(2)}) collective-permute-start(bf16[512,256]{1,0:T(8,128)(2,1)S(1)} %collective-permute-done.9.refs_3_), channel_id=1, source_target_pairs={{0,1},{1,0},{2,3},{3,2},{4,5},{5,4},{6,7},{7,6},{8,9},{9,8},{10,11... | collective-permute-start | bytes 786440 | tf_op jit(solution)/shard_map/ppermute | solution.py:29
  59.6 1.0 copy-start.11
  97.1 12.8 %all-to-all-start.2 = ((bf16[8,64,256]{2,1,0:T(8,128)(2,1)}), bf16[8,64,256]{2,1,0:T(8,128)(2,1)S(1)}, u32[]{:S(2)}, u32[]{:S(2)}) async-start(bf16[8,64,256]{2,1,0:T(8,128)(2,1)} %bitcast.4), calls=%async_computation.2 | async-start | bytes 524288 | tf_op jit(solution)/shard_map/all_to_all | solution.py:39
  109.9 1.2 copy-start.12
  116.5 1.6 copy-start
  118.2 43.0 %copy-start.14 = (bf16[256,256]{1,0:T(8,128)(2,1)S(1)}, bf16[256,256]{1,0:T(8,128)(2,1)}, u32[]{:S(2)}) copy-start(bf16[256,256]{1,0:T(8,128)(2,1)} %constant.4.clone.order_ref) | copy-start | bytes 393220
  118.2 43.0 %copy-start.15 = (bf16[256,256]{1,0:T(8,128)(2,1)S(1)}, bf16[256,256]{1,0:T(8,128)(2,1)}, u32[]{:S(2)}) copy-start(bf16[256,256]{1,0:T(8,128)(2,1)} %constant.5.clone.back_ref) | copy-start | bytes 393220
  118.2 43.0 %all-to-all-start.3 = ((bf16[64,48,512]{2,1,0:T(8,128)(2,1)}), bf16[64,48,512]{2,1,0:T(8,128)(2,1)S(1)}, u32[]{:S(2)}, u32[]{:S(2)}) async-start(bf16[64,48,512]{2,1,0:T(8,128)(2,1)} %bitcast.14), calls=%async_computation.3 | async-start | bytes 6291456 | tf_op jit(solution)/shard_map/all_to_all | solution.py:39
  123.2 5.4 %collective-permute-start.14 = (bf16[2048,512]{1,0:T(8,128)(2,1)}, bf16[2048,512]{1,0:T(8,128)(2,1)S(1)}, u32[]{:S(2)}, u32[]{:S(2)}) collective-permute-start(bf16[2048,512]{1,0:T(8,128)(2,1)} %bitcast.15), channel_id=1, source_target_pairs={{0,1},{1,0},{2,3},{3,2},{4,5},{5,4},{6,7},{7,6},{8,9},{9,8},{10,11... | collective-permute-start | bytes 6291464 | tf_op jit(solution)/shard_map/ppermute | solution.py:29
  124.6 7.0 %collective-permute-start.15 = (bf16[2048,512]{1,0:T(8,128)(2,1)}, bf16[2048,512]{1,0:T(8,128)(2,1)S(1)}, u32[]{:S(2)}, u32[]{:S(2)}) collective-permute-start(bf16[2048,512]{1,0:T(8,128)(2,1)} %bitcast.17), channel_id=1, source_target_pairs={{0,1},{1,0},{2,3},{3,2},{4,5},{5,4},{6,7},{7,6},{8,9},{9,8},{10,11... | collective-permute-start | bytes 6291464 | tf_op jit(solution)/shard_map/ppermute | solution.py:29
  124.7 9.9 %collective-permute-start.16 = (bf16[512,2048]{1,0:T(8,128)(2,1)}, bf16[512,2048]{1,0:T(8,128)(2,1)S(1)}, u32[]{:S(2)}, u32[]{:S(2)}) collective-permute-start(bf16[512,2048]{1,0:T(8,128)(2,1)} %bitcast.19), channel_id=1, source_target_pairs={{0,1},{1,0},{2,3},{3,2},{4,5},{5,4},{6,7},{7,6},{8,9},{9,8},{10,11... | collective-permute-start | bytes 6291464 | tf_op jit(solution)/shard_map/ppermute | solution.py:29
  128.6 1.3 copy-start.4
  131.6 1.3 copy-start.6
  134.6 1.4 copy-start.8
  161.2 1.6 copy-start.1
  162.8 1.6 copy-start.2
  164.4 1.6 copy-start.3
  166.0 1.6 copy-start.5
  167.6 1.6 copy-start.7
  169.2 1.6 copy-start.9
  181.7 52.6 %copy-start.10 = (bf16[256,3072]{1,0:T(8,128)(2,1)S(1)}, bf16[256,3072]{1,0:T(8,128)(2,1)}, u32[]{:S(2)}) copy-start(bf16[256,3072]{1,0:T(8,128)(2,1)} %get-tuple-element.27.table_ref) | copy-start | bytes 4718596
  181.7 52.6 %copy-start.13 = (f32[64,2048]{1,0:T(8,128)S(1)}, f32[64,2048]{1,0:T(8,128)}, u32[]{:S(2)}) copy-start(f32[64,2048]{1,0:T(8,128)} %get-tuple-element.28.residual_ref) | copy-start | bytes 1572868
